TPU v7x, 128 devices: a whole 4x4x4 slice. The times are simulated.
128 devices in a mesh: sec: 2 (over core), blk: 64 (over x, y, z).
Axes of the slice: x: 4, y: 4, z: 4, core: 2. Of those that a mesh axis runs over, the one named last changes fastest.
Arguments:
- source: float32 [8192, 4096], P(('sec', 'blk')), may hold values from -6 to 6
- parent: int32 [1024], P(('sec', 'blk')), may hold values from -1 to 8191, as said below
- neighbor: int32 [1024, 6], P(('sec', 'blk')), may hold values from -1 to 1023, as said below
Outputs:
- solution: float32 [8192, 4096], P(('sec', 'blk'))
- residual: float32 [8192, 4096], P(('sec', 'blk'))
Inputs may be any that keep to these rules, and one draw needn't show every extreme that they name: parent[g] is -1 for every family on sec index 1; a family on sec index 0 and blk index b names a block of a family on sec index 1 at blk index b or at blk index b + 1 (modulo the blk axis), exactly half of each device's families each way; no two families name the same block. neighbor[g, d] lies on the same index of sec as g, either on g's device or on the device whose blk index is g's minus (d = 0) or plus (d = 1) a quarter of the blk axis, minus (d = 2) or plus (d = 3) a sixteenth of it, minus (d = 4) or plus (d = 5) one; the relation is symmetric (if h is beside g in direction d, g is beside h in direction d xor 1); on each device at most 4 families have a neighbor on another device in direction -x, and likewise +x, at most 4 in -y and in +y, at most 4 in -z and in +z, and exactly so on some devices.
All inputs are finite; a program needn't handle non-finite values.
Results may differ from a plain program's by a relative error of at most 0.0001.
Values sent between devices are 32-bit elements; how exact they have to be, the bound alone decides.
No kernel may reach another device: no remote copies, remote signals or barrier semaphores. Data moves between devices by JAX's collectives and lax.ppermute only.
A program may use at most 128 MiB of HBM per device.

v0:
```python
import jax
import jax.numpy as jnp
from jax import lax
from jax.sharding import PartitionSpec as P

BS = 16
NU = 3
ITERS = 2


DAMPING = 0.8
RESTRICT_WEIGHT = 0.5
OPPOSITE = (1, 0, 3, 2, 5, 4)


def passed_along(block, axis, distance):
    devices = range(lax.axis_size(axis))
    route = [(i - distance, i) for i in devices if i - distance in devices]
    return lax.ppermute(block, axis, route)


def shifted(x, axis, by):
    length = lax.axis_size(axis)
    return lax.ppermute(x, axis, [(i, (i + by) % length) for i in range(length)])


def to_family(blocks):
    total = blocks.shape[0] // 8
    cube = blocks.reshape(total, 2, 2, 2, BS, BS, BS)
    return cube.transpose(0, 1, 4, 2, 5, 3, 6).reshape(total, 2 * BS, 4 * BS * BS)


def to_blocks(family):
    total = family.shape[0]
    cube = family.reshape(total, 2, BS, 2, BS, 2, BS)
    return cube.transpose(0, 1, 3, 5, 2, 4, 6).reshape(total * 8, BS * BS * BS)


def faces_of(family):
    total, side_len = (family.shape[0], family.shape[1])
    face_area = side_len * side_len
    return jnp.stack(
        [
            family[:, 0],
            family[:, -1],
            family[:, :, :side_len].reshape(total, face_area),
            family[:, :, face_area - side_len :].reshape(total, face_area),
            family[:, :, 0::side_len].reshape(total, face_area),
            family[:, :, side_len - 1 :: side_len].reshape(total, face_area),
        ],
        axis=1,
    )


def apply_operator(family, halo_rows):
    total, side_len = (family.shape[0], family.shape[1])
    lower_x = jnp.concatenate([halo_rows[:, 0:1], family[:, :-1]], axis=1)
    upper_x = jnp.concatenate([family[:, 1:], halo_rows[:, 1:2]], axis=1)
    lower_y = jnp.concatenate(
        [halo_rows[:, 2].reshape(total, side_len, side_len), family[:, :, :-side_len]], axis=2
    )
    upper_y = jnp.concatenate(
        [family[:, :, side_len:], halo_rows[:, 3].reshape(total, side_len, side_len)], axis=2
    )
    position = jnp.arange(side_len * side_len, dtype=jnp.int32) % side_len
    first_z = position == 0
    last_z = position == side_len - 1
    face_low = jnp.repeat(halo_rows[:, 4].reshape(total, side_len, side_len), side_len, axis=2)
    face_high = jnp.repeat(halo_rows[:, 5].reshape(total, side_len, side_len), side_len, axis=2)
    shifted_down = jnp.concatenate([jnp.zeros_like(family[:, :, :1]), family[:, :, :-1]], axis=2)
    shifted_up = jnp.concatenate([family[:, :, 1:], jnp.zeros_like(family[:, :, :1])], axis=2)
    lower_z = jnp.where(first_z, face_low, shifted_down)
    upper_z = jnp.where(last_z, face_high, shifted_up)
    return 6.0 * family - (lower_x + upper_x + lower_y + upper_y + lower_z + upper_z)


def restrict(family):
    total = family.shape[0]
    cube = family.reshape(total, BS, 2, BS, 2, BS, 2)
    return RESTRICT_WEIGHT * cube.sum(axis=(2, 4, 6)).reshape(total, BS * BS * BS)


def prolong(blocks):
    total = blocks.shape[0]
    cube = blocks.reshape(total, BS, 1, BS, 1, BS, 1)
    return jnp.broadcast_to(cube, (total, BS, 2, BS, 2, BS, 2)).reshape(total, 2 * BS, 4 * BS * BS)


def smooth(right_side):
    zero_halo = jnp.zeros((right_side.shape[0], 6, right_side.shape[2]), right_side.dtype)
    correction = DAMPING / 6.0 * right_side
    for sweep_index in range(NU - 1):
        correction = correction + DAMPING / 6.0 * (
            right_side - apply_operator(correction, zero_halo)
        )
    return correction


def local(source, parent, neighbor):
    peer_count = lax.axis_size("blk")
    my_chip = lax.axis_index("blk")
    coarse_side = lax.axis_index("sec") == 1
    fam_total = neighbor.shape[0]
    block_total = source.shape[0]
    depth = peer_count // 16
    strides = (peer_count // 4, peer_count // 4, depth, depth, 1, 1)
    linked = neighbor >= 0
    owner_chip = jnp.maximum(neighbor, 0) // fam_total % peer_count
    nearby = linked & (owner_chip == my_chip)
    local_row = jnp.maximum(neighbor, 0) % fam_total
    send_rows = []
    recv_rows = []
    for direction in range(6):
        send_rows.append(None)
        recv_rows.append(local_row[:, direction])

    def gather_halo(family):
        face_table = faces_of(family)
        sides = []
        for direction in range(6):
            sent = face_table[:, OPPOSITE[direction]]
            offset = strides[direction] if direction % 2 == 0 else -strides[direction]
            arrived = passed_along(sent, "blk", offset)
            from_remote = jnp.take(arrived, recv_rows[direction], axis=0)
            from_nearby = jnp.take(sent, local_row[:, direction], axis=0)
            picked = jnp.where(nearby[:, direction, None], from_nearby, from_remote)
            sides.append(jnp.where(linked[:, direction, None], picked, 0.0))
        return jnp.stack(sides, axis=1)

    has_parent = parent >= 0
    coarse_chip = jnp.where(has_parent, parent // block_total - peer_count, -1)
    to_own = has_parent & (coarse_chip == my_chip)
    to_next = has_parent & (coarse_chip == (my_chip + 1) % peer_count)
    local_block = (jnp.maximum(parent, 0) % block_total).astype(jnp.float32)
    tag_own = jnp.where(to_own, local_block, -1.0)
    tag_next = jnp.where(to_next, local_block, -1.0)
    source_fam = to_family(source)
    solution = jnp.zeros_like(source_fam)
    for iteration in range(ITERS):
        residue = source_fam - apply_operator(solution, gather_halo(solution))
        down = restrict(residue)
        prev_rows, prev_tags = shifted((down, tag_next), "blk", 1)
        in_own, tags_own, in_prev, tags_prev = passed_along(
            (down, tag_own, prev_rows, prev_tags), "sec", 1
        )
        incoming = jnp.concatenate([in_own, in_prev], axis=0)
        tags = jnp.concatenate([tags_own, tags_prev], axis=0)
        live = (tags >= 0.0) & coarse_side
        target = jnp.where(live, tags.astype(jnp.int32), block_total)
        lookup = jnp.maximum(tags, 0.0).astype(jnp.int32)
        right_blocks = to_blocks(residue).at[target].add(incoming, mode="drop")
        correction = smooth(to_family(right_blocks))
        answers = jnp.where(live[:, None], jnp.take(to_blocks(correction), lookup, axis=0), 0.0)
        ans_own = answers[:fam_total]
        ans_prev = answers[fam_total:]
        back_own, back_prev = passed_along((ans_own, ans_prev), "sec", -1)
        back_next = shifted(back_prev, "blk", -1)
        lifted = jnp.where(to_own[:, None], back_own, jnp.where(to_next[:, None], back_next, 0.0))
        solution = solution + correction + prolong(lifted)
    residue = source_fam - apply_operator(solution, gather_halo(solution))
    return (to_blocks(solution), to_blocks(residue))


def solution(mesh):
    return jax.shard_map(
        local,
        mesh=mesh,
        in_specs=(P(("sec", "blk"), None), P(("sec", "blk")), P(("sec", "blk"), None)),
        out_specs=(P(("sec", "blk"), None), P(("sec", "blk"), None)),
        check_vma=False,
    )
```

profile of v0, /device:TPU:18, one launch (start us, length us, event | category | flops | bytes accessed | tf_op | source)
XLA Modules:
  0.0 607.6 jit_solution(2905432357940590836)
XLA Ops:
  3.0 5.8 collective-permute-start.5
  23.8 6.2 %reshape.190 = f32[8,2,2,2,16,16,16]{6,5,4,3,2,1,0:T(8,128)} reshape(f32[64,4096]{1,0:T(8,128)} %param.7) | data formatting | bytes 2097152 | tf_op jit(solution)/shard_map/reshape | solution.py:29
  30.0 15.4 %copy.103 = f32[8,2,2,2,16,16,16]{6,3,5,2,0,4,1:T(2,128)} copy(f32[8,2,2,2,16,16,16]{6,5,4,3,2,1,0:T(8,128)} %reshape.190) | data formatting | bytes 2097152 | tf_op jit(solution)/shard_map/reshape | solution.py:29
  45.4 14.2 %reshape.191 = f32[8,32,1024]{2,0,1:T(8,128)S(1)} reshape(f32[8,2,16,2,16,2,16]{6,5,4,3,0,2,1:T(2,128)} %bitcast.106) | data formatting | bytes 2097152 | tf_op jit(solution)/shard_map/reshape | solution.py:30
  76.5 4.6 reshape.192
  83.3 8.3 %copy.63 = f32[8,32,1024]{0,2,1:T(8,128)} copy(f32[8,32,1024]{2,0,1:T(8,128)S(1)} %subtract_subtract_fusion) | data formatting | bytes 2097152 | tf_op jit(solution)/shard_map/sub | solution.py:140
  91.6 13.7 %reduce_sum.18 = f32[8,16,16,16]{0,3,2,1:T(8,128)} reduce(f32[8,16,2,16,2,16,2]{0,6,5,4,3,2,1:T(2,128)} %bitcast.104, f32[]{:T(128)} %constant.145.clone.1), dimensions={2,4,6}, to_apply=%region_0.2 | reduce | flops 229376 | bytes 1179652 | tf_op jit(solution)/shard_map/reduce_sum | solution.py:80
  123.5 12.6 %reshape.194 = f32[8,2,16,2,16,2,16]{6,5,4,3,0,2,1:T(2,128)} reshape(f32[8,32,1024]{2,0,1:T(8,128)S(1)} %subtract_subtract_fusion) | data formatting | bytes 2097152 | tf_op jit(solution)/shard_map/reshape | solution.py:35
  136.1 7.8 %copy.102 = f32[8,2,16,2,16,2,16]{6,4,2,5,3,1,0:T(8,128)} copy(f32[8,2,16,2,16,2,16]{6,5,4,3,0,2,1:T(2,128)} %reshape.194) | data formatting | bytes 2097152 | tf_op jit(solution)/shard_map/reshape | solution.py:35
  143.9 7.9 %reshape.195 = f32[64,4096]{1,0:T(8,128)S(1)} reshape(f32[8,2,2,2,16,16,16]{6,5,4,3,2,1,0:T(8,128)} %bitcast.107) | data formatting | bytes 2097152 | tf_op jit(solution)/shard_map/reshape | solution.py:36
  153.3 4.9 reshape.197
  158.2 15.4 %copy.66 = f32[8,2,16,2,16,2,16]{6,5,4,3,0,2,1:T(2,128)} copy(f32[8,2,16,2,16,2,16]{6,4,2,5,3,1,0:T(8,128)} %bitcast.108) | data formatting | bytes 2097152 | tf_op jit(solution)/shard_map/transpose | solution.py:30
  173.6 14.2 %reshape.198 = f32[8,32,1024]{2,0,1:T(8,128)S(1)} reshape(f32[8,2,16,2,16,2,16]{6,5,4,3,0,2,1:T(2,128)} %copy.66) | data formatting | bytes 2097152 | tf_op jit(solution)/shard_map/reshape | solution.py:30
  191.9 12.6 %reshape.199 = f32[8,2,16,2,16,2,16]{6,5,4,3,0,2,1:T(2,128)} reshape(f32[8,32,1024]{2,0,1:T(8,128)S(1)} %multiply_add_fusion.2) | data formatting | bytes 2097152 | tf_op jit(solution)/shard_map/reshape | solution.py:35
  204.5 7.8 %copy.67 = f32[8,2,2,2,16,16,16]{6,5,4,3,2,1,0:T(8,128)} copy(f32[8,2,2,2,16,16,16]{6,3,5,2,0,4,1:T(2,128)} %bitcast.112) | data formatting | bytes 2097152 | tf_op jit(solution)/shard_map/transpose | solution.py:36
  212.3 8.1 %reshape.200 = f32[64,4096]{1,0:T(8,128)S(1)} reshape(f32[8,2,2,2,16,16,16]{6,5,4,3,2,1,0:T(8,128)} %copy.67) | data formatting | bytes 2097152 | tf_op jit(solution)/shard_map/reshape | solution.py:36
  226.4 4.3 collective-permute-done.14
  232.7 10.4 %broadcast_in_dim.373 = f32[8,16,2,16,2,16,2]{0,6,5,4,3,2,1:T(2,128)} broadcast(f32[8,16,16,16]{0,3,2,1:T(8,128)} %bitcast.114), dimensions={0,1,3,5} | broadcast | bytes 1179648 | tf_op jit(solution)/shard_map/broadcast_in_dim | solution.py:86
  243.1 9.8 %copy.69 = f32[8,32,1024]{2,0,1:T(8,128)} copy(f32[8,32,1024]{0,2,1:T(8,128)} %bitcast.101) | data formatting | bytes 2097152 | tf_op jit(solution)/shard_map/reshape | solution.py:86
  267.8 5.7 collective-permute-start.20
  282.9 4.2 collective-permute-start.17
  297.3 4.6 reshape.202
  304.4 4.6 reshape.203
  309.7 4.6 fusion.5
  314.3 8.3 %copy.79 = f32[8,32,1024]{0,2,1:T(8,128)} copy(f32[8,32,1024]{2,0,1:T(8,128)S(1)} %fusion.5) | data formatting | bytes 2097152 | tf_op jit(solution)/shard_map/sub | solution.py:140
  322.5 13.7 %reduce_sum.19 = f32[8,16,16,16]{0,3,2,1:T(8,128)} reduce(f32[8,16,2,16,2,16,2]{0,6,5,4,3,2,1:T(2,128)} %bitcast.102, f32[]{:T(128)} %constant.145.clone.1), dimensions={2,4,6}, to_apply=%region_2.5 | reduce | flops 229376 | bytes 1179652 | tf_op jit(solution)/shard_map/reduce_sum | solution.py:80
  342.8 8.0 %collective-permute-done.22 = f32[8,4096]{1,0:T(8,128)} collective-permute-done((f32[8,4096]{1,0:T(8,128)S(1)}, f32[8,4096]{1,0:T(8,128)}, u32[]{:S(2)}, u32[]{:S(2)}) %collective-permute-start.22) | collective-permute-done | bytes 131104 | tf_op jit(solution)/shard_map/ppermute | solution.py:24
  352.1 12.6 %reshape.204 = f32[8,2,16,2,16,2,16]{6,5,4,3,0,2,1:T(2,128)} reshape(f32[8,32,1024]{2,0,1:T(8,128)S(1)} %fusion.5) | data formatting | bytes 2097152 | tf_op jit(solution)/shard_map/reshape | solution.py:35
  364.7 7.8 %copy.101 = f32[8,2,16,2,16,2,16]{6,4,2,5,3,1,0:T(8,128)} copy(f32[8,2,16,2,16,2,16]{6,5,4,3,0,2,1:T(2,128)} %reshape.204) | data formatting | bytes 2097152 | tf_op jit(solution)/shard_map/reshape | solution.py:35
  372.5 7.9 %reshape.205 = f32[64,4096]{1,0:T(8,128)S(1)} reshape(f32[8,2,2,2,16,16,16]{6,5,4,3,2,1,0:T(8,128)} %bitcast.109) | data formatting | bytes 2097152 | tf_op jit(solution)/shard_map/reshape | solution.py:36
  381.8 5.1 reshape.207
  386.9 15.4 %copy.82 = f32[8,2,16,2,16,2,16]{6,5,4,3,0,2,1:T(2,128)} copy(f32[8,2,16,2,16,2,16]{6,4,2,5,3,1,0:T(8,128)} %bitcast.110) | data formatting | bytes 2097152 | tf_op jit(solution)/shard_map/transpose | solution.py:30
  402.3 14.2 %reshape.208 = f32[8,32,1024]{2,0,1:T(8,128)S(1)} reshape(f32[8,2,16,2,16,2,16]{6,5,4,3,0,2,1:T(2,128)} %copy.82) | data formatting | bytes 2097152 | tf_op jit(solution)/shard_map/reshape | solution.py:30
  421.7 13.5 %reshape.209 = f32[8,2,16,2,16,2,16]{6,5,4,3,0,2,1:T(2,128)} reshape(f32[8,32,1024]{2,0,1:T(8,128)} %multiply_add_fusion) | data formatting | bytes 2097152 | tf_op jit(solution)/shard_map/reshape | solution.py:35
  435.2 7.8 %copy.83 = f32[8,2,2,2,16,16,16]{6,5,4,3,2,1,0:T(8,128)} copy(f32[8,2,2,2,16,16,16]{6,3,5,2,0,4,1:T(2,128)} %bitcast.113) | data formatting | bytes 2097152 | tf_op jit(solution)/shard_map/transpose | solution.py:36
  443.0 8.1 %reshape.210 = f32[64,4096]{1,0:T(8,128)S(1)} reshape(f32[8,2,2,2,16,16,16]{6,5,4,3,2,1,0:T(8,128)} %copy.83) | data formatting | bytes 2097152 | tf_op jit(solution)/shard_map/reshape | solution.py:36
  463.3 10.4 %broadcast_in_dim.377 = f32[8,16,2,16,2,16,2]{0,6,5,4,3,2,1:T(2,128)} broadcast(f32[8,16,16,16]{0,3,2,1:T(8,128)} %bitcast.115), dimensions={0,1,3,5} | broadcast | bytes 1179648 | tf_op jit(solution)/shard_map/broadcast_in_dim | solution.py:86
  473.6 9.8 %copy.85 = f32[8,32,1024]{2,0,1:T(8,128)} copy(f32[8,32,1024]{0,2,1:T(8,128)} %bitcast.103) | data formatting | bytes 2097152 | tf_op jit(solution)/shard_map/reshape | solution.py:86
  503.0 6.0 collective-permute-start.32
  509.9 6.0 collective-permute-start.30
  516.6 12.6 %reshape.212 = f32[8,2,16,2,16,2,16]{6,5,4,3,0,2,1:T(2,128)} reshape(f32[8,32,1024]{2,0,1:T(8,128)S(1)} %add_add_fusion) | data formatting | bytes 2097152 | tf_op jit(solution)/shard_map/reshape | solution.py:35
  529.9 7.8 %copy.86 = f32[8,2,2,2,16,16,16]{6,5,4,3,2,1,0:T(8,128)} copy(f32[8,2,2,2,16,16,16]{6,3,5,2,0,4,1:T(2,128)} %bitcast.105) | data formatting | bytes 2097152 | tf_op jit(solution)/shard_map/transpose | solution.py:36
  537.8 8.7 %reshape.213 = f32[64,4096]{1,0:T(8,128)} reshape(f32[8,2,2,2,16,16,16]{6,5,4,3,2,1,0:T(8,128)} %copy.86) | data formatting | bytes 2097152 | tf_op jit(solution)/shard_map/reshape | solution.py:36
  565.4 4.6 reshape.214
  572.0 5.2 fusion.11
  577.2 13.5 %reshape.216 = f32[8,2,16,2,16,2,16]{6,5,4,3,0,2,1:T(2,128)} reshape(f32[8,32,1024]{2,0,1:T(8,128)} %fusion.11) | data formatting | bytes 2097152 | tf_op jit(solution)/shard_map/reshape | solution.py:35
  590.7 7.8 %copy.95 = f32[8,2,2,2,16,16,16]{6,5,4,3,2,1,0:T(8,128)} copy(f32[8,2,2,2,16,16,16]{6,3,5,2,0,4,1:T(2,128)} %bitcast.111) | data formatting | bytes 2097152 | tf_op jit(solution)/shard_map/transpose | solution.py:36
  598.5 8.7 %reshape.217 = f32[64,4096]{1,0:T(8,128)} reshape(f32[8,2,2,2,16,16,16]{6,5,4,3,2,1,0:T(8,128)} %copy.95) | data formatting | bytes 2097152 | tf_op jit(solution)/shard_map/reshape | solution.py:36
  (346 shorter events, 174.0 us)
Async XLA Ops:
  0.6 59.0 %collective-permute-start.3 = (f32[8,1024]{1,0:T(8,128)S(1)}, f32[8,1024]{1,0:T(8,128)S(1)}, u32[]{:S(2)}, u32[]{:S(2)}) collective-permute-start(f32[8,1024]{1,0:T(8,128)S(1)} %broadcast.236), channel_id=1, source_target_pairs={{4,0},{5,1},{6,2},{7,3},{8,4},{9,5},{10,6},{11,7},{12,8},{13,9},{1... | collective-permute-start | bytes 98312 | tf_op jit(solution)/shard_map/ppermute | solution.py:19
  3.0 61.2 %collective-permute-start.5 = (f32[8,1024]{1,0:T(8,128)S(1)}, f32[8,1024]{1,0:T(8,128)S(1)}, u32[]{:S(2)}, u32[]{:S(2)}) collective-permute-start(f32[8,1024]{1,0:T(8,128)S(1)} %broadcast.236), channel_id=1, source_target_pairs={{1,0},{2,1},{3,2},{4,3},{5,4},{6,5},{7,6},{8,7},{9,8},{10,9},{11,1... | collective-permute-start | bytes 98312 | tf_op jit(solution)/shard_map/ppermute | solution.py:19
  8.8 56.0 %collective-permute-start.2 = (f32[8,1024]{1,0:T(8,128)S(1)}, f32[8,1024]{1,0:T(8,128)S(1)}, u32[]{:S(2)}, u32[]{:S(2)}) collective-permute-start(f32[8,1024]{1,0:T(8,128)S(1)} %broadcast.236), channel_id=1, source_target_pairs={{0,4},{1,5},{2,6},{3,7},{4,8},{5,9},{6,10},{7,11},{8,12},{9,13},{1... | collective-permute-start | bytes 98312 | tf_op jit(solution)/shard_map/ppermute | solution.py:19
  12.3 53.2 %collective-permute-start.4 = (f32[8,1024]{1,0:T(8,128)S(1)}, f32[8,1024]{1,0:T(8,128)S(1)}, u32[]{:S(2)}, u32[]{:S(2)}) collective-permute-start(f32[8,1024]{1,0:T(8,128)S(1)} %broadcast.236), channel_id=1, source_target_pairs={{0,1},{1,2},{2,3},{3,4},{4,5},{5,6},{6,7},{7,8},{8,9},{9,10},{10,1... | collective-permute-start | bytes 98312 | tf_op jit(solution)/shard_map/ppermute | solution.py:19
  14.3 51.9 %collective-permute-start.1 = (f32[8,1024]{1,0:T(8,128)S(1)}, f32[8,1024]{1,0:T(8,128)S(1)}, u32[]{:S(2)}, u32[]{:S(2)}) collective-permute-start(f32[8,1024]{1,0:T(8,128)S(1)} %broadcast.236), channel_id=1, source_target_pairs={{16,0},{17,1},{18,2},{19,3},{20,4},{21,5},{22,6},{23,7},{24,8},{25... | collective-permute-start | bytes 98312 | tf_op jit(solution)/shard_map/ppermute | solution.py:19
  17.7 270.6 %copy-start.35 = (pred[8]{0:T(512)(128)(4,1)}, pred[8]{0:T(512)(128)(4,1)S(1)}, u32[]{:S(2)}) copy-start(pred[8]{0:T(512)(128)(4,1)S(1)} %compare_and_fusion.1) | copy-start | bytes 28
  17.8 272.0 %copy-start.33 = (pred[8]{0:T(512)(128)(4,1)}, pred[8]{0:T(512)(128)(4,1)S(1)}, u32[]{:S(2)}) copy-start(pred[8]{0:T(512)(128)(4,1)S(1)} %compare_and_fusion.3) | copy-start | bytes 28
  17.8 275.7 %copy-start.31 = (pred[8]{0:T(512)(128)(4,1)}, pred[8]{0:T(512)(128)(4,1)S(1)}, u32[]{:S(2)}) copy-start(pred[8]{0:T(512)(128)(4,1)S(1)} %compare_and_fusion.4) | copy-start | bytes 28
  17.9 269.8 %copy-start.28 = (pred[8]{0:T(512)(128)(4,1)}, pred[8]{0:T(512)(128)(4,1)S(1)}, u32[]{:S(2)}) copy-start(pred[8]{0:T(512)(128)(4,1)S(1)} %get-tuple-element.80) | copy-start | bytes 28
  17.9 291.7 %copy-start.27 = (pred[8]{0:T(512)(128)(4,1)}, pred[8]{0:T(512)(128)(4,1)S(1)}, u32[]{:S(2)}) copy-start(pred[8]{0:T(512)(128)(4,1)S(1)} %get-tuple-element.81) | copy-start | bytes 28
  19.8 269.3 %copy-start = (s32[1024]{0:T(1024)}, s32[1024]{0:T(1024)S(1)}, u32[]{:S(2)}) copy-start(s32[1024]{0:T(1024)S(1)} %pad_clamp_fusion.3) | copy-start | bytes 12292
  19.8 268.6 %copy-start.2 = (s32[1024]{0:T(1024)}, s32[1024]{0:T(1024)S(1)}, u32[]{:S(2)}) copy-start(s32[1024]{0:T(1024)S(1)} %pad_clamp_fusion.2) | copy-start | bytes 12292
  20.3 268.7 %copy-start.19 = (pred[8]{0:T(512)(128)(4,1)}, pred[8]{0:T(512)(128)(4,1)S(1)}, u32[]{:S(2)}) copy-start(pred[8]{0:T(512)(128)(4,1)S(1)} %get-tuple-element.18) | copy-start | bytes 28
  20.3 268.7 %copy-start.21 = (pred[8]{0:T(512)(128)(4,1)}, pred[8]{0:T(512)(128)(4,1)S(1)}, u32[]{:S(2)}) copy-start(pred[8]{0:T(512)(128)(4,1)S(1)} %get-tuple-element.86) | copy-start | bytes 28
  20.3 269.4 %copy-start.11 = (pred[8]{0:T(512)(128)(4,1)}, pred[8]{0:T(512)(128)(4,1)S(1)}, u32[]{:S(2)}) copy-start(pred[8]{0:T(512)(128)(4,1)S(1)} %get-tuple-element.19) | copy-start | bytes 28
  20.3 269.4 %copy-start.13 = (pred[8]{0:T(512)(128)(4,1)}, pred[8]{0:T(512)(128)(4,1)S(1)}, u32[]{:S(2)}) copy-start(pred[8]{0:T(512)(128)(4,1)S(1)} %get-tuple-element.85) | copy-start | bytes 28
  20.3 273.1 %copy-start.7 = (pred[8]{0:T(512)(128)(4,1)}, pred[8]{0:T(512)(128)(4,1)S(1)}, u32[]{:S(2)}) copy-start(pred[8]{0:T(512)(128)(4,1)S(1)} %get-tuple-element.20) | copy-start | bytes 28
  20.3 273.1 %copy-start.9 = (pred[8]{0:T(512)(128)(4,1)}, pred[8]{0:T(512)(128)(4,1)S(1)}, u32[]{:S(2)}) copy-start(pred[8]{0:T(512)(128)(4,1)S(1)} %get-tuple-element.84) | copy-start | bytes 28
  20.3 289.2 %copy-start.4 = (pred[8]{0:T(512)(128)(4,1)}, pred[8]{0:T(512)(128)(4,1)S(1)}, u32[]{:S(2)}) copy-start(pred[8]{0:T(512)(128)(4,1)S(1)} %get-tuple-element.16) | copy-start | bytes 28
  20.3 289.2 %copy-start.6 = (pred[8]{0:T(512)(128)(4,1)}, pred[8]{0:T(512)(128)(4,1)S(1)}, u32[]{:S(2)}) copy-start(pred[8]{0:T(512)(128)(4,1)S(1)} %get-tuple-element.87) | copy-start | bytes 28
  59.7 21.4 %collective-permute-start = (f32[8,1024]{1,0:T(8,128)S(1)}, f32[8,1024]{1,0:T(8,128)S(1)}, u32[]{:S(2)}, u32[]{:S(2)}) collective-permute-start(f32[8,1024]{1,0:T(8,128)S(1)} %broadcast.236), channel_id=1, source_target_pairs={{0,16},{1,17},{2,18},{3,19},{4,20},{5,21},{6,22},{7,23},{8,24},{9,... | collective-permute-start | bytes 98312 | tf_op jit(solution)/shard_map/ppermute | solution.py:19
  110.5 11.6 %collective-permute-start.10 = (f32[8,4096]{1,0:T(8,128)S(1)}, f32[8,4096]{1,0:T(8,128)S(1)}, u32[]{:S(2)}, u32[]{:S(2)}) collective-permute-start(f32[8,4096]{1,0:T(8,128)S(1)} %copy.64), channel_id=1, source_target_pairs={{0,1},{1,2},{2,3},{3,4},{4,5},{5,6},{6,7},{7,8},{8,9},{9,10},{10,1... | collective-permute-start | bytes 393224 | tf_op jit(solution)/shard_map/ppermute | solution.py:24
  110.6 7.1 %collective-permute-start.7 = (f32[8]{0:T(128)S(1)}, f32[8]{0:T(128)S(1)}, u32[]{:S(2)}, u32[]{:S(2)}) collective-permute-start(f32[8]{0:T(128)S(1)} %get-tuple-element.27), channel_id=1, source_target_pairs={{0,1},{1,2},{2,3},{3,4},{4,5},{5,6},{6,7},{7,8},{8,9},{9,10},{10,1... | collective-permute-start | bytes 104 | tf_op jit(solution)/shard_map/ppermute | solution.py:24
  112.6 6.4 %collective-permute-start.6 = (f32[8]{0:T(128)S(1)}, f32[8]{0:T(128)S(1)}, u32[]{:S(2)}, u32[]{:S(2)}) collective-permute-start(f32[8]{0:T(128)S(1)} %copy-done.50), channel_id=1, source_target_pairs={{0,64},{1,65},{2,66},{3,67},{4,68},{5,69},{6,70},{7,71},{8,72},{9,... | collective-permute-start | bytes 104 | tf_op jit(solution)/shard_map/ppermute | solution.py:19
  117.7 2.1 collective-permute-start.8
  119.9 31.9 %collective-permute-start.9 = (f32[8,4096]{1,0:T(8,128)S(1)}, f32[8,4096]{1,0:T(8,128)S(1)}, u32[]{:S(2)}, u32[]{:S(2)}) collective-permute-start(f32[8,4096]{1,0:T(8,128)S(1)} %copy.64), channel_id=1, source_target_pairs={{0,64},{1,65},{2,66},{3,67},{4,68},{5,69},{6,70},{7,71},{8,72},{9,... | collective-permute-start | bytes 393224 | tf_op jit(solution)/shard_map/ppermute | solution.py:19
  122.1 29.7 %collective-permute-start.11 = (f32[8,4096]{1,0:T(8,128)S(1)}, f32[8,4096]{1,0:T(8,128)S(1)}, u32[]{:S(2)}, u32[]{:S(2)}) collective-permute-start(f32[8,4096]{1,0:T(8,128)S(1)} %collective-permute-done.10), channel_id=1, source_target_pairs={{0,64},{1,65},{2,66},{3,67},{4,68},{5,69},{6,70},{7,71},{8,72},{9,... | collective-permute-start | bytes 393224 | tf_op jit(solution)/shard_map/ppermute | solution.py:19
  221.2 3.2 collective-permute-start.13
  222.5 4.0 collective-permute-start.12
  224.4 6.3 %collective-permute-start.14 = (f32[8,4096]{1,0:T(8,128)S(1)}, f32[8,4096]{1,0:T(8,128)S(1)}, u32[]{:S(2)}, u32[]{:S(2)}) collective-permute-start(f32[8,4096]{1,0:T(8,128)S(1)} %collective-permute-done.13), channel_id=1, source_target_pairs={{0,63},{1,0},{2,1},{3,2},{4,3},{5,4},{6,5},{7,6},{8,7},{9,8},{10,9... | collective-permute-start | bytes 393224 | tf_op jit(solution)/shard_map/ppermute | solution.py:24
  254.9 28.0 %collective-permute-start.16 = (f32[8,1024]{1,0:T(8,128)S(1)}, f32[8,1024]{1,0:T(8,128)S(1)}, u32[]{:S(2)}, u32[]{:S(2)}) collective-permute-start(f32[8,1024]{1,0:T(8,128)S(1)} %get-tuple-element.59), channel_id=1, source_target_pairs={{16,0},{17,1},{18,2},{19,3},{20,4},{21,5},{22,6},{23,7},{24,8},{25... | collective-permute-start | bytes 98312 | tf_op jit(solution)/shard_map/ppermute | solution.py:19
  257.9 51.1 %collective-permute-start.15 = (f32[8,1024]{1,0:T(8,128)S(1)}, f32[8,1024]{1,0:T(8,128)S(1)}, u32[]{:S(2)}, u32[]{:S(2)}) collective-permute-start(f32[8,1024]{1,0:T(8,128)S(1)} %get-tuple-element.60), channel_id=1, source_target_pairs={{0,16},{1,17},{2,18},{3,19},{4,20},{5,21},{6,22},{7,23},{8,24},{9,... | collective-permute-start | bytes 98312 | tf_op jit(solution)/shard_map/ppermute | solution.py:19
  267.8 20.0 %collective-permute-start.20 = (f32[8,1024]{1,0:T(8,128)S(1)}, f32[8,1024]{1,0:T(8,128)S(1)}, u32[]{:S(2)}, u32[]{:S(2)}) collective-permute-start(f32[8,1024]{1,0:T(8,128)S(1)} %squeeze_stack_reshape.27), channel_id=1, source_target_pairs={{1,0},{2,1},{3,2},{4,3},{5,4},{6,5},{7,6},{8,7},{9,8},{10,9},{11,1... | collective-permute-start | bytes 98312 | tf_op jit(solution)/shard_map/ppermute | solution.py:19
  275.6 12.8 %collective-permute-start.19 = (f32[8,1024]{1,0:T(8,128)S(1)}, f32[8,1024]{1,0:T(8,128)S(1)}, u32[]{:S(2)}, u32[]{:S(2)}) collective-permute-start(f32[8,1024]{1,0:T(8,128)S(1)} %squeeze_stack_reshape.26), channel_id=1, source_target_pairs={{0,1},{1,2},{2,3},{3,4},{4,5},{5,6},{6,7},{7,8},{8,9},{9,10},{10,1... | collective-permute-start | bytes 98312 | tf_op jit(solution)/shard_map/ppermute | solution.py:19
  278.2 10.9 %collective-permute-start.18 = (f32[8,1024]{1,0:T(8,128)S(1)}, f32[8,1024]{1,0:T(8,128)S(1)}, u32[]{:S(2)}, u32[]{:S(2)}) collective-permute-start(f32[8,1024]{1,0:T(8,128)S(1)} %squeeze_stack_reshape.25), channel_id=1, source_target_pairs={{4,0},{5,1},{6,2},{7,3},{8,4},{9,5},{10,6},{11,7},{12,8},{13,9},{1... | collective-permute-start | bytes 98312 | tf_op jit(solution)/shard_map/ppermute | solution.py:19
  282.9 10.0 %collective-permute-start.17 = (f32[8,1024]{1,0:T(8,128)S(1)}, f32[8,1024]{1,0:T(8,128)S(1)}, u32[]{:S(2)}, u32[]{:S(2)}) collective-permute-start(f32[8,1024]{1,0:T(8,128)S(1)} %squeeze_stack_reshape.24), channel_id=1, source_target_pairs={{0,4},{1,5},{2,6},{3,7},{4,8},{5,9},{6,10},{7,11},{8,12},{9,13},{1... | collective-permute-start | bytes 98312 | tf_op jit(solution)/shard_map/ppermute | solution.py:19
  341.5 9.3 %collective-permute-start.22 = (f32[8,4096]{1,0:T(8,128)S(1)}, f32[8,4096]{1,0:T(8,128)}, u32[]{:S(2)}, u32[]{:S(2)}) collective-permute-start(f32[8,4096]{1,0:T(8,128)S(1)} %copy.80), channel_id=1, source_target_pairs={{0,1},{1,2},{2,3},{3,4},{4,5},{5,6},{6,7},{7,8},{8,9},{9,10},{10,1... | collective-permute-start | bytes 393224 | tf_op jit(solution)/shard_map/ppermute | solution.py:24
  341.5 38.8 %collective-permute-start.21 = (f32[8,4096]{1,0:T(8,128)S(1)}, f32[8,4096]{1,0:T(8,128)S(1)}, u32[]{:S(2)}, u32[]{:S(2)}) collective-permute-start(f32[8,4096]{1,0:T(8,128)S(1)} %copy.80), channel_id=1, source_target_pairs={{0,64},{1,65},{2,66},{3,67},{4,68},{5,69},{6,70},{7,71},{8,72},{9,... | collective-permute-start | bytes 393224 | tf_op jit(solution)/shard_map/ppermute | solution.py:19
  350.8 29.5 %collective-permute-start.23 = (f32[8,4096]{1,0:T(8,128)}, f32[8,4096]{1,0:T(8,128)S(1)}, u32[]{:S(2)}, u32[]{:S(2)}) collective-permute-start(f32[8,4096]{1,0:T(8,128)} %collective-permute-done.22), channel_id=1, source_target_pairs={{0,64},{1,65},{2,66},{3,67},{4,68},{5,69},{6,70},{7,71},{8,72},{9,... | collective-permute-start | bytes 393224 | tf_op jit(solution)/shard_map/ppermute | solution.py:19
  452.0 3.2 collective-permute-start.25
  453.3 4.0 collective-permute-start.24
  455.2 6.0 collective-permute-start.26
  486.0 60.5 %collective-permute-start.28 = (f32[8,1024]{1,0:T(8,128)S(1)}, f32[8,1024]{1,0:T(8,128)S(1)}, u32[]{:S(2)}, u32[]{:S(2)}) collective-permute-start(f32[8,1024]{1,0:T(8,128)S(1)} %get-tuple-element.37), channel_id=1, source_target_pairs={{16,0},{17,1},{18,2},{19,3},{20,4},{21,5},{22,6},{23,7},{24,8},{25... | collective-permute-start | bytes 98312 | tf_op jit(solution)/shard_map/ppermute | solution.py:19
  488.5 81.5 %collective-permute-start.27 = (f32[8,1024]{1,0:T(8,128)S(1)}, f32[8,1024]{1,0:T(8,128)S(1)}, u32[]{:S(2)}, u32[]{:S(2)}) collective-permute-start(f32[8,1024]{1,0:T(8,128)S(1)} %get-tuple-element.38), channel_id=1, source_target_pairs={{0,16},{1,17},{2,18},{3,19},{4,20},{5,21},{6,22},{7,23},{8,24},{9,... | collective-permute-start | bytes 98312 | tf_op jit(solution)/shard_map/ppermute | solution.py:19
  498.9 50.3 %collective-permute-start.31 = (f32[8,1024]{1,0:T(8,128)S(1)}, f32[8,1024]{1,0:T(8,128)S(1)}, u32[]{:S(2)}, u32[]{:S(2)}) collective-permute-start(f32[8,1024]{1,0:T(8,128)S(1)} %squeeze_stack_reshape.30), channel_id=1, source_target_pairs={{0,1},{1,2},{2,3},{3,4},{4,5},{5,6},{6,7},{7,8},{8,9},{9,10},{10,1... | collective-permute-start | bytes 98312 | tf_op jit(solution)/shard_map/ppermute | solution.py:19
  503.0 47.0 %collective-permute-start.32 = (f32[8,1024]{1,0:T(8,128)S(1)}, f32[8,1024]{1,0:T(8,128)S(1)}, u32[]{:S(2)}, u32[]{:S(2)}) collective-permute-start(f32[8,1024]{1,0:T(8,128)S(1)} %squeeze_stack_reshape.31), channel_id=1, source_target_pairs={{1,0},{2,1},{3,2},{4,3},{5,4},{6,5},{7,6},{8,7},{9,8},{10,9},{11,1... | collective-permute-start | bytes 98312 | tf_op jit(solution)/shard_map/ppermute | solution.py:19
  509.9 41.0 %collective-permute-start.30 = (f32[8,1024]{1,0:T(8,128)S(1)}, f32[8,1024]{1,0:T(8,128)S(1)}, u32[]{:S(2)}, u32[]{:S(2)}) collective-permute-start(f32[8,1024]{1,0:T(8,128)S(1)} %squeeze_stack_reshape.29), channel_id=1, source_target_pairs={{4,0},{5,1},{6,2},{7,3},{8,4},{9,5},{10,6},{11,7},{12,8},{13,9},{1... | collective-permute-start | bytes 98312 | tf_op jit(solution)/shard_map/ppermute | solution.py:19
  546.5 6.8 %collective-permute-start.29 = (f32[8,1024]{1,0:T(8,128)S(1)}, f32[8,1024]{1,0:T(8,128)S(1)}, u32[]{:S(2)}, u32[]{:S(2)}) collective-permute-start(f32[8,1024]{1,0:T(8,128)S(1)} %squeeze_stack_reshape.28), channel_id=1, source_target_pairs={{0,4},{1,5},{2,6},{3,7},{4,8},{5,9},{6,10},{7,11},{8,12},{9,13},{1... | collective-permute-start | bytes 98312 | tf_op jit(solution)/shard_map/ppermute | solution.py:19
  (37 other events, 2473.8 us)
where the time goes:
time: 618 us; the launch traced here: 608 us
  local copies, waits for them, and re-layouts  434 us (70%)
  starting transfers between devices  82.6 us (13%)
  other arithmetic  61.5 us (10%)
  waiting for transfers between devices  26.9 us (4%)
    reshape x8, local copies, waits for them, and re-layouts, to_blocks(): cube = family.reshape(total, 2, BS, 2, BS, 2, BS)  93 us
    ppermute x28, starting transfers between devices, passed_along(): return lax.ppermute(block, axis, route)  76.5 us
    reshape x6, local copies, waits for them, and re-layouts, to_blocks(): return cube.transpose(0, 1, 3, 5, 2, 4, 6).reshape(total * 8, BS * BS * BS)  49.2 us
    reshape x3, local copies, waits for them, and re-layouts, to_family(): cube.transpose(0, 1, 4, 2, 5, 3, 6).reshape(total, 2 * BS, 4 * BS * BS)  42.6 us
    reshape x4, local copies, waits for them, and re-layouts, to_family(): cube = blocks.reshape(total, 2, 2, 2, BS, BS, BS)  31.6 us
    transpose x4, local copies, waits for them, and re-layouts, to_blocks(): return cube.transpose(0, 1, 3, 5, 2, 4, 6).reshape(total * 8, BS * BS * BS)  31.1 us
    transpose x2, local copies, waits for them, and re-layouts, to_family(): cube.transpose(0, 1, 4, 2, 5, 3, 6).reshape(total, 2 * BS, 4 * BS * BS)  30.8 us
    reduce_sum x2, other arithmetic, restrict(): cube.sum(axis=(2, 4, 6)).reshape(total, BS * BS * BS)  27.3 us
  transfers between devices with their start and end apart: 33, of which 9 were waited for; matrix products, arithmetic and copies ran while one was open for 34% of the time, Pallas kernels for 0%

commit v1 on v0

v1 whole, which is shorter than its diff:
```python
import jax
import jax.numpy as jnp
from jax import lax
from jax.experimental import pallas as pl
from jax.experimental.pallas import tpu as pltpu
from jax.sharding import PartitionSpec as P

AX = ("sec", "blk")
N_BLK = 64
FAM = 8
WEIGHT = 0.8 / 6.0
PAD_ROWS = 34 * 64
F32 = jnp.float32
VMEM = pl.BlockSpec(memory_space=pltpu.VMEM)
SMEM = pl.BlockSpec(memory_space=pltpu.SMEM)


def swap_pairs(unit, color):
    pairs, used = [], set()
    for b in range(N_BLK - unit):
        if (b // unit) % 2 == color:
            for s in (0, N_BLK):
                pairs += [(s + b, s + b + unit), (s + b + unit, s + b)]
            used |= {b, b + unit}
    for b in range(N_BLK):
        if b not in used:
            pairs += [(b, N_BLK + b), (N_BLK + b, b)]
    return pairs


def level_pairs(step):
    pairs = []
    for b in range(N_BLK):
        c = N_BLK + (b + step) % N_BLK
        pairs += [(b, c), (c, b)]
    return pairs


UNITS = (16, 4, 1)
HALO_PAIRS = [swap_pairs(unit, color) for unit in UNITS for color in (0, 1)]
OWN_PAIRS = level_pairs(0)
NEXT_PAIRS = level_pairs(1)


def swap(x, pairs):
    return lax.ppermute(x, AX, pairs)


def position():
    return lax.axis_index("sec"), lax.axis_index("blk")


def parities(blk):
    return [(blk >> 4) & 1, (blk >> 2) & 1, blk & 1]


def lane_parts():
    lane = lax.broadcasted_iota(jnp.int32, (8, 128), 1)
    return lane >> 4, lane & 15


def roll(x, by):
    return pltpu.roll(x, by, 1)


def rows(ref, start, size=8):
    return ref[pl.ds(pl.multiple_of(start, 8), size), :]


def put(ref, start, value):
    ref[pl.ds(pl.multiple_of(start, 8), value.shape[0]), :] = value


def plane(ref, x):
    base = (x + 1) * 64
    return [[rows(ref, base + (q * 2 + oz) * 8) for oz in range(2)] for q in range(4)]


def around(a, below, above, ylo, z, hy=None, hz=None):
    zero = jnp.zeros((8, 128), F32)
    if hy is None:
        hy = [[zero, zero], [zero, zero]]
    if hz is None:
        hz = [[zero, zero] for _ in range(4)]
    y_first, y_last = ylo == 0, ylo == 7
    z_first, z_last = z == 0, z == 15
    down = [[roll(a[q][o], 16) for o in range(2)] for q in range(4)]
    up = [[roll(a[q][o], 112) for o in range(2)] for q in range(4)]
    total = []
    for q in range(4):
        line = []
        for o in range(2):
            low_y = jnp.where(y_first, down[q - 1][o] if q else hy[0][o], down[q][o])
            high_y = jnp.where(y_last, up[q + 1][o] if q < 3 else hy[1][o], up[q][o])
            if o == 0:
                low_z = jnp.where(z_first, hz[q][0], roll(a[q][0], 1))
                high_z = roll(jnp.where(z_first, down[q][1], a[q][0]), 127)
            else:
                low_z = roll(jnp.where(z_last, up[q][0], a[q][1]), 1)
                high_z = jnp.where(z_last, hz[q][1], roll(a[q][1], 127))
            line.append((low_y + high_y) + (low_z + high_z) + (below[q][o] + above[q][o]))
        total.append(line)
    return total


def clear_pads(ref):
    for start in (0, 33 * 64):
        ref[start : start + 64, :] = jnp.zeros((64, 128), F32)


def smooth(rhs, mid, emit):
    ylo, z = lane_parts()
    clear_pads(rhs)
    clear_pads(mid)

    def first(x, _):
        a = plane(rhs, x)
        m = around(a, plane(rhs, x - 1), plane(rhs, x + 1), ylo, z)
        for q in range(4):
            for o in range(2):
                put(mid, (x + 1) * 64 + (q * 2 + o) * 8, 1.2 * a[q][o] + WEIGHT * m[q][o])
        return 0

    def second(x, _):
        a = plane(mid, x)
        m = around(a, plane(mid, x - 1), plane(mid, x + 1), ylo, z)
        for q in range(4):
            for o in range(2):
                at = (x + 1) * 64 + (q * 2 + o) * 8
                emit(at, WEIGHT * (rows(rhs, at) + 0.2 * a[q][o] + WEIGHT * m[q][o]))
        return 0

    lax.fori_loop(0, 32, first, 0)
    lax.fori_loop(0, 32, second, 0)


def restrict_pair(p, i, ylo, z, down):
    z_even, y_even = (z & 1) == 0, (ylo & 1) == 0
    index = (2 * (ylo & 3) + (ylo >> 2)) * 16 + 2 * (z & 7) + (z >> 3)
    for oy in range(2):
        u = []
        for a in range(2):
            lo, hi = p[2 * oy + a]
            u.append(jnp.where(z_even, lo + roll(lo, 127), hi + roll(hi, 1)))
        m = jnp.where(y_even, u[0] + roll(u[0], 112), u[1] + roll(u[1], 16))
        put(down, (oy * 16 + i) * 8, 0.5 * jnp.take_along_axis(m, index, axis=1))


def parent_slots(parent, blk):
    own_count, next_count = jnp.int32(0), jnp.int32(0)
    found = []
    for g in range(FAM):
        value = parent[g]
        chip = (value >> 6) - N_BLK
        to_own = (value >= 0) & (chip == blk)
        to_next = (value >= 0) & (chip == ((blk + 1) & (N_BLK - 1)))
        found.append((to_own, to_next, own_count, next_count, value & 63))
        own_count = own_count + to_own.astype(jnp.int32)
        next_count = next_count + to_next.astype(jnp.int32)
    return found


def send_down(down, parent, blk, own, nxt, tags):
    for buf in (own, nxt):
        if tags:
            buf[128:136, :] = jnp.full((8, 128), -1.0, F32)
    for g, (to_own, to_next, own_slot, next_slot, block) in enumerate(parent_slots(parent, blk)):
        for going, slot, buf in ((to_own, own_slot, own), (to_next, next_slot, nxt)):

            @pl.when(going)
            def _(slot=slot, buf=buf, block=block, g=g):
                put(buf, slot * 32, down[pl.ds(g, 32, stride=8), :])
                if tags:
                    buf[pl.ds(128 + slot, 1), :] = jnp.full((1, 128), block.astype(F32), F32)


def block_start(block):
    f, o = block >> 3, block & 7
    return ((o >> 2) * 16 + 1) * 64 + (((o >> 1) & 1) * 4 + (o & 1)) * 8 + f


def add_incoming(rhs, tags, arrived):
    for j in range(8):
        buf, slot, tag = arrived[j // 4], j % 4, tags[j]

        @pl.when(tag >= 0)
        def _(buf=buf, slot=slot, tag=tag):
            start = block_start(tag)
            for yh in range(2):
                at = pl.ds(start + yh * 16, 16, stride=64)
                rhs[at, :] = rhs[at, :] + buf[slot * 32 + yh * 16 : slot * 32 + yh * 16 + 16, :]


def answer(correction, tags, out):
    for j in range(8):
        buf, slot, tag = out[j // 4], j % 4, tags[j]

        @pl.when(tag >= 0)
        def _(buf=buf, slot=slot, tag=tag):
            start = block_start(tag)
            for yh in range(2):
                buf[slot * 32 + yh * 16 : slot * 32 + yh * 16 + 16, :] = correction[
                    pl.ds(start + yh * 16, 16, stride=64), :
                ]


def first_down_kernel(parent, source, own, nxt, down):
    sec, blk = position()
    ylo, z = lane_parts()

    @pl.when(sec == 0)
    def _():
        def pair(i, _):
            x = (2 * i) & 15
            ox4 = (i >> 3) * 4
            p = []
            for q in range(4):
                line = []
                for oz in range(2):
                    o = ox4 + (q // 2) * 2 + oz
                    c = x * 2 + q % 2
                    line.append(
                        source[pl.ds(c * 8 + o, 8, stride=256), :]
                        + source[pl.ds((c + 2) * 8 + o, 8, stride=256), :]
                    )
                p.append(line)
            restrict_pair(p, i, ylo, z, down)
            return 0

        lax.fori_loop(0, 16, pair, 0)
        send_down(down, parent, blk, own, nxt, True)


def load_kernel(source, src, sol, mid):
    sec, _ = position()

    def copy(x, _):
        for ox in range(2):
            for q in range(4):
                for oz in range(2):
                    o = ox * 4 + (q // 2) * 2 + oz
                    c = x * 2 + q % 2
                    put(src, (ox * 16 + x + 1) * 64 + (q * 2 + oz) * 8, source[pl.ds(c * 8 + o, 8, stride=256), :])
        return 0

    lax.fori_loop(0, 16, copy, 0)

    @pl.when(sec == 0)
    def _():
        def emit(at, value):
            put(sol, at, value)

        smooth(src, mid, emit)


def coarse_kernel(first, *refs):
    if first:
        res, sol, in_own, in_next, out_sol, out_own, out_next, tags, rhs, mid, smem, sem = refs
    else:
        tags, res, sol, in_own, in_next, out_sol, out_own, out_next, rhs, mid, corr = refs
    sec, _ = position()

    if first:
        for j in range(8):
            tags[j] = jnp.int32(-1)

    @pl.when(sec == 0)
    def _():
        def copy(i, _):
            put(out_sol, i * 64, rows(sol, i * 64, 64))
            return 0

        lax.fori_loop(1, 33, copy, 0)

    @pl.when(sec == 1)
    def _():
        if first:
            copies = [
                pltpu.make_async_copy(buf.at[128:136, :], smem.at[k], sem.at[k])
                for k, buf in enumerate((in_own, in_next))
            ]
            for c in copies:
                c.start()

        def copy(i, _):
            put(rhs, i * 64, rows(res, i * 64, 64))
            return 0

        lax.fori_loop(1, 33, copy, 0)
        if first:
            for k, c in enumerate(copies):
                c.wait()
                for j in range(4):
                    tags[k * 4 + j] = smem[k, j, 0].astype(jnp.int32)
        add_incoming(rhs, tags, (in_own, in_next))

        def emit(at, value):
            if first:
                put(out_sol, at, value)
            else:
                put(corr, at, value)
                put(out_sol, at, rows(sol, at) + value)

        smooth(rhs, mid, emit)
        answer(out_sol if first else corr, tags, (out_own, out_next))


def lift_kernel(parent, sol, in_own, in_next, out_sol, *refs):
    out, (lift, face) = refs[:6], refs[6:]
    sec, blk = position()
    ylo, z = lane_parts()

    @pl.when(sec == 1)
    def _():
        def copy(i, _):
            put(out_sol, i * 64, rows(sol, i * 64, 64))
            return 0

        lax.fori_loop(1, 33, copy, 0)

    @pl.when(sec == 0)
    def _():
        for g, (to_own, to_next, own_slot, next_slot, _) in enumerate(parent_slots(parent, blk)):
            at = pl.ds(g, 32, stride=8)

            @pl.when(to_own)
            def _(at=at, slot=own_slot):
                lift[at, :] = rows(in_own, slot * 32, 32)

            @pl.when(to_next)
            def _(at=at, slot=next_slot):
                lift[at, :] = rows(in_next, slot * 32, 32)

            @pl.when(jnp.logical_not(to_own | to_next))
            def _(at=at):
                lift[at, :] = jnp.zeros((32, 128), F32)

        index = [[(4 * a + (ylo >> 1)) * 16 + 8 * b + (z >> 1) for b in range(2)] for a in range(2)]

        def add(i, _):
            for oy in range(2):
                value = rows(lift, (oy * 16 + i) * 8)
                for a in range(2):
                    for b in range(2):
                        wide = jnp.take_along_axis(value, index[a][b], axis=1)
                        for x in range(2):
                            at = (2 * i + x + 1) * 64 + ((2 * oy + a) * 2 + b) * 8
                            put(out_sol, at, rows(sol, at) + wide)
            return 0

        lax.fori_loop(0, 16, add, 0)

    put(face, 0, rows(out_sol, 64, 64))
    put(face, 64, rows(out_sol, 32 * 64, 64))

    def pack(x, _):
        base = (x + 1) * 64
        y_at, z_at = x & 7, x & 15
        y_mask, z_mask = ylo == y_at, z == z_at
        for oz in range(2):
            at = (oz * 4 + (x >> 3)) * 8
            low = roll(rows(out_sol, base + oz * 8), 16 * y_at)
            high = roll(rows(out_sol, base + (6 + oz) * 8), (16 * y_at + 16) & 127)
            put(face, 128 + at, jnp.where(y_mask, low, rows(face, 128 + at)))
            put(face, 192 + at, jnp.where(y_mask, high, rows(face, 192 + at)))
        for q in range(4):
            at = (q * 2 + (x >> 4)) * 8
            low = roll(rows(out_sol, base + q * 16), z_at)
            high = roll(rows(out_sol, base + q * 16 + 8), (z_at + 113) & 127)
            put(face, 256 + at, jnp.where(z_mask, low, rows(face, 256 + at)))
            put(face, 320 + at, jnp.where(z_mask, high, rows(face, 320 + at)))
        return 0

    lax.fori_loop(0, 32, pack, 0)
    for axis, parity in enumerate(parities(blk)):
        for color in range(2):
            d = 2 * axis + (parity == color).astype(jnp.int32)
            out[2 * axis + color][...] = rows(face, d * 64, 64)


def residual_kernel(last, parent, neighbor, src, sol, *refs):
    sent, got = refs[:6], refs[6:12]
    if last:
        res, halo, table = refs[12:]
    else:
        res, own, nxt, halo, table, down = refs[12:]
    sec, blk = position()
    ylo, z = lane_parts()

    for axis, parity in enumerate(parities(blk)):
        for color in range(2):
            odd = (parity == color).astype(jnp.int32)
            put(table, (2 * axis + 1 - odd) * 128, sent[2 * axis + color][...])
            put(table, (2 * axis + odd) * 128 + 64, got[2 * axis + color][...])
    device = sec * N_BLK + blk

    def gather(g, _):
        for d in range(6):
            other = neighbor[g, d]
            local = (other >> 3) == device
            start = d * 128 + jnp.where(local, 0, 64) + (other & 7)
            value = table[pl.ds(start, 8, stride=8), :]
            halo[pl.ds(d * 64 + g, 8, stride=8), :] = jnp.where(other >= 0, value, 0.0)
        return 0

    lax.fori_loop(0, FAM, gather, 0)

    def side(base):
        return [[rows(halo, base + (q * 2 + o) * 8) for o in range(2)] for q in range(4)]

    def residue(x, below, above):
        a = plane(sol, x)
        y_at, z_at = x & 7, x & 15
        y_rows = [128 + (o * 4 + (x >> 3)) * 8 for o in range(2)]
        hy = [
            [roll(rows(halo, y_rows[o]), (128 - 16 * y_at) & 127) for o in range(2)],
            [roll(rows(halo, y_rows[o] + 64), 112 - 16 * y_at) for o in range(2)],
        ]
        hz = []
        for q in range(4):
            at = 256 + (q * 2 + (x >> 4)) * 8
            hz.append([roll(rows(halo, at), (128 - z_at) & 127), roll(rows(halo, at + 64), 15 - z_at)])
        m = around(a, below, above, ylo, z, hy, hz)
        s = plane(src, x)
        return [[s[q][o] - 6.0 * a[q][o] + m[q][o] for o in range(2)] for q in range(4)]

    def store(x, r):
        if last:
            for q in range(4):
                for o in range(2):
                    octant = (x >> 4) * 4 + (q // 2) * 2 + o
                    c = (x & 15) * 2 + q % 2
                    res[pl.ds(c * 8 + octant, 8, stride=256), :] = r[q][o]
        else:
            for q in range(4):
                for o in range(2):
                    put(res, (x + 1) * 64 + (q * 2 + o) * 8, r[q][o])

    def pair(i, _, low=None, high=None):
        x = 2 * i
        r0 = residue(x, plane(sol, x - 1) if low is None else low, plane(sol, x + 1))
        r1 = residue(x + 1, plane(sol, x), plane(sol, x + 2) if high is None else high)
        store(x, r0)
        store(x + 1, r1)
        if not last:

            @pl.when(sec == 0)
            def _():
                p = [[r0[q][o] + r1[q][o] for o in range(2)] for q in range(4)]
                restrict_pair(p, i, ylo, z, down)

        return 0

    pair(0, 0, low=side(0))
    lax.fori_loop(1, 15, pair, 0)
    pair(15, 0, high=side(64))
    if not last:

        @pl.when(sec == 0)
        def _():
            send_down(down, parent, blk, own, nxt, False)


def fine_kernel(res, sol, out_sol, rhs, mid):
    sec, _ = position()

    @pl.when(sec == 1)
    def _():
        def copy(i, _):
            put(out_sol, i * 64, rows(sol, i * 64, 64))
            return 0

        lax.fori_loop(1, 33, copy, 0)

    @pl.when(sec == 0)
    def _():
        def copy(i, _):
            put(rhs, i * 64, rows(res, i * 64, 64))
            return 0

        lax.fori_loop(1, 33, copy, 0)

        def emit(at, value):
            put(out_sol, at, rows(sol, at) + value)

        smooth(rhs, mid, emit)


def unload_kernel(sol, out):
    def copy(x, _):
        for ox in range(2):
            for q in range(4):
                for oz in range(2):
                    o = ox * 4 + (q // 2) * 2 + oz
                    c = x * 2 + q % 2
                    out[pl.ds(c * 8 + o, 8, stride=256), :] = rows(sol, (ox * 16 + x + 1) * 64 + (q * 2 + oz) * 8)
        return 0

    lax.fori_loop(0, 16, copy, 0)


def shape(n, dtype=F32):
    return jax.ShapeDtypeStruct((n, 128), dtype)


def scratch(n):
    return pltpu.VMEM((n, 128), F32)


def call(kernel, name, in_specs, out_shape, scratch_shapes=(), out_specs=None):
    return pl.pallas_call(
        kernel,
        name=name,
        in_specs=in_specs,
        out_shape=out_shape,
        out_specs=out_specs or [VMEM] * len(out_shape),
        scratch_shapes=list(scratch_shapes),
        compiler_params=pltpu.CompilerParams(vmem_limit_bytes=32 << 20),
    )


def local(source, parent, neighbor):
    tiles = source.reshape(FAM, 8, 32, 128).transpose(0, 2, 1, 3).reshape(2048, 128)
    pad, pads = shape(PAD_ROWS), scratch(PAD_ROWS)

    def both(own, nxt):
        return swap(nxt, NEXT_PAIRS), swap(own, OWN_PAIRS)

    own, nxt = call(first_down_kernel, "first_down", [SMEM, VMEM], (shape(136), shape(136)), [scratch(256)])(
        parent, tiles
    )
    got_next, got_own = both(own, nxt)
    src, sol = call(load_kernel, "load", [VMEM], (pad, pad), [pads])(tiles)
    res, tags = src, None
    for iteration in range(2):
        first = iteration == 0
        if first:
            sol, own, nxt, tags = call(
                lambda *refs: coarse_kernel(True, *refs),
                "coarse_0",
                [VMEM] * 4,
                (pad, shape(128), shape(128), jax.ShapeDtypeStruct((8,), jnp.int32)),
                [pads, pads, pltpu.SMEM((2, 8, 128), F32), pltpu.SemaphoreType.DMA((2,))],
                [VMEM, VMEM, VMEM, SMEM],
            )(res, sol, got_own, got_next)
        else:
            sol, own, nxt = call(
                lambda *refs: coarse_kernel(False, *refs),
                "coarse_1",
                [SMEM] + [VMEM] * 4,
                (pad, shape(128), shape(128)),
                [pads, pads, pads],
            )(tags, res, sol, got_own, got_next)
        got_next, got_own = both(own, nxt)
        out = call(
            lift_kernel,
            f"lift_{iteration}",
            [SMEM, VMEM, VMEM, VMEM],
            (pad,) + (shape(64),) * 6,
            [scratch(256), scratch(384)],
        )(parent, sol, got_own, got_next)
        sol, sent = out[0], out[1:]
        got = [swap(s, pairs) for s, pairs in zip(sent, HALO_PAIRS)]
        ins = [SMEM, SMEM] + [VMEM] * 14
        if first:
            res, own, nxt = call(
                lambda *refs: residual_kernel(False, *refs),
                "residual_0",
                ins,
                (pad, shape(128), shape(128)),
                [scratch(384), scratch(768), scratch(256)],
            )(parent, neighbor, src, sol, *sent, *got)
            got_next, got_own = both(own, nxt)
            (sol,) = call(fine_kernel, "fine", [VMEM, VMEM], (pad,), [pads, pads])(res, sol)
        else:
            (solution,) = call(unload_kernel, "unload", [VMEM], (shape(2048),))(sol)
            (residual,) = call(
                lambda *refs: residual_kernel(True, *refs),
                "residual_1",
                ins,
                (shape(2048),),
                [scratch(384), scratch(768)],
            )(parent, neighbor, src, sol, *sent, *got)

    def blocks(x):
        return x.reshape(FAM, 32, 8, 128).transpose(0, 2, 1, 3).reshape(64, 4096)

    return blocks(solution), blocks(residual)


def solution(mesh):
    return jax.shard_map(
        local,
        mesh=mesh,
        in_specs=(P(AX, None), P(AX), P(AX, None)),
        out_specs=(P(AX, None), P(AX, None)),
        check_vma=False,
    )
```

time: 618 us -> 102 us (0.17)
  the two profiles are of different devices: /device:TPU:18 before, /device:TPU:3 now
where the time goes in v1:
time: 102 us
  Pallas kernels  41.1 us (40%)
  starting transfers between devices  29.4 us (29%)
  waiting for transfers between devices  28.9 us (28%)
  local copies, waits for them, and re-layouts  1.88 us (2%)
    ppermute x20, starting transfers between devices, swap(): return lax.ppermute(x, AX, pairs)  29.4 us
    ppermute x20, waiting for transfers between devices, swap(): return lax.ppermute(x, AX, pairs)  28.9 us
    pallas_call x1, Pallas kernels, local(): call(lambda *refs: coarse_kernel(True, *refs), 'coarse_0', [VMEM] * 4, (p...  11.5 us
    pallas_call x1, Pallas kernels, local(): call(lambda *refs: coarse_kernel(False, *refs), 'coarse_1', [SMEM] + [VME...  11 us
    pallas_call x2, Pallas kernels, local(): call(lift_kernel, f'lift_{iteration}', [SMEM, VMEM, VMEM, VMEM], (pad,) +...  6.74 us
    pallas_call x1, Pallas kernels, local(): call(lambda *refs: residual_kernel(True, *refs), 'residual_1', ins, (shap...  4.96 us
    pallas_call x1, Pallas kernels, local(): call(lambda *refs: residual_kernel(False, *refs), 'residual_0', ins, (pad...  3.91 us
  transfers between devices with their start and end apart: 20, of which 11 were waited for; matrix products, arithmetic and copies ran while one was open for 0% of the time, Pallas kernels for 2%

profile of v1, /device:TPU:3, one launch (start us, length us, event | category | flops | bytes accessed | tf_op | source)
XLA Modules:
  0.0 102.0 jit_solution(6617623279561122024)
XLA Ops:
  0.6 1.2 %copy-done = f32[64,4096]{1,0:T(8,128)S(1)} copy-done((f32[64,4096]{1,0:T(8,128)S(1)}, f32[64,4096]{1,0:T(8,128)}, u32[]{:S(2)}) %copy-start) | copy-done | bytes 1048600
  1.9 0.7 copy-done.2
  2.5 0.6 first_down.1
  3.1 4.8 %collective-permute-start = (f32[136,128]{1,0:T(8,128)S(1)}, f32[136,128]{1,0:T(8,128)S(1)}, u32[]{:S(2)}, u32[]{:S(2)}) collective-permute-start(f32[136,128]{1,0:T(8,128)S(1)} %get-tuple-element.32), channel_id=1, source_target_pairs={{0,64},{64,0},{1,65},{65,1},{2,66},{66,2},{3,67},{67,3},{4,68},{68... | collective-permute-start | bytes 208904 | tf_op jit(solution)/shard_map/ppermute | solution.py:46
  7.9 6.2 %collective-permute-start.1 = (f32[136,128]{1,0:T(8,128)S(1)}, f32[136,128]{1,0:T(8,128)S(1)}, u32[]{:S(2)}, u32[]{:S(2)}) collective-permute-start(f32[136,128]{1,0:T(8,128)S(1)} %get-tuple-element.33), channel_id=1, source_target_pairs={{0,65},{65,0},{1,66},{66,1},{2,67},{67,2},{3,68},{68,3},{4,69},{69... | collective-permute-start | bytes 208904 | tf_op jit(solution)/shard_map/ppermute | solution.py:46
  14.0 0.7 load.1
  14.7 0.0 collective-permute-done.refs_2_
  14.7 1.3 %collective-permute-done.1.refs_3_ = f32[136,128]{1,0:T(8,128)S(1)} collective-permute-done((f32[136,128]{1,0:T(8,128)S(1)}, f32[136,128]{1,0:T(8,128)S(1)}, u32[]{:S(2)}, u32[]{:S(2)}) %collective-permute-start.1) | collective-permute-done | bytes 69664 | tf_op jit(solution)/shard_map/ppermute | solution.py:46
  16.0 11.5 %coarse_0.1 = (f32[2176,128]{1,0:T(8,128)S(1)}, f32[128,128]{1,0:T(8,128)S(1)}, f32[128,128]{1,0:T(8,128)S(1)}, s32[8]{0:T(128)S(1)}) custom-call(f32[2176,128]{1,0:T(8,128)S(1)} %get-tuple-element.30.refs_0_.refs_2_, f32[2176,128]{1,0:T(8,128)S(1)} %get-tuple-element.31.refs_1_, f32[136,128]{1,0:T(8,128)S(1)} %collective-permute-done.refs_2_, ...), custom_call_target="tpu_custom_call" | custom-call | tf_op jit(solution)/shard_map/coarse_0/pallas_call | solution.py:538
  27.5 0.0 copy-start.1
  27.5 0.1 collective-permute-start.2
  27.6 2.1 %collective-permute-start.3 = (f32[128,128]{1,0:T(8,128)S(1)}, f32[128,128]{1,0:T(8,128)S(1)}, u32[]{:S(2)}, u32[]{:S(2)}) collective-permute-start(f32[128,128]{1,0:T(8,128)S(1)} %get-tuple-element.37), channel_id=1, source_target_pairs={{0,65},{65,0},{1,66},{66,1},{2,67},{67,2},{3,68},{68,3},{4,69},{69... | collective-permute-start | bytes 196616 | tf_op jit(solution)/shard_map/ppermute | solution.py:46
  29.8 0.0 collective-permute-done.2.in_own
  29.8 5.8 %collective-permute-done.3.in_next = f32[128,128]{1,0:T(8,128)S(1)} collective-permute-done((f32[128,128]{1,0:T(8,128)S(1)}, f32[128,128]{1,0:T(8,128)S(1)}, u32[]{:S(2)}, u32[]{:S(2)}) %collective-permute-start.3) | collective-permute-done | bytes 65568 | tf_op jit(solution)/shard_map/ppermute | solution.py:46
  35.6 3.4 %lift_0.1 = (f32[2176,128]{1,0:T(8,128)S(1)}, f32[64,128]{1,0:T(8,128)S(1)}, f32[64,128]{1,0:T(8,128)S(1)}, f32[64,128]{1,0:T(8,128)S(1)}, f32[64,128]{1,0:T(8,1...) custom-call(s32[8]{0:T(128)S(1)} %copy-done.2, f32[2176,128]{1,0:T(8,128)S(1)} %get-tuple-element.35.sol, ...), custom_call_target="tpu_custom_call" | custom-call | tf_op jit(solution)/shard_map/lift_0/pallas_call | solution.py:555
  39.0 3.8 %collective-permute-start.4 = (f32[64,128]{1,0:T(8,128)S(1)}, f32[64,128]{1,0:T(8,128)S(1)}, u32[]{:S(2)}, u32[]{:S(2)}) collective-permute-start(f32[64,128]{1,0:T(8,128)S(1)} %get-tuple-element.39.refs_4_), channel_id=1, source_target_pairs={{0,16},{16,0},{64,80},{80,64},{1,17},{17,1},{65,81},{81,65},{2,18}... | collective-permute-start | bytes 98312 | tf_op jit(solution)/shard_map/ppermute | solution.py:46
  42.8 0.0 collective-permute-start.5
  42.8 0.1 collective-permute-start.8
  42.9 1.5 %collective-permute-done.4.refs_10_ = f32[64,128]{1,0:T(8,128)S(1)} collective-permute-done((f32[64,128]{1,0:T(8,128)S(1)}, f32[64,128]{1,0:T(8,128)S(1)}, u32[]{:S(2)}, u32[]{:S(2)}) %collective-permute-start.4) | collective-permute-done | bytes 32800 | tf_op jit(solution)/shard_map/ppermute | solution.py:46
  44.4 0.0 collective-permute-start.9
  44.4 1.2 %collective-permute-done.5.refs_11_ = f32[64,128]{1,0:T(8,128)S(1)} collective-permute-done((f32[64,128]{1,0:T(8,128)S(1)}, f32[64,128]{1,0:T(8,128)S(1)}, u32[]{:S(2)}, u32[]{:S(2)}) %collective-permute-start.5) | collective-permute-done | bytes 32800 | tf_op jit(solution)/shard_map/ppermute | solution.py:46
  45.5 0.0 collective-permute-done.6.refs_12_
  45.5 2.1 %collective-permute-done.7.refs_13_ = f32[64,128]{1,0:T(8,128)S(1)} collective-permute-done((f32[64,128]{1,0:T(8,128)S(1)}, f32[64,128]{1,0:T(8,128)S(1)}, u32[]{:S(2)}, u32[]{:S(2)}) %collective-permute-start.7) | collective-permute-done | bytes 32800 | tf_op jit(solution)/shard_map/ppermute | solution.py:46
  47.6 0.0 collective-permute-done.8.refs_14_
  47.6 3.7 %collective-permute-done.9.refs_15_ = f32[64,128]{1,0:T(8,128)S(1)} collective-permute-done((f32[64,128]{1,0:T(8,128)S(1)}, f32[64,128]{1,0:T(8,128)S(1)}, u32[]{:S(2)}, u32[]{:S(2)}) %collective-permute-start.9) | collective-permute-done | bytes 32800 | tf_op jit(solution)/shard_map/ppermute | solution.py:46
  51.3 3.9 %residual_0.1 = (f32[2176,128]{1,0:T(8,128)S(1)}, f32[128,128]{1,0:T(8,128)S(1)}, f32[128,128]{1,0:T(8,128)S(1)}) custom-call(s32[8]{0:T(128)S(1)} %copy-done.2, s32[8,6]{1,0:T(8,128)S(1)} %copy-done.1, f32[2176,128]{1,0:T(8,128)S(1)} %get-tuple-element.30.refs_0_.refs_2_, f32[2176,128]{1,0:T(8,128)S(1)} %get-tuple-element.38.refs_3_.sol, ...), custom_call_target="tpu_custom_call" | custom-call | tf_op jit(solution)/shard_map/residual_0/pallas_call | solution.py:566
  55.3 1.6 %collective-permute-start.10 = (f32[128,128]{1,0:T(8,128)S(1)}, f32[128,128]{1,0:T(8,128)S(1)}, u32[]{:S(2)}, u32[]{:S(2)}) collective-permute-start(f32[128,128]{1,0:T(8,128)S(1)} %get-tuple-element.46), channel_id=1, source_target_pairs={{0,64},{64,0},{1,65},{65,1},{2,66},{66,2},{3,67},{67,3},{4,68},{68... | collective-permute-start | bytes 196616 | tf_op jit(solution)/shard_map/ppermute | solution.py:46
  56.9 5.2 %collective-permute-start.11 = (f32[128,128]{1,0:T(8,128)S(1)}, f32[128,128]{1,0:T(8,128)S(1)}, u32[]{:S(2)}, u32[]{:S(2)}) collective-permute-start(f32[128,128]{1,0:T(8,128)S(1)} %get-tuple-element.47), channel_id=1, source_target_pairs={{0,65},{65,0},{1,66},{66,1},{2,67},{67,2},{3,68},{68,3},{4,69},{69... | collective-permute-start | bytes 196616 | tf_op jit(solution)/shard_map/ppermute | solution.py:46
  62.1 0.2 fine.1.refs_2_
  62.3 0.0 collective-permute-done.10.refs_3_
  62.3 2.5 %collective-permute-done.11.refs_4_ = f32[128,128]{1,0:T(8,128)S(1)} collective-permute-done((f32[128,128]{1,0:T(8,128)S(1)}, f32[128,128]{1,0:T(8,128)S(1)}, u32[]{:S(2)}, u32[]{:S(2)}) %collective-permute-start.11) | collective-permute-done | bytes 65568 | tf_op jit(solution)/shard_map/ppermute | solution.py:46
  64.8 11.0 %coarse_1.1 = (f32[2176,128]{1,0:T(8,128)S(1)}, f32[128,128]{1,0:T(8,128)S(1)}, f32[128,128]{1,0:T(8,128)S(1)}) custom-call(s32[8]{0:T(128)S(1)} %get-tuple-element.34.refs_0_, f32[2176,128]{1,0:T(8,128)S(1)} %get-tuple-element.45.res.refs_1_, f32[2176,128]{1,0:T(8,128)S(1)} %fine.1.refs_2_, f32[128,128]{1,0:T(8,128)S(1)} %collective-permute-done.10.refs_3_, ...), custom_call_target="tpu_custom_call" | custom-call | tf_op jit(solution)/shard_map/coarse_1/pallas_call | solution.py:547
  75.8 0.1 collective-permute-start.12
  75.9 1.4 %collective-permute-start.13 = (f32[128,128]{1,0:T(8,128)S(1)}, f32[128,128]{1,0:T(8,128)S(1)}, u32[]{:S(2)}, u32[]{:S(2)}) collective-permute-start(f32[128,128]{1,0:T(8,128)S(1)} %get-tuple-element.50), channel_id=1, source_target_pairs={{0,65},{65,0},{1,66},{66,1},{2,67},{67,2},{3,68},{68,3},{4,69},{69... | collective-permute-start | bytes 196616 | tf_op jit(solution)/shard_map/ppermute | solution.py:46
  77.3 0.0 collective-permute-done.12.in_own
  77.3 6.6 %collective-permute-done.13.in_next = f32[128,128]{1,0:T(8,128)S(1)} collective-permute-done((f32[128,128]{1,0:T(8,128)S(1)}, f32[128,128]{1,0:T(8,128)S(1)}, u32[]{:S(2)}, u32[]{:S(2)}) %collective-permute-start.13) | collective-permute-done | bytes 65568 | tf_op jit(solution)/shard_map/ppermute | solution.py:46
  83.9 3.4 %lift_1.1 = (f32[2176,128]{1,0:T(8,128)S(1)}, f32[64,128]{1,0:T(8,128)S(1)}, f32[64,128]{1,0:T(8,128)S(1)}, f32[64,128]{1,0:T(8,128)S(1)}, f32[64,128]{1,0:T(8,1...) custom-call(s32[8]{0:T(128)S(1)} %copy-done.2, f32[2176,128]{1,0:T(8,128)S(1)} %get-tuple-element.48.sol, ...), custom_call_target="tpu_custom_call" | custom-call | tf_op jit(solution)/shard_map/lift_1/pallas_call | solution.py:555
  87.3 0.6 collective-permute-start.14
  87.8 1.6 %collective-permute-start.15 = (f32[64,128]{1,0:T(8,128)S(1)}, f32[64,128]{1,0:T(8,128)S(1)}, u32[]{:S(2)}, u32[]{:S(2)}) collective-permute-start(f32[64,128]{1,0:T(8,128)S(1)} %get-tuple-element.53.refs_5_), channel_id=1, source_target_pairs={{16,32},{32,16},{80,96},{96,80},{17,33},{33,17},{81,97},{97,81},{1... | collective-permute-start | bytes 98312 | tf_op jit(solution)/shard_map/ppermute | solution.py:46
  89.4 0.0 collective-permute-start.16
  89.4 0.0 collective-permute-start.17
  89.4 0.0 collective-permute-start.18
  89.4 0.7 collective-permute-done.14.refs_10_
  90.1 1.8 %collective-permute-start.19 = (f32[64,128]{1,0:T(8,128)S(1)}, f32[64,128]{1,0:T(8,128)S(1)}, u32[]{:S(2)}, u32[]{:S(2)}) collective-permute-start(f32[64,128]{1,0:T(8,128)S(1)} %get-tuple-element.57.refs_9_), channel_id=1, source_target_pairs={{1,2},{2,1},{65,66},{66,65},{3,4},{4,3},{67,68},{68,67},{5,6},{6,5... | collective-permute-start | bytes 98312 | tf_op jit(solution)/shard_map/ppermute | solution.py:46
  91.9 1.6 %unload.1 = f32[2048,128]{1,0:T(8,128)} custom-call(f32[2176,128]{1,0:T(8,128)S(1)} %get-tuple-element.51.sol.refs_3_), custom_call_target="tpu_custom_call" | custom-call | tf_op jit(solution)/shard_map/unload/pallas_call | solution.py:576
  93.5 0.8 collective-permute-done.17.refs_13_
  94.3 2.8 %collective-permute-done.19.refs_15_ = f32[64,128]{1,0:T(8,128)S(1)} collective-permute-done((f32[64,128]{1,0:T(8,128)S(1)}, f32[64,128]{1,0:T(8,128)S(1)}, u32[]{:S(2)}, u32[]{:S(2)}) %collective-permute-start.19) | collective-permute-done | bytes 32800 | tf_op jit(solution)/shard_map/ppermute | solution.py:46
  97.1 5.0 %residual_1.1 = f32[2048,128]{1,0:T(8,128)} custom-call(s32[8]{0:T(128)S(1)} %copy-done.2, s32[8,6]{1,0:T(8,128)S(1)} %copy-done.1, f32[2176,128]{1,0:T(8,128)S(1)} %get-tuple-element.30.refs_0_.refs_2_, f32[2176,128]{1,0:T(8,128)S(1)} %get-tuple-element.51.sol.refs_3_, f32[64,128]{1,0:T(8,128)S(1)} %get-tuple-element.52.refs_4_, ...), custom_call_target="tpu_custom_call" | custom-call | tf_op jit(solution)/shard_map/residual_1/pallas_call | solution.py:577
  (8 shorter events, 0.0 us)
Async XLA Ops:
  0.6 1.2 %copy-start = (f32[64,4096]{1,0:T(8,128)S(1)}, f32[64,4096]{1,0:T(8,128)}, u32[]{:S(2)}) copy-start(f32[64,4096]{1,0:T(8,128)} %param.3) | copy-start | bytes 3145732
  1.9 0.7 copy-start.2
  3.1 11.6 %collective-permute-start = (f32[136,128]{1,0:T(8,128)S(1)}, f32[136,128]{1,0:T(8,128)S(1)}, u32[]{:S(2)}, u32[]{:S(2)}) collective-permute-start(f32[136,128]{1,0:T(8,128)S(1)} %get-tuple-element.32), channel_id=1, source_target_pairs={{0,64},{64,0},{1,65},{65,1},{2,66},{66,2},{3,67},{67,3},{4,68},{68... | collective-permute-start | bytes 208904 | tf_op jit(solution)/shard_map/ppermute | solution.py:46
  7.9 8.2 %collective-permute-start.1 = (f32[136,128]{1,0:T(8,128)S(1)}, f32[136,128]{1,0:T(8,128)S(1)}, u32[]{:S(2)}, u32[]{:S(2)}) collective-permute-start(f32[136,128]{1,0:T(8,128)S(1)} %get-tuple-element.33), channel_id=1, source_target_pairs={{0,65},{65,0},{1,66},{66,1},{2,67},{67,2},{3,68},{68,3},{4,69},{69... | collective-permute-start | bytes 208904 | tf_op jit(solution)/shard_map/ppermute | solution.py:46
  27.5 23.8 %copy-start.1 = (s32[8,6]{1,0:T(8,128)S(1)}, s32[8,6]{1,0:T(8,128)}, u32[]{:S(2)}) copy-start(s32[8,6]{1,0:T(8,128)} %refs_1_.3) | copy-start | bytes 580
  27.5 2.2 %collective-permute-start.2 = (f32[128,128]{1,0:T(8,128)S(1)}, f32[128,128]{1,0:T(8,128)S(1)}, u32[]{:S(2)}, u32[]{:S(2)}) collective-permute-start(f32[128,128]{1,0:T(8,128)S(1)} %get-tuple-element.36), channel_id=1, source_target_pairs={{0,64},{64,0},{1,65},{65,1},{2,66},{66,2},{3,67},{67,3},{4,68},{68... | collective-permute-start | bytes 196616 | tf_op jit(solution)/shard_map/ppermute | solution.py:46
  27.6 8.0 %collective-permute-start.3 = (f32[128,128]{1,0:T(8,128)S(1)}, f32[128,128]{1,0:T(8,128)S(1)}, u32[]{:S(2)}, u32[]{:S(2)}) collective-permute-start(f32[128,128]{1,0:T(8,128)S(1)} %get-tuple-element.37), channel_id=1, source_target_pairs={{0,65},{65,0},{1,66},{66,1},{2,67},{67,2},{3,68},{68,3},{4,69},{69... | collective-permute-start | bytes 196616 | tf_op jit(solution)/shard_map/ppermute | solution.py:46
  39.0 5.4 %collective-permute-start.4 = (f32[64,128]{1,0:T(8,128)S(1)}, f32[64,128]{1,0:T(8,128)S(1)}, u32[]{:S(2)}, u32[]{:S(2)}) collective-permute-start(f32[64,128]{1,0:T(8,128)S(1)} %get-tuple-element.39.refs_4_), channel_id=1, source_target_pairs={{0,16},{16,0},{64,80},{80,64},{1,17},{17,1},{65,81},{81,65},{2,18}... | collective-permute-start | bytes 98312 | tf_op jit(solution)/shard_map/ppermute | solution.py:46
  42.8 2.8 %collective-permute-start.5 = (f32[64,128]{1,0:T(8,128)S(1)}, f32[64,128]{1,0:T(8,128)S(1)}, u32[]{:S(2)}, u32[]{:S(2)}) collective-permute-start(f32[64,128]{1,0:T(8,128)S(1)} %get-tuple-element.40.refs_5_), channel_id=1, source_target_pairs={{16,32},{32,16},{80,96},{96,80},{17,33},{33,17},{81,97},{97,81},{1... | collective-permute-start | bytes 98312 | tf_op jit(solution)/shard_map/ppermute | solution.py:46
  42.8 2.8 %collective-permute-start.6 = (f32[64,128]{1,0:T(8,128)S(1)}, f32[64,128]{1,0:T(8,128)S(1)}, u32[]{:S(2)}, u32[]{:S(2)}) collective-permute-start(f32[64,128]{1,0:T(8,128)S(1)} %get-tuple-element.41.refs_6_), channel_id=1, source_target_pairs={{0,4},{4,0},{64,68},{68,64},{1,5},{5,1},{65,69},{69,65},{2,6},{6,2... | collective-permute-start | bytes 98312 | tf_op jit(solution)/shard_map/ppermute | solution.py:46
  42.8 4.9 %collective-permute-start.7 = (f32[64,128]{1,0:T(8,128)S(1)}, f32[64,128]{1,0:T(8,128)S(1)}, u32[]{:S(2)}, u32[]{:S(2)}) collective-permute-start(f32[64,128]{1,0:T(8,128)S(1)} %get-tuple-element.42.refs_7_), channel_id=1, source_target_pairs={{4,8},{8,4},{68,72},{72,68},{5,9},{9,5},{69,73},{73,69},{6,10},{10... | collective-permute-start | bytes 98312 | tf_op jit(solution)/shard_map/ppermute | solution.py:46
  42.8 4.9 %collective-permute-start.8 = (f32[64,128]{1,0:T(8,128)S(1)}, f32[64,128]{1,0:T(8,128)S(1)}, u32[]{:S(2)}, u32[]{:S(2)}) collective-permute-start(f32[64,128]{1,0:T(8,128)S(1)} %get-tuple-element.43.refs_8_), channel_id=1, source_target_pairs={{0,1},{1,0},{64,65},{65,64},{2,3},{3,2},{66,67},{67,66},{4,5},{5,4... | collective-permute-start | bytes 98312 | tf_op jit(solution)/shard_map/ppermute | solution.py:46
  44.4 7.0 %collective-permute-start.9 = (f32[64,128]{1,0:T(8,128)S(1)}, f32[64,128]{1,0:T(8,128)S(1)}, u32[]{:S(2)}, u32[]{:S(2)}) collective-permute-start(f32[64,128]{1,0:T(8,128)S(1)} %get-tuple-element.44.refs_9_), channel_id=1, source_target_pairs={{1,2},{2,1},{65,66},{66,65},{3,4},{4,3},{67,68},{68,67},{5,6},{6,5... | collective-permute-start | bytes 98312 | tf_op jit(solution)/shard_map/ppermute | solution.py:46
  55.3 7.0 %collective-permute-start.10 = (f32[128,128]{1,0:T(8,128)S(1)}, f32[128,128]{1,0:T(8,128)S(1)}, u32[]{:S(2)}, u32[]{:S(2)}) collective-permute-start(f32[128,128]{1,0:T(8,128)S(1)} %get-tuple-element.46), channel_id=1, source_target_pairs={{0,64},{64,0},{1,65},{65,1},{2,66},{66,2},{3,67},{67,3},{4,68},{68... | collective-permute-start | bytes 196616 | tf_op jit(solution)/shard_map/ppermute | solution.py:46
  56.9 7.9 %collective-permute-start.11 = (f32[128,128]{1,0:T(8,128)S(1)}, f32[128,128]{1,0:T(8,128)S(1)}, u32[]{:S(2)}, u32[]{:S(2)}) collective-permute-start(f32[128,128]{1,0:T(8,128)S(1)} %get-tuple-element.47), channel_id=1, source_target_pairs={{0,65},{65,0},{1,66},{66,1},{2,67},{67,2},{3,68},{68,3},{4,69},{69... | collective-permute-start | bytes 196616 | tf_op jit(solution)/shard_map/ppermute | solution.py:46
  75.8 1.5 %collective-permute-start.12 = (f32[128,128]{1,0:T(8,128)S(1)}, f32[128,128]{1,0:T(8,128)S(1)}, u32[]{:S(2)}, u32[]{:S(2)}) collective-permute-start(f32[128,128]{1,0:T(8,128)S(1)} %get-tuple-element.49), channel_id=1, source_target_pairs={{0,64},{64,0},{1,65},{65,1},{2,66},{66,2},{3,67},{67,3},{4,68},{68... | collective-permute-start | bytes 196616 | tf_op jit(solution)/shard_map/ppermute | solution.py:46
  75.9 8.0 %collective-permute-start.13 = (f32[128,128]{1,0:T(8,128)S(1)}, f32[128,128]{1,0:T(8,128)S(1)}, u32[]{:S(2)}, u32[]{:S(2)}) collective-permute-start(f32[128,128]{1,0:T(8,128)S(1)} %get-tuple-element.50), channel_id=1, source_target_pairs={{0,65},{65,0},{1,66},{66,1},{2,67},{67,2},{3,68},{68,3},{4,69},{69... | collective-permute-start | bytes 196616 | tf_op jit(solution)/shard_map/ppermute | solution.py:46
  87.3 2.8 %collective-permute-start.14 = (f32[64,128]{1,0:T(8,128)S(1)}, f32[64,128]{1,0:T(8,128)S(1)}, u32[]{:S(2)}, u32[]{:S(2)}) collective-permute-start(f32[64,128]{1,0:T(8,128)S(1)} %get-tuple-element.52.refs_4_), channel_id=1, source_target_pairs={{0,16},{16,0},{64,80},{80,64},{1,17},{17,1},{65,81},{81,65},{2,18}... | collective-permute-start | bytes 98312 | tf_op jit(solution)/shard_map/ppermute | solution.py:46
  87.8 5.7 %collective-permute-start.15 = (f32[64,128]{1,0:T(8,128)S(1)}, f32[64,128]{1,0:T(8,128)S(1)}, u32[]{:S(2)}, u32[]{:S(2)}) collective-permute-start(f32[64,128]{1,0:T(8,128)S(1)} %get-tuple-element.53.refs_5_), channel_id=1, source_target_pairs={{16,32},{32,16},{80,96},{96,80},{17,33},{33,17},{81,97},{97,81},{1... | collective-permute-start | bytes 98312 | tf_op jit(solution)/shard_map/ppermute | solution.py:46
  89.4 4.1 %collective-permute-start.16 = (f32[64,128]{1,0:T(8,128)S(1)}, f32[64,128]{1,0:T(8,128)S(1)}, u32[]{:S(2)}, u32[]{:S(2)}) collective-permute-start(f32[64,128]{1,0:T(8,128)S(1)} %get-tuple-element.54.refs_6_), channel_id=1, source_target_pairs={{0,4},{4,0},{64,68},{68,64},{1,5},{5,1},{65,69},{69,65},{2,6},{6,2... | collective-permute-start | bytes 98312 | tf_op jit(solution)/shard_map/ppermute | solution.py:46
  89.4 4.9 %collective-permute-start.17 = (f32[64,128]{1,0:T(8,128)S(1)}, f32[64,128]{1,0:T(8,128)S(1)}, u32[]{:S(2)}, u32[]{:S(2)}) collective-permute-start(f32[64,128]{1,0:T(8,128)S(1)} %get-tuple-element.55.refs_7_), channel_id=1, source_target_pairs={{4,8},{8,4},{68,72},{72,68},{5,9},{9,5},{69,73},{73,69},{6,10},{10... | collective-permute-start | bytes 98312 | tf_op jit(solution)/shard_map/ppermute | solution.py:46
  89.4 4.9 %collective-permute-start.18 = (f32[64,128]{1,0:T(8,128)S(1)}, f32[64,128]{1,0:T(8,128)S(1)}, u32[]{:S(2)}, u32[]{:S(2)}) collective-permute-start(f32[64,128]{1,0:T(8,128)S(1)} %get-tuple-element.56.refs_8_), channel_id=1, source_target_pairs={{0,1},{1,0},{64,65},{65,64},{2,3},{3,2},{66,67},{67,66},{4,5},{5,4... | collective-permute-start | bytes 98312 | tf_op jit(solution)/shard_map/ppermute | solution.py:46
  90.1 7.0 %collective-permute-start.19 = (f32[64,128]{1,0:T(8,128)S(1)}, f32[64,128]{1,0:T(8,128)S(1)}, u32[]{:S(2)}, u32[]{:S(2)}) collective-permute-start(f32[64,128]{1,0:T(8,128)S(1)} %get-tuple-element.57.refs_9_), channel_id=1, source_target_pairs={{1,2},{2,1},{65,66},{66,65},{3,4},{4,3},{67,68},{68,67},{5,6},{6,5... | collective-permute-start | bytes 98312 | tf_op jit(solution)/shard_map/ppermute | solution.py:46

commit v2 on v1

--- a/solution.py
+++ b/solution.py
@@ -1,3 +1,5 @@
+import functools
+
 import jax
 import jax.numpy as jnp
 from jax import lax
@@ -10,6 +12,7 @@
 FAM = 8
 WEIGHT = 0.8 / 6.0
 PAD_ROWS = 34 * 64
+GROUP = 4
 F32 = jnp.float32
 VMEM = pl.BlockSpec(memory_space=pltpu.VMEM)
 SMEM = pl.BlockSpec(memory_space=pltpu.SMEM)
@@ -76,31 +79,80 @@
     return [[rows(ref, base + (q * 2 + oz) * 8) for oz in range(2)] for q in range(4)]
 
 
-def around(a, below, above, ylo, z, hy=None, hz=None):
+def around(a, below, above, j, k, hy=None, hz=None):
     zero = jnp.zeros((8, 128), F32)
     if hy is None:
         hy = [[zero, zero], [zero, zero]]
     if hz is None:
         hz = [[zero, zero] for _ in range(4)]
-    y_first, y_last = ylo == 0, ylo == 7
-    z_first, z_last = z == 0, z == 15
-    down = [[roll(a[q][o], 16) for o in range(2)] for q in range(4)]
-    up = [[roll(a[q][o], 112) for o in range(2)] for q in range(4)]
+    y_low = [jnp.where(j == 0, hy[0][p], roll(a[3][p], 16)) for p in range(2)]
+    y_high = [jnp.where(j == 7, hy[1][p], roll(a[0][p], 112)) for p in range(2)]
     total = []
-    for q in range(4):
+    for r in range(4):
+        z_low = jnp.where(k == 0, hz[r][0], roll(a[r][1], 1))
+        z_high = jnp.where(k == 15, hz[r][1], roll(a[r][0], 127))
         line = []
-        for o in range(2):
-            low_y = jnp.where(y_first, down[q - 1][o] if q else hy[0][o], down[q][o])
-            high_y = jnp.where(y_last, up[q + 1][o] if q < 3 else hy[1][o], up[q][o])
-            if o == 0:
-                low_z = jnp.where(z_first, hz[q][0], roll(a[q][0], 1))
-                high_z = roll(jnp.where(z_first, down[q][1], a[q][0]), 127)
-            else:
-                low_z = roll(jnp.where(z_last, up[q][0], a[q][1]), 1)
-                high_z = jnp.where(z_last, hz[q][1], roll(a[q][1], 127))
-            line.append((low_y + high_y) + (low_z + high_z) + (below[q][o] + above[q][o]))
+        for p in range(2):
+            y_sum = (a[r - 1][p] if r else y_low[p]) + (a[r + 1][p] if r < 3 else y_high[p])
+            z_sum = a[r][1 - p] + (z_high if p else z_low)
+            line.append((y_sum + z_sum) + (below[r][p] + above[r][p]))
         total.append(line)
     return total
+
+
+def exchange(a, b, bit, shift):
+    return jnp.where(bit, roll(b, shift), a), jnp.where(bit, b, roll(a, 128 - shift))
+
+
+def spread_index(j, k):
+    return ((j & 1) * 4 + (j >> 1)) * 16 + 2 * (k & 7) + (k >> 3)
+
+
+def to_working(v, j, k):
+    s = [exchange(v[q][0], v[q][1], (k & 1) == 1, 1) for q in range(4)]
+    index = spread_index(j, k)
+    result = [[None, None] for _ in range(4)]
+    for p in range(2):
+        t = [exchange(s[2 * h][p], s[2 * h + 1][p], (j & 1) == 1, 16) for h in range(2)]
+        for low in range(2):
+            pair = exchange(t[0][low], t[1][low], (j & 2) == 2, 32)
+            for high in range(2):
+                result[low + 2 * high][p] = jnp.take_along_axis(pair[high], index, axis=1)
+    return result
+
+
+def to_given(a, j, k):
+    index = (2 * (j & 3) + (j >> 2)) * 16 + (k >> 1) + 8 * (k & 1)
+    s = [[None, None] for _ in range(4)]
+    for p in range(2):
+        t = [[None, None], [None, None]]
+        for low in range(2):
+            pair = [jnp.take_along_axis(a[low + 2 * high][p], index, axis=1) for high in range(2)]
+            t[0][low], t[1][low] = exchange(pair[0], pair[1], (j & 2) == 2, 32)
+        for h in range(2):
+            s[2 * h][p], s[2 * h + 1][p] = exchange(t[h][0], t[h][1], (j & 1) == 1, 16)
+    return [exchange(s[q][0], s[q][1], (k & 1) == 1, 1) for q in range(4)]
+
+
+def given_rows(x, q, oz):
+    octant = (x >> 4) * 4 + (q // 2) * 2 + oz
+    return pl.ds(((x & 15) * 2 + q % 2) * 8 + octant, 8, stride=256)
+
+
+def given_plane(ref, x):
+    return [[ref[given_rows(x, q, oz), :] for oz in range(2)] for q in range(4)]
+
+
+def put_given(ref, x, v):
+    for q in range(4):
+        for oz in range(2):
+            ref[given_rows(x, q, oz), :] = v[q][oz]
+
+
+def put_plane(ref, x, a):
+    for r in range(4):
+        for p in range(2):
+            put(ref, (x + 1) * 64 + (r * 2 + p) * 8, a[r][p])
 
 
 def clear_pads(ref):
@@ -109,41 +161,54 @@
 
 
 def smooth(rhs, mid, emit):
-    ylo, z = lane_parts()
+    j, k = lane_parts()
     clear_pads(rhs)
     clear_pads(mid)
 
-    def first(x, _):
-        a = plane(rhs, x)
-        m = around(a, plane(rhs, x - 1), plane(rhs, x + 1), ylo, z)
-        for q in range(4):
-            for o in range(2):
-                put(mid, (x + 1) * 64 + (q * 2 + o) * 8, 1.2 * a[q][o] + WEIGHT * m[q][o])
-        return 0
-
-    def second(x, _):
-        a = plane(mid, x)
-        m = around(a, plane(mid, x - 1), plane(mid, x + 1), ylo, z)
-        for q in range(4):
-            for o in range(2):
-                at = (x + 1) * 64 + (q * 2 + o) * 8
-                emit(at, WEIGHT * (rows(rhs, at) + 0.2 * a[q][o] + WEIGHT * m[q][o]))
-        return 0
-
-    lax.fori_loop(0, 32, first, 0)
-    lax.fori_loop(0, 32, second, 0)
-
-
-def restrict_pair(p, i, ylo, z, down):
-    z_even, y_even = (z & 1) == 0, (ylo & 1) == 0
-    index = (2 * (ylo & 3) + (ylo >> 2)) * 16 + 2 * (z & 7) + (z >> 3)
-    for oy in range(2):
-        u = []
-        for a in range(2):
-            lo, hi = p[2 * oy + a]
-            u.append(jnp.where(z_even, lo + roll(lo, 127), hi + roll(hi, 1)))
-        m = jnp.where(y_even, u[0] + roll(u[0], 112), u[1] + roll(u[1], 16))
-        put(down, (oy * 16 + i) * 8, 0.5 * jnp.take_along_axis(m, index, axis=1))
+    def sweep(src, write):
+        def body(i, _):
+            x0 = i * GROUP
+            p = [plane(src, x0 + m - 1) for m in range(GROUP + 2)]
+            result = [around(p[m + 1], p[m], p[m + 2], j, k) for m in range(GROUP)]
+            for m in range(GROUP):
+                for r in range(4):
+                    for c in range(2):
+                        write((x0 + m + 1) * 64 + (r * 2 + c) * 8, p[m + 1][r][c], result[m][r][c])
+            return 0
+
+        lax.fori_loop(0, 32 // GROUP, body, 0)
+
+    def first(at, a, m):
+        put(mid, at, 1.2 * a + WEIGHT * m)
+
+    def second(at, a, m):
+        emit(at, WEIGHT * (rows(rhs, at) + 0.2 * a + WEIGHT * m))
+
+    sweep(rhs, first)
+    sweep(mid, second)
+
+
+def put_down(down, i, pair):
+    for r in range(2):
+        put(down, (r * 16 + i) * 8, pair[r])
+
+
+def restrict_pair(a, b):
+    c = [[a[r][p] + b[r][p] for p in range(2)] for r in range(4)]
+    return [0.5 * ((c[2 * r][0] + c[2 * r][1]) + (c[2 * r + 1][0] + c[2 * r + 1][1])) for r in range(2)]
+
+
+def restrict_given(a, b, j, k):
+    z_even, y_even, high = (k & 1) == 0, (j & 1) == 0, (j & 2) == 2
+    u = []
+    for q in range(4):
+        lo, hi = a[q][0] + b[q][0], a[q][1] + b[q][1]
+        u.append(jnp.where(z_even, lo + roll(lo, 127), hi + roll(hi, 1)))
+    m = []
+    for h in range(2):
+        m.append(jnp.where(y_even, u[2 * h] + roll(u[2 * h], 112), u[2 * h + 1] + roll(u[2 * h + 1], 16)))
+    index = spread_index(j, k)
+    return [0.5 * jnp.take_along_axis(n, index, axis=1) for n in exchange(m[0], m[1], high, 32)]
 
 
 def parent_slots(parent, blk):
@@ -174,76 +239,83 @@
                     buf[pl.ds(128 + slot, 1), :] = jnp.full((1, 128), block.astype(F32), F32)
 
 
-def block_start(block):
+def block_place(block, s, half):
     f, o = block >> 3, block & 7
-    return ((o >> 2) * 16 + 1) * 64 + (((o >> 1) & 1) * 4 + (o & 1)) * 8 + f
+    start = ((o >> 2) * 16 + 8 * half + 1) * 64 + f
+    at = [[pl.ds(start + ((2 * t + s) * 2 + p) * 8, 8, stride=64) for p in range(2)] for t in range(2)]
+    return at, (o >> 1) & 1, o & 1
 
 
 def add_incoming(rhs, tags, arrived):
-    for j in range(8):
-        buf, slot, tag = arrived[j // 4], j % 4, tags[j]
+    j, k = lane_parts()
+    index = [[(2 * (j & 3) + t) * 16 + 2 * (k & 7) + p for p in range(2)] for t in range(2)]
+    for n in range(8):
+        buf, slot, tag = arrived[n // 4], n % 4, tags[n]
 
         @pl.when(tag >= 0)
         def _(buf=buf, slot=slot, tag=tag):
-            start = block_start(tag)
-            for yh in range(2):
-                at = pl.ds(start + yh * 16, 16, stride=64)
-                rhs[at, :] = rhs[at, :] + buf[slot * 32 + yh * 16 : slot * 32 + yh * 16 + 16, :]
+            for s in range(2):
+                for half in range(2):
+                    at, oy, oz = block_place(tag, s, half)
+                    here = ((j >> 2) == oy) & ((k >> 3) == oz)
+                    value = rows(buf, slot * 32 + s * 16 + half * 8)
+                    for t in range(2):
+                        for p in range(2):
+                            spread = jnp.take_along_axis(value, index[t][p], axis=1)
+                            rhs[at[t][p], :] = rhs[at[t][p], :] + jnp.where(here, spread, 0.0)
 
 
 def answer(correction, tags, out):
-    for j in range(8):
-        buf, slot, tag = out[j // 4], j % 4, tags[j]
+    j, k = lane_parts()
+    y_odd, z_odd = (j & 1) == 1, (k & 1) == 1
+    for n in range(8):
+        buf, slot, tag = out[n // 4], n % 4, tags[n]
 
         @pl.when(tag >= 0)
         def _(buf=buf, slot=slot, tag=tag):
-            start = block_start(tag)
-            for yh in range(2):
-                buf[slot * 32 + yh * 16 : slot * 32 + yh * 16 + 16, :] = correction[
-                    pl.ds(start + yh * 16, 16, stride=64), :
-                ]
+            for s in range(2):
+                for half in range(2):
+                    at, oy, oz = block_place(tag, s, half)
+                    index = (4 * oy + (j >> 1)) * 16 + 8 * oz + (k >> 1)
+                    v = [
+                        [jnp.take_along_axis(correction[at[t][p], :], index, axis=1) for p in range(2)]
+                        for t in range(2)
+                    ]
+                    v = [jnp.where(z_odd, v[t][1], v[t][0]) for t in range(2)]
+                    put(buf, slot * 32 + s * 16 + half * 8, jnp.where(y_odd, v[1], v[0]))
 
 
 def first_down_kernel(parent, source, own, nxt, down):
     sec, blk = position()
-    ylo, z = lane_parts()
+    j, k = lane_parts()
 
     @pl.when(sec == 0)
     def _():
-        def pair(i, _):
-            x = (2 * i) & 15
-            ox4 = (i >> 3) * 4
-            p = []
-            for q in range(4):
-                line = []
-                for oz in range(2):
-                    o = ox4 + (q // 2) * 2 + oz
-                    c = x * 2 + q % 2
-                    line.append(
-                        source[pl.ds(c * 8 + o, 8, stride=256), :]
-                        + source[pl.ds((c + 2) * 8 + o, 8, stride=256), :]
-                    )
-                p.append(line)
-            restrict_pair(p, i, ylo, z, down)
+        def pair(i):
+            return restrict_given(given_plane(source, 2 * i), given_plane(source, 2 * i + 1), j, k)
+
+        def pairs(n, _):
+            done = [pair(4 * n + m) for m in range(4)]
+            for m in range(4):
+                put_down(down, 4 * n + m, done[m])
             return 0
 
-        lax.fori_loop(0, 16, pair, 0)
+        lax.fori_loop(0, 4, pairs, 0)
         send_down(down, parent, blk, own, nxt, True)
 
 
 def load_kernel(source, src, sol, mid):
     sec, _ = position()
 
-    def copy(x, _):
-        for ox in range(2):
-            for q in range(4):
-                for oz in range(2):
-                    o = ox * 4 + (q // 2) * 2 + oz
-                    c = x * 2 + q % 2
-                    put(src, (ox * 16 + x + 1) * 64 + (q * 2 + oz) * 8, source[pl.ds(c * 8 + o, 8, stride=256), :])
+    j, k = lane_parts()
+
+    def convert(i, _):
+        planes = [to_working(given_plane(source, GROUP * i + m), j, k) for m in range(GROUP)]
+        for m in range(GROUP):
+            put_plane(src, GROUP * i + m, planes[m])
         return 0
 
-    lax.fori_loop(0, 16, copy, 0)
+    lax.fori_loop(0, 32 // GROUP, convert, 0)
 
     @pl.when(sec == 0)
     def _():
@@ -308,15 +380,32 @@
 def lift_kernel(parent, sol, in_own, in_next, out_sol, *refs):
     out, (lift, face) = refs[:6], refs[6:]
     sec, blk = position()
-    ylo, z = lane_parts()
-
-    @pl.when(sec == 1)
-    def _():
-        def copy(i, _):
-            put(out_sol, i * 64, rows(sol, i * 64, 64))
-            return 0
-
-        lax.fori_loop(1, 33, copy, 0)
+    j, k = lane_parts()
+
+    def pack(make, g, _):
+        planes = make(g)
+        zero = jnp.zeros((8, 128), F32)
+        y_low, y_high, z_low, z_high = [zero] * 2, [zero] * 2, [zero] * 4, [zero] * 4
+        for m, a in enumerate(planes):
+            y_mask, z_mask = j == m, k == m
+            for p in range(2):
+                y_low[p] = jnp.where(y_mask, roll(a[0][p], 16 * m), y_low[p])
+                y_high[p] = jnp.where(y_mask, roll(a[3][p], (16 * m + 16) % 128), y_high[p])
+            for r in range(4):
+                z_low[r] = jnp.where(z_mask, roll(a[r][0], m), z_low[r])
+                z_high[r] = jnp.where(z_mask, roll(a[r][1], (m + 113) % 128), z_high[r])
+        for m, a in enumerate(planes):
+            put_plane(out_sol, 8 * g + m, a)
+        for o in range(2):
+            put(face, 128 + (o * 4 + g) * 8, y_low[o])
+            put(face, 192 + (o * 4 + g) * 8, y_high[o])
+        half = g & 1
+        here = (k >> 3) == half
+        for q in range(4):
+            at = 256 + (q * 2 + (g >> 1)) * 8
+            put(face, at, jnp.where(here, roll(z_low[q], 8 * half), rows(face, at)))
+            put(face, at + 64, jnp.where(here, roll(z_high[q], 8 * half), rows(face, at + 64)))
+        return 0
 
     @pl.when(sec == 0)
     def _():
@@ -335,43 +424,24 @@
             def _(at=at):
                 lift[at, :] = jnp.zeros((32, 128), F32)
 
-        index = [[(4 * a + (ylo >> 1)) * 16 + 8 * b + (z >> 1) for b in range(2)] for a in range(2)]
-
-        def add(i, _):
-            for oy in range(2):
-                value = rows(lift, (oy * 16 + i) * 8)
-                for a in range(2):
-                    for b in range(2):
-                        wide = jnp.take_along_axis(value, index[a][b], axis=1)
-                        for x in range(2):
-                            at = (2 * i + x + 1) * 64 + ((2 * oy + a) * 2 + b) * 8
-                            put(out_sol, at, rows(sol, at) + wide)
-            return 0
-
-        lax.fori_loop(0, 16, add, 0)
+        def lifted(g):
+            planes = [plane(sol, 8 * g + m) for m in range(8)]
+            for m in range(4):
+                for s in range(2):
+                    value = rows(lift, (s * 16 + 4 * g + m) * 8)
+                    for x in (2 * m, 2 * m + 1):
+                        for r in (2 * s, 2 * s + 1):
+                            planes[x][r] = [planes[x][r][p] + value for p in range(2)]
+            return planes
+
+        lax.fori_loop(0, 4, functools.partial(pack, lifted), 0)
+
+    @pl.when(sec == 1)
+    def _():
+        lax.fori_loop(0, 4, functools.partial(pack, lambda g: [plane(sol, 8 * g + m) for m in range(8)]), 0)
 
     put(face, 0, rows(out_sol, 64, 64))
     put(face, 64, rows(out_sol, 32 * 64, 64))
-
-    def pack(x, _):
-        base = (x + 1) * 64
-        y_at, z_at = x & 7, x & 15
-        y_mask, z_mask = ylo == y_at, z == z_at
-        for oz in range(2):
-            at = (oz * 4 + (x >> 3)) * 8
-            low = roll(rows(out_sol, base + oz * 8), 16 * y_at)
-            high = roll(rows(out_sol, base + (6 + oz) * 8), (16 * y_at + 16) & 127)
-            put(face, 128 + at, jnp.where(y_mask, low, rows(face, 128 + at)))
-            put(face, 192 + at, jnp.where(y_mask, high, rows(face, 192 + at)))
-        for q in range(4):
-            at = (q * 2 + (x >> 4)) * 8
-            low = roll(rows(out_sol, base + q * 16), z_at)
-            high = roll(rows(out_sol, base + q * 16 + 8), (z_at + 113) & 127)
-            put(face, 256 + at, jnp.where(z_mask, low, rows(face, 256 + at)))
-            put(face, 320 + at, jnp.where(z_mask, high, rows(face, 320 + at)))
-        return 0
-
-    lax.fori_loop(0, 32, pack, 0)
     for axis, parity in enumerate(parities(blk)):
         for color in range(2):
             d = 2 * axis + (parity == color).astype(jnp.int32)
@@ -385,7 +455,7 @@
     else:
         res, own, nxt, halo, table, down = refs[12:]
     sec, blk = position()
-    ylo, z = lane_parts()
+    j, k = lane_parts()
 
     for axis, parity in enumerate(parities(blk)):
         for color in range(2):
@@ -408,8 +478,7 @@
     def side(base):
         return [[rows(halo, base + (q * 2 + o) * 8) for o in range(2)] for q in range(4)]
 
-    def residue(x, below, above):
-        a = plane(sol, x)
+    def residue(x, a, below, above):
         y_at, z_at = x & 7, x & 15
         y_rows = [128 + (o * 4 + (x >> 3)) * 8 for o in range(2)]
         hy = [
@@ -420,40 +489,32 @@
         for q in range(4):
             at = 256 + (q * 2 + (x >> 4)) * 8
             hz.append([roll(rows(halo, at), (128 - z_at) & 127), roll(rows(halo, at + 64), 15 - z_at)])
-        m = around(a, below, above, ylo, z, hy, hz)
+        m = around(a, below, above, j, k, hy, hz)
         s = plane(src, x)
         return [[s[q][o] - 6.0 * a[q][o] + m[q][o] for o in range(2)] for q in range(4)]
 
     def store(x, r):
         if last:
-            for q in range(4):
-                for o in range(2):
-                    octant = (x >> 4) * 4 + (q // 2) * 2 + o
-                    c = (x & 15) * 2 + q % 2
-                    res[pl.ds(c * 8 + octant, 8, stride=256), :] = r[q][o]
+            put_given(res, x, to_given(r, j, k))
         else:
-            for q in range(4):
-                for o in range(2):
-                    put(res, (x + 1) * 64 + (q * 2 + o) * 8, r[q][o])
-
-    def pair(i, _, low=None, high=None):
-        x = 2 * i
-        r0 = residue(x, plane(sol, x - 1) if low is None else low, plane(sol, x + 1))
-        r1 = residue(x + 1, plane(sol, x), plane(sol, x + 2) if high is None else high)
-        store(x, r0)
-        store(x + 1, r1)
+            put_plane(res, x, r)
+
+    def group(i, _, low=None, high=None):
+        x = GROUP * i
+        p = [plane(sol, x + m) for m in range(GROUP)]
+        p = [plane(sol, x - 1) if low is None else low] + p + [plane(sol, x + GROUP) if high is None else high]
+        r = [residue(x + m, p[m + 1], p[m], p[m + 2]) for m in range(GROUP)]
+        for m in range(GROUP):
+            store(x + m, r[m])
         if not last:
-
-            @pl.when(sec == 0)
-            def _():
-                p = [[r0[q][o] + r1[q][o] for o in range(2)] for q in range(4)]
-                restrict_pair(p, i, ylo, z, down)
-
+            for m in range(GROUP // 2):
+                put_down(down, (GROUP // 2) * i + m, restrict_pair(r[2 * m], r[2 * m + 1]))
         return 0
 
-    pair(0, 0, low=side(0))
-    lax.fori_loop(1, 15, pair, 0)
-    pair(15, 0, high=side(64))
+    count = 32 // GROUP
+    group(0, 0, low=side(0))
+    lax.fori_loop(1, count - 1, group, 0)
+    group(count - 1, 0, high=side(64))
     if not last:
 
         @pl.when(sec == 0)
@@ -487,16 +548,15 @@
 
 
 def unload_kernel(sol, out):
-    def copy(x, _):
-        for ox in range(2):
-            for q in range(4):
-                for oz in range(2):
-                    o = ox * 4 + (q // 2) * 2 + oz
-                    c = x * 2 + q % 2
-                    out[pl.ds(c * 8 + o, 8, stride=256), :] = rows(sol, (ox * 16 + x + 1) * 64 + (q * 2 + oz) * 8)
+    j, k = lane_parts()
+
+    def convert(i, _):
+        planes = [to_given(plane(sol, GROUP * i + m), j, k) for m in range(GROUP)]
+        for m in range(GROUP):
+            put_given(out, GROUP * i + m, planes[m])
         return 0
 
-    lax.fori_loop(0, 16, copy, 0)
+    lax.fori_loop(0, 32 // GROUP, convert, 0)
 
 
 def shape(n, dtype=F32):

time: 102 us -> 81.5 us (0.80)
  Pallas kernels: 41.1 us -> 27.9 us
  starting transfers between devices: 29.4 us -> 16.6 us
  waiting for transfers between devices: 28.9 us -> 34.2 us
    ppermute x20, starting transfers between devices: 29.4 us -> 16.6 us  [swap(): return lax.ppermute(x, AX, pairs)]
    pallas_call x1, Pallas kernels: 11 us -> 4.7 us  [local(): call(lambda *refs: coarse_kernel(False, *refs), 'coarse_1', [SMEM] + [VME...]
    pallas_call x1, Pallas kernels: 11.5 us -> 5.23 us  [local(): call(lambda *refs: coarse_kernel(True, *refs), 'coarse_0', [VMEM] * 4, (p...]
    ppermute x20, waiting for transfers between devices: 28.9 us -> 34.2 us  [swap(): return lax.ppermute(x, AX, pairs)]
    pallas_call x2, Pallas kernels: 6.74 us -> 2.88 us  [local(): call(lift_kernel, f'lift_{iteration}', [SMEM, VMEM, VMEM, VMEM], (pad,) +...]
    pallas_call x1, Pallas kernels: 1.6 us -> 3.78 us  [local(): solution, = call(unload_kernel, 'unload', [VMEM], (shape(2048),))(sol)]
    pallas_call x1, Pallas kernels: 0.68 us -> 2.78 us  [local(): src, sol = call(load_kernel, 'load', [VMEM], (pad, pad), [pads])(tiles)]
    pallas_call x1, Pallas kernels: 3.91 us -> 2.27 us  [local(): call(lambda *refs: residual_kernel(False, *refs), 'residual_0', ins, (pad...]
  transfers between devices with their start and end apart: 20 -> 20, of which waited for: 11 -> 11; matrix products, arithmetic and copies ran while one was open for 0% -> 0% of each run, Pallas kernels for 2% -> 8%
where the time goes in v2:
time: 81.5 us; the launch traced here: 81.4 us
  waiting for transfers between devices  34.2 us (42%)
  Pallas kernels  27.9 us (34%)
  starting transfers between devices  16.6 us (20%)
  local copies, waits for them, and re-layouts  1.88 us (2%)
    ppermute x20, waiting for transfers between devices, swap(): return lax.ppermute(x, AX, pairs)  34.2 us
    ppermute x20, starting transfers between devices, swap(): return lax.ppermute(x, AX, pairs)  16.6 us
    pallas_call x1, Pallas kernels, local(): call(lambda *refs: residual_kernel(True, *refs), 'residual_1', ins, (shap...  5.51 us
    pallas_call x1, Pallas kernels, local(): call(lambda *refs: coarse_kernel(True, *refs), 'coarse_0', [VMEM] * 4, (p...  5.23 us
    pallas_call x1, Pallas kernels, local(): call(lambda *refs: coarse_kernel(False, *refs), 'coarse_1', [SMEM] + [VME...  4.7 us
    pallas_call x1, Pallas kernels, local(): solution, = call(unload_kernel, 'unload', [VMEM], (shape(2048),))(sol)  3.78 us
    pallas_call x2, Pallas kernels, local(): call(lift_kernel, f'lift_{iteration}', [SMEM, VMEM, VMEM, VMEM], (pad,) +...  2.88 us
    pallas_call x1, Pallas kernels, local(): src, sol = call(load_kernel, 'load', [VMEM], (pad, pad), [pads])(tiles)  2.78 us
  transfers between devices with their start and end apart: 20, of which 11 were waited for; matrix products, arithmetic and copies ran while one was open for 0% of the time, Pallas kernels for 8%

profile of v2, /device:TPU:3, one launch (start us, length us, event | category | flops | bytes accessed | tf_op | source)
XLA Modules:
  0.0 81.4 jit_solution(16806593108062208457)
XLA Ops:
  0.6 1.2 %copy-done = f32[64,4096]{1,0:T(8,128)S(1)} copy-done((f32[64,4096]{1,0:T(8,128)S(1)}, f32[64,4096]{1,0:T(8,128)}, u32[]{:S(2)}) %copy-start) | copy-done | bytes 1048600
  1.9 0.7 copy-done.2
  2.5 0.6 first_down.1
  3.1 2.5 %collective-permute-start = (f32[136,128]{1,0:T(8,128)S(1)}, f32[136,128]{1,0:T(8,128)S(1)}, u32[]{:S(2)}, u32[]{:S(2)}) collective-permute-start(f32[136,128]{1,0:T(8,128)S(1)} %get-tuple-element.32), channel_id=1, source_target_pairs={{0,64},{64,0},{1,65},{65,1},{2,66},{66,2},{3,67},{67,3},{4,68},{68... | collective-permute-start | bytes 208904 | tf_op jit(solution)/shard_map/ppermute | solution.py:49
  5.6 6.2 %collective-permute-start.1 = (f32[136,128]{1,0:T(8,128)S(1)}, f32[136,128]{1,0:T(8,128)S(1)}, u32[]{:S(2)}, u32[]{:S(2)}) collective-permute-start(f32[136,128]{1,0:T(8,128)S(1)} %get-tuple-element.33), channel_id=1, source_target_pairs={{0,65},{65,0},{1,66},{66,1},{2,67},{67,2},{3,68},{68,3},{4,69},{69... | collective-permute-start | bytes 208904 | tf_op jit(solution)/shard_map/ppermute | solution.py:49
  11.8 2.8 %load.1 = (f32[2176,128]{1,0:T(8,128)S(1)}, f32[2176,128]{1,0:T(8,128)S(1)}) custom-call(f32[2048,128]{1,0:T(8,128)S(1)} %bitcast.16), custom_call_target="tpu_custom_call" | custom-call | tf_op jit(solution)/shard_map/load/pallas_call | solution.py:593
  14.6 0.0 collective-permute-done.refs_2_
  14.6 0.0 collective-permute-done.1.refs_3_
  14.6 5.2 %coarse_0.1 = (f32[2176,128]{1,0:T(8,128)S(1)}, f32[128,128]{1,0:T(8,128)S(1)}, f32[128,128]{1,0:T(8,128)S(1)}, s32[8]{0:T(128)S(1)}) custom-call(f32[2176,128]{1,0:T(8,128)S(1)} %get-tuple-element.30.refs_0_.refs_2_, f32[2176,128]{1,0:T(8,128)S(1)} %get-tuple-element.31.refs_1_, f32[136,128]{1,0:T(8,128)S(1)} %collective-permute-done.refs_2_, ...), custom_call_target="tpu_custom_call" | custom-call | tf_op jit(solution)/shard_map/coarse_0/pallas_call | solution.py:598
  19.8 0.0 copy-start.1
  19.8 0.1 collective-permute-start.2
  19.9 1.3 %collective-permute-start.3 = (f32[128,128]{1,0:T(8,128)S(1)}, f32[128,128]{1,0:T(8,128)S(1)}, u32[]{:S(2)}, u32[]{:S(2)}) collective-permute-start(f32[128,128]{1,0:T(8,128)S(1)} %get-tuple-element.37), channel_id=1, source_target_pairs={{0,65},{65,0},{1,66},{66,1},{2,67},{67,2},{3,68},{68,3},{4,69},{69... | collective-permute-start | bytes 196616 | tf_op jit(solution)/shard_map/ppermute | solution.py:49
  21.2 6.7 %collective-permute-done.3.in_next = f32[128,128]{1,0:T(8,128)S(1)} collective-permute-done((f32[128,128]{1,0:T(8,128)S(1)}, f32[128,128]{1,0:T(8,128)S(1)}, u32[]{:S(2)}, u32[]{:S(2)}) %collective-permute-start.3) | collective-permute-done | bytes 65568 | tf_op jit(solution)/shard_map/ppermute | solution.py:49
  27.9 1.4 %lift_0.1 = (f32[2176,128]{1,0:T(8,128)S(1)}, f32[64,128]{1,0:T(8,128)S(1)}, f32[64,128]{1,0:T(8,128)S(1)}, f32[64,128]{1,0:T(8,128)S(1)}, f32[64,128]{1,0:T(8,1...) custom-call(s32[8]{0:T(128)S(1)} %copy-done.2, f32[2176,128]{1,0:T(8,128)S(1)} %get-tuple-element.35.sol, ...), custom_call_target="tpu_custom_call" | custom-call | tf_op jit(solution)/shard_map/lift_0/pallas_call | solution.py:615
  29.4 3.8 %collective-permute-start.4 = (f32[64,128]{1,0:T(8,128)S(1)}, f32[64,128]{1,0:T(8,128)S(1)}, u32[]{:S(2)}, u32[]{:S(2)}) collective-permute-start(f32[64,128]{1,0:T(8,128)S(1)} %get-tuple-element.39.refs_4_), channel_id=1, source_target_pairs={{0,16},{16,0},{64,80},{80,64},{1,17},{17,1},{65,81},{81,65},{2,18}... | collective-permute-start | bytes 98312 | tf_op jit(solution)/shard_map/ppermute | solution.py:49
  33.1 0.0 collective-permute-start.5
  33.1 0.0 collective-permute-start.6
  33.1 0.0 collective-permute-start.7
  33.1 0.1 collective-permute-start.8
  33.2 1.2 %collective-permute-done.4.refs_10_ = f32[64,128]{1,0:T(8,128)S(1)} collective-permute-done((f32[64,128]{1,0:T(8,128)S(1)}, f32[64,128]{1,0:T(8,128)S(1)}, u32[]{:S(2)}, u32[]{:S(2)}) %collective-permute-start.4) | collective-permute-done | bytes 32800 | tf_op jit(solution)/shard_map/ppermute | solution.py:49
  34.4 0.0 collective-permute-start.9
  34.4 1.7 %collective-permute-done.5.refs_11_ = f32[64,128]{1,0:T(8,128)S(1)} collective-permute-done((f32[64,128]{1,0:T(8,128)S(1)}, f32[64,128]{1,0:T(8,128)S(1)}, u32[]{:S(2)}, u32[]{:S(2)}) %collective-permute-start.5) | collective-permute-done | bytes 32800 | tf_op jit(solution)/shard_map/ppermute | solution.py:49
  36.2 0.3 collective-permute-done.6.refs_12_
  36.4 1.8 %collective-permute-done.7.refs_13_ = f32[64,128]{1,0:T(8,128)S(1)} collective-permute-done((f32[64,128]{1,0:T(8,128)S(1)}, f32[64,128]{1,0:T(8,128)S(1)}, u32[]{:S(2)}, u32[]{:S(2)}) %collective-permute-start.7) | collective-permute-done | bytes 32800 | tf_op jit(solution)/shard_map/ppermute | solution.py:49
  38.2 0.0 collective-permute-done.8.refs_14_
  38.2 3.2 %collective-permute-done.9.refs_15_ = f32[64,128]{1,0:T(8,128)S(1)} collective-permute-done((f32[64,128]{1,0:T(8,128)S(1)}, f32[64,128]{1,0:T(8,128)S(1)}, u32[]{:S(2)}, u32[]{:S(2)}) %collective-permute-start.9) | collective-permute-done | bytes 32800 | tf_op jit(solution)/shard_map/ppermute | solution.py:49
  41.4 2.3 %residual_0.1 = (f32[2176,128]{1,0:T(8,128)S(1)}, f32[128,128]{1,0:T(8,128)S(1)}, f32[128,128]{1,0:T(8,128)S(1)}) custom-call(s32[8]{0:T(128)S(1)} %copy-done.2, s32[8,6]{1,0:T(8,128)S(1)} %copy-done.1, f32[2176,128]{1,0:T(8,128)S(1)} %get-tuple-element.30.refs_0_.refs_2_, f32[2176,128]{1,0:T(8,128)S(1)} %get-tuple-element.38.refs_3_.sol, ...), custom_call_target="tpu_custom_call" | custom-call | tf_op jit(solution)/shard_map/residual_0/pallas_call | solution.py:626
  43.7 0.1 collective-permute-start.10
  43.8 1.7 %collective-permute-start.11 = (f32[128,128]{1,0:T(8,128)S(1)}, f32[128,128]{1,0:T(8,128)S(1)}, u32[]{:S(2)}, u32[]{:S(2)}) collective-permute-start(f32[128,128]{1,0:T(8,128)S(1)} %get-tuple-element.47), channel_id=1, source_target_pairs={{0,65},{65,0},{1,66},{66,1},{2,67},{67,2},{3,68},{68,3},{4,69},{69... | collective-permute-start | bytes 196616 | tf_op jit(solution)/shard_map/ppermute | solution.py:49
  45.5 0.2 fine.1.refs_2_
  45.7 6.1 %collective-permute-done.11.refs_4_ = f32[128,128]{1,0:T(8,128)S(1)} collective-permute-done((f32[128,128]{1,0:T(8,128)S(1)}, f32[128,128]{1,0:T(8,128)S(1)}, u32[]{:S(2)}, u32[]{:S(2)}) %collective-permute-start.11) | collective-permute-done | bytes 65568 | tf_op jit(solution)/shard_map/ppermute | solution.py:49
  51.8 4.7 %coarse_1.1 = (f32[2176,128]{1,0:T(8,128)S(1)}, f32[128,128]{1,0:T(8,128)S(1)}, f32[128,128]{1,0:T(8,128)S(1)}) custom-call(s32[8]{0:T(128)S(1)} %get-tuple-element.34.refs_0_, f32[2176,128]{1,0:T(8,128)S(1)} %get-tuple-element.45.res.refs_1_, f32[2176,128]{1,0:T(8,128)S(1)} %fine.1.refs_2_, f32[128,128]{1,0:T(8,128)S(1)} %collective-permute-done.10.refs_3_, ...), custom_call_target="tpu_custom_call" | custom-call | tf_op jit(solution)/shard_map/coarse_1/pallas_call | solution.py:607
  56.5 0.1 collective-permute-start.12
  56.6 0.1 collective-permute-start.13
  56.7 1.1 %collective-permute-done.12.in_own = f32[128,128]{1,0:T(8,128)S(1)} collective-permute-done((f32[128,128]{1,0:T(8,128)S(1)}, f32[128,128]{1,0:T(8,128)S(1)}, u32[]{:S(2)}, u32[]{:S(2)}) %collective-permute-start.12) | collective-permute-done | bytes 65568 | tf_op jit(solution)/shard_map/ppermute | solution.py:49
  57.8 6.7 %collective-permute-done.13.in_next = f32[128,128]{1,0:T(8,128)S(1)} collective-permute-done((f32[128,128]{1,0:T(8,128)S(1)}, f32[128,128]{1,0:T(8,128)S(1)}, u32[]{:S(2)}, u32[]{:S(2)}) %collective-permute-start.13) | collective-permute-done | bytes 65568 | tf_op jit(solution)/shard_map/ppermute | solution.py:49
  64.6 1.4 %lift_1.1 = (f32[2176,128]{1,0:T(8,128)S(1)}, f32[64,128]{1,0:T(8,128)S(1)}, f32[64,128]{1,0:T(8,128)S(1)}, f32[64,128]{1,0:T(8,128)S(1)}, f32[64,128]{1,0:T(8,1...) custom-call(s32[8]{0:T(128)S(1)} %copy-done.2, f32[2176,128]{1,0:T(8,128)S(1)} %get-tuple-element.48.sol, ...), custom_call_target="tpu_custom_call" | custom-call | tf_op jit(solution)/shard_map/lift_1/pallas_call | solution.py:615
  66.0 0.1 collective-permute-start.14
  66.1 0.6 collective-permute-start.15
  66.8 0.0 collective-permute-start.16
  66.8 0.0 collective-permute-start.17
  66.8 0.0 collective-permute-start.18
  66.8 2.1 %collective-permute-done.14.refs_10_ = f32[64,128]{1,0:T(8,128)S(1)} collective-permute-done((f32[64,128]{1,0:T(8,128)S(1)}, f32[64,128]{1,0:T(8,128)S(1)}, u32[]{:S(2)}, u32[]{:S(2)}) %collective-permute-start.14) | collective-permute-done | bytes 32800 | tf_op jit(solution)/shard_map/ppermute | solution.py:49
  68.9 0.0 collective-permute-start.19
  68.9 3.8 %unload.1 = f32[2048,128]{1,0:T(8,128)} custom-call(f32[2176,128]{1,0:T(8,128)S(1)} %get-tuple-element.51.sol.refs_3_), custom_call_target="tpu_custom_call" | custom-call | tf_op jit(solution)/shard_map/unload/pallas_call | solution.py:636
  72.7 0.0 collective-permute-done.18.refs_14_
  72.7 3.2 %collective-permute-done.19.refs_15_ = f32[64,128]{1,0:T(8,128)S(1)} collective-permute-done((f32[64,128]{1,0:T(8,128)S(1)}, f32[64,128]{1,0:T(8,128)S(1)}, u32[]{:S(2)}, u32[]{:S(2)}) %collective-permute-start.19) | collective-permute-done | bytes 32800 | tf_op jit(solution)/shard_map/ppermute | solution.py:49
  75.8 5.5 %residual_1.1 = f32[2048,128]{1,0:T(8,128)} custom-call(s32[8]{0:T(128)S(1)} %copy-done.2, s32[8,6]{1,0:T(8,128)S(1)} %copy-done.1, f32[2176,128]{1,0:T(8,128)S(1)} %get-tuple-element.30.refs_0_.refs_2_, f32[2176,128]{1,0:T(8,128)S(1)} %get-tuple-element.51.sol.refs_3_, f32[64,128]{1,0:T(8,128)S(1)} %get-tuple-element.52.refs_4_, ...), custom_call_target="tpu_custom_call" | custom-call | tf_op jit(solution)/shard_map/residual_1/pallas_call | solution.py:637
  (8 shorter events, 0.0 us)
Async XLA Ops:
  0.6 1.2 %copy-start = (f32[64,4096]{1,0:T(8,128)S(1)}, f32[64,4096]{1,0:T(8,128)}, u32[]{:S(2)}) copy-start(f32[64,4096]{1,0:T(8,128)} %param.3) | copy-start | bytes 3145732
  1.9 0.7 copy-start.2
  3.1 11.5 %collective-permute-start = (f32[136,128]{1,0:T(8,128)S(1)}, f32[136,128]{1,0:T(8,128)S(1)}, u32[]{:S(2)}, u32[]{:S(2)}) collective-permute-start(f32[136,128]{1,0:T(8,128)S(1)} %get-tuple-element.32), channel_id=1, source_target_pairs={{0,64},{64,0},{1,65},{65,1},{2,66},{66,2},{3,67},{67,3},{4,68},{68... | collective-permute-start | bytes 208904 | tf_op jit(solution)/shard_map/ppermute | solution.py:49
  5.6 9.0 %collective-permute-start.1 = (f32[136,128]{1,0:T(8,128)S(1)}, f32[136,128]{1,0:T(8,128)S(1)}, u32[]{:S(2)}, u32[]{:S(2)}) collective-permute-start(f32[136,128]{1,0:T(8,128)S(1)} %get-tuple-element.33), channel_id=1, source_target_pairs={{0,65},{65,0},{1,66},{66,1},{2,67},{67,2},{3,68},{68,3},{4,69},{69... | collective-permute-start | bytes 208904 | tf_op jit(solution)/shard_map/ppermute | solution.py:49
  19.8 21.6 %copy-start.1 = (s32[8,6]{1,0:T(8,128)S(1)}, s32[8,6]{1,0:T(8,128)}, u32[]{:S(2)}) copy-start(s32[8,6]{1,0:T(8,128)} %refs_1_.3) | copy-start | bytes 580
  19.8 1.4 %collective-permute-start.2 = (f32[128,128]{1,0:T(8,128)S(1)}, f32[128,128]{1,0:T(8,128)S(1)}, u32[]{:S(2)}, u32[]{:S(2)}) collective-permute-start(f32[128,128]{1,0:T(8,128)S(1)} %get-tuple-element.36), channel_id=1, source_target_pairs={{0,64},{64,0},{1,65},{65,1},{2,66},{66,2},{3,67},{67,3},{4,68},{68... | collective-permute-start | bytes 196616 | tf_op jit(solution)/shard_map/ppermute | solution.py:49
  19.9 8.0 %collective-permute-start.3 = (f32[128,128]{1,0:T(8,128)S(1)}, f32[128,128]{1,0:T(8,128)S(1)}, u32[]{:S(2)}, u32[]{:S(2)}) collective-permute-start(f32[128,128]{1,0:T(8,128)S(1)} %get-tuple-element.37), channel_id=1, source_target_pairs={{0,65},{65,0},{1,66},{66,1},{2,67},{67,2},{3,68},{68,3},{4,69},{69... | collective-permute-start | bytes 196616 | tf_op jit(solution)/shard_map/ppermute | solution.py:49
  29.4 5.1 %collective-permute-start.4 = (f32[64,128]{1,0:T(8,128)S(1)}, f32[64,128]{1,0:T(8,128)S(1)}, u32[]{:S(2)}, u32[]{:S(2)}) collective-permute-start(f32[64,128]{1,0:T(8,128)S(1)} %get-tuple-element.39.refs_4_), channel_id=1, source_target_pairs={{0,16},{16,0},{64,80},{80,64},{1,17},{17,1},{65,81},{81,65},{2,18}... | collective-permute-start | bytes 98312 | tf_op jit(solution)/shard_map/ppermute | solution.py:49
  33.1 3.1 %collective-permute-start.5 = (f32[64,128]{1,0:T(8,128)S(1)}, f32[64,128]{1,0:T(8,128)S(1)}, u32[]{:S(2)}, u32[]{:S(2)}) collective-permute-start(f32[64,128]{1,0:T(8,128)S(1)} %get-tuple-element.40.refs_5_), channel_id=1, source_target_pairs={{16,32},{32,16},{80,96},{96,80},{17,33},{33,17},{81,97},{97,81},{1... | collective-permute-start | bytes 98312 | tf_op jit(solution)/shard_map/ppermute | solution.py:49
  33.1 3.3 %collective-permute-start.6 = (f32[64,128]{1,0:T(8,128)S(1)}, f32[64,128]{1,0:T(8,128)S(1)}, u32[]{:S(2)}, u32[]{:S(2)}) collective-permute-start(f32[64,128]{1,0:T(8,128)S(1)} %get-tuple-element.41.refs_6_), channel_id=1, source_target_pairs={{0,4},{4,0},{64,68},{68,64},{1,5},{5,1},{65,69},{69,65},{2,6},{6,2... | collective-permute-start | bytes 98312 | tf_op jit(solution)/shard_map/ppermute | solution.py:49
  33.1 5.1 %collective-permute-start.7 = (f32[64,128]{1,0:T(8,128)S(1)}, f32[64,128]{1,0:T(8,128)S(1)}, u32[]{:S(2)}, u32[]{:S(2)}) collective-permute-start(f32[64,128]{1,0:T(8,128)S(1)} %get-tuple-element.42.refs_7_), channel_id=1, source_target_pairs={{4,8},{8,4},{68,72},{72,68},{5,9},{9,5},{69,73},{73,69},{6,10},{10... | collective-permute-start | bytes 98312 | tf_op jit(solution)/shard_map/ppermute | solution.py:49
  33.1 5.1 %collective-permute-start.8 = (f32[64,128]{1,0:T(8,128)S(1)}, f32[64,128]{1,0:T(8,128)S(1)}, u32[]{:S(2)}, u32[]{:S(2)}) collective-permute-start(f32[64,128]{1,0:T(8,128)S(1)} %get-tuple-element.43.refs_8_), channel_id=1, source_target_pairs={{0,1},{1,0},{64,65},{65,64},{2,3},{3,2},{66,67},{67,66},{4,5},{5,4... | collective-permute-start | bytes 98312 | tf_op jit(solution)/shard_map/ppermute | solution.py:49
  34.4 7.0 %collective-permute-start.9 = (f32[64,128]{1,0:T(8,128)S(1)}, f32[64,128]{1,0:T(8,128)S(1)}, u32[]{:S(2)}, u32[]{:S(2)}) collective-permute-start(f32[64,128]{1,0:T(8,128)S(1)} %get-tuple-element.44.refs_9_), channel_id=1, source_target_pairs={{1,2},{2,1},{65,66},{66,65},{3,4},{4,3},{67,68},{68,67},{5,6},{6,5... | collective-permute-start | bytes 98312 | tf_op jit(solution)/shard_map/ppermute | solution.py:49
  43.7 2.0 %collective-permute-start.10 = (f32[128,128]{1,0:T(8,128)S(1)}, f32[128,128]{1,0:T(8,128)S(1)}, u32[]{:S(2)}, u32[]{:S(2)}) collective-permute-start(f32[128,128]{1,0:T(8,128)S(1)} %get-tuple-element.46), channel_id=1, source_target_pairs={{0,64},{64,0},{1,65},{65,1},{2,66},{66,2},{3,67},{67,3},{4,68},{68... | collective-permute-start | bytes 196616 | tf_op jit(solution)/shard_map/ppermute | solution.py:49
  43.8 8.0 %collective-permute-start.11 = (f32[128,128]{1,0:T(8,128)S(1)}, f32[128,128]{1,0:T(8,128)S(1)}, u32[]{:S(2)}, u32[]{:S(2)}) collective-permute-start(f32[128,128]{1,0:T(8,128)S(1)} %get-tuple-element.47), channel_id=1, source_target_pairs={{0,65},{65,0},{1,66},{66,1},{2,67},{67,2},{3,68},{68,3},{4,69},{69... | collective-permute-start | bytes 196616 | tf_op jit(solution)/shard_map/ppermute | solution.py:49
  56.5 1.3 %collective-permute-start.12 = (f32[128,128]{1,0:T(8,128)S(1)}, f32[128,128]{1,0:T(8,128)S(1)}, u32[]{:S(2)}, u32[]{:S(2)}) collective-permute-start(f32[128,128]{1,0:T(8,128)S(1)} %get-tuple-element.49), channel_id=1, source_target_pairs={{0,64},{64,0},{1,65},{65,1},{2,66},{66,2},{3,67},{67,3},{4,68},{68... | collective-permute-start | bytes 196616 | tf_op jit(solution)/shard_map/ppermute | solution.py:49
  56.6 8.0 %collective-permute-start.13 = (f32[128,128]{1,0:T(8,128)S(1)}, f32[128,128]{1,0:T(8,128)S(1)}, u32[]{:S(2)}, u32[]{:S(2)}) collective-permute-start(f32[128,128]{1,0:T(8,128)S(1)} %get-tuple-element.50), channel_id=1, source_target_pairs={{0,65},{65,0},{1,66},{66,1},{2,67},{67,2},{3,68},{68,3},{4,69},{69... | collective-permute-start | bytes 196616 | tf_op jit(solution)/shard_map/ppermute | solution.py:49
  66.0 2.8 %collective-permute-start.14 = (f32[64,128]{1,0:T(8,128)S(1)}, f32[64,128]{1,0:T(8,128)S(1)}, u32[]{:S(2)}, u32[]{:S(2)}) collective-permute-start(f32[64,128]{1,0:T(8,128)S(1)} %get-tuple-element.52.refs_4_), channel_id=1, source_target_pairs={{0,16},{16,0},{64,80},{80,64},{1,17},{17,1},{65,81},{81,65},{2,18}... | collective-permute-start | bytes 98312 | tf_op jit(solution)/shard_map/ppermute | solution.py:49
  66.1 6.5 %collective-permute-start.15 = (f32[64,128]{1,0:T(8,128)S(1)}, f32[64,128]{1,0:T(8,128)S(1)}, u32[]{:S(2)}, u32[]{:S(2)}) collective-permute-start(f32[64,128]{1,0:T(8,128)S(1)} %get-tuple-element.53.refs_5_), channel_id=1, source_target_pairs={{16,32},{32,16},{80,96},{96,80},{17,33},{33,17},{81,97},{97,81},{1... | collective-permute-start | bytes 98312 | tf_op jit(solution)/shard_map/ppermute | solution.py:49
  66.8 5.9 %collective-permute-start.16 = (f32[64,128]{1,0:T(8,128)S(1)}, f32[64,128]{1,0:T(8,128)S(1)}, u32[]{:S(2)}, u32[]{:S(2)}) collective-permute-start(f32[64,128]{1,0:T(8,128)S(1)} %get-tuple-element.54.refs_6_), channel_id=1, source_target_pairs={{0,4},{4,0},{64,68},{68,64},{1,5},{5,1},{65,69},{69,65},{2,6},{6,2... | collective-permute-start | bytes 98312 | tf_op jit(solution)/shard_map/ppermute | solution.py:49
  66.8 5.9 %collective-permute-start.17 = (f32[64,128]{1,0:T(8,128)S(1)}, f32[64,128]{1,0:T(8,128)S(1)}, u32[]{:S(2)}, u32[]{:S(2)}) collective-permute-start(f32[64,128]{1,0:T(8,128)S(1)} %get-tuple-element.55.refs_7_), channel_id=1, source_target_pairs={{4,8},{8,4},{68,72},{72,68},{5,9},{9,5},{69,73},{73,69},{6,10},{10... | collective-permute-start | bytes 98312 | tf_op jit(solution)/shard_map/ppermute | solution.py:49
  66.8 5.9 %collective-permute-start.18 = (f32[64,128]{1,0:T(8,128)S(1)}, f32[64,128]{1,0:T(8,128)S(1)}, u32[]{:S(2)}, u32[]{:S(2)}) collective-permute-start(f32[64,128]{1,0:T(8,128)S(1)} %get-tuple-element.56.refs_8_), channel_id=1, source_target_pairs={{0,1},{1,0},{64,65},{65,64},{2,3},{3,2},{66,67},{67,66},{4,5},{5,4... | collective-permute-start | bytes 98312 | tf_op jit(solution)/shard_map/ppermute | solution.py:49
  68.9 7.0 %collective-permute-start.19 = (f32[64,128]{1,0:T(8,128)S(1)}, f32[64,128]{1,0:T(8,128)S(1)}, u32[]{:S(2)}, u32[]{:S(2)}) collective-permute-start(f32[64,128]{1,0:T(8,128)S(1)} %get-tuple-element.57.refs_9_), channel_id=1, source_target_pairs={{1,2},{2,1},{65,66},{66,65},{3,4},{4,3},{67,68},{68,67},{5,6},{6,5... | collective-permute-start | bytes 98312 | tf_op jit(solution)/shard_map/ppermute | solution.py:49

commit v3 on v2

--- a/solution.py
+++ b/solution.py
@@ -31,18 +31,20 @@
     return pairs
 
 
-def level_pairs(step):
-    pairs = []
+def level_pairs():
+    own, down, up = [], [], []
     for b in range(N_BLK):
-        c = N_BLK + (b + step) % N_BLK
-        pairs += [(b, c), (c, b)]
-    return pairs
+        c, beyond = N_BLK + b, N_BLK + (b + 1) % N_BLK
+        own += [(b, c), (c, b)]
+        down += [(b, beyond), (c, b)]
+        up += [(beyond, b), (b, c)]
+    return own, down, up
 
 
 UNITS = (16, 4, 1)
+ORDER = (4, 5, 2, 3, 0, 1)
 HALO_PAIRS = [swap_pairs(unit, color) for unit in UNITS for color in (0, 1)]
-OWN_PAIRS = level_pairs(0)
-NEXT_PAIRS = level_pairs(1)
+OWN_PAIRS, DOWN_PAIRS, UP_PAIRS = level_pairs()
 
 
 def swap(x, pairs):
@@ -100,8 +102,14 @@
     return total
 
 
-def exchange(a, b, bit, shift):
-    return jnp.where(bit, roll(b, shift), a), jnp.where(bit, b, roll(a, 128 - shift))
+def exchange(a, b, bit, partner):
+    moved = jnp.take_along_axis(jnp.where(bit, a, b), partner, axis=1)
+    return jnp.where(bit, moved, a), jnp.where(bit, b, moved)
+
+
+def lane_bits(j, k):
+    lane = j * 16 + k
+    return [((lane & m) != 0, lane ^ m) for m in (1, 16, 32)]
 
 
 def spread_index(j, k):
@@ -109,29 +117,31 @@
 
 
 def to_working(v, j, k):
-    s = [exchange(v[q][0], v[q][1], (k & 1) == 1, 1) for q in range(4)]
+    z_bit, y_bit, y_next = lane_bits(j, k)
+    s = [exchange(v[q][0], v[q][1], *z_bit) for q in range(4)]
     index = spread_index(j, k)
     result = [[None, None] for _ in range(4)]
     for p in range(2):
-        t = [exchange(s[2 * h][p], s[2 * h + 1][p], (j & 1) == 1, 16) for h in range(2)]
+        t = [exchange(s[2 * h][p], s[2 * h + 1][p], *y_bit) for h in range(2)]
         for low in range(2):
-            pair = exchange(t[0][low], t[1][low], (j & 2) == 2, 32)
+            pair = exchange(t[0][low], t[1][low], *y_next)
             for high in range(2):
                 result[low + 2 * high][p] = jnp.take_along_axis(pair[high], index, axis=1)
     return result
 
 
 def to_given(a, j, k):
+    z_bit, y_bit, y_next = lane_bits(j, k)
     index = (2 * (j & 3) + (j >> 2)) * 16 + (k >> 1) + 8 * (k & 1)
     s = [[None, None] for _ in range(4)]
     for p in range(2):
         t = [[None, None], [None, None]]
         for low in range(2):
             pair = [jnp.take_along_axis(a[low + 2 * high][p], index, axis=1) for high in range(2)]
-            t[0][low], t[1][low] = exchange(pair[0], pair[1], (j & 2) == 2, 32)
+            t[0][low], t[1][low] = exchange(pair[0], pair[1], *y_next)
         for h in range(2):
-            s[2 * h][p], s[2 * h + 1][p] = exchange(t[h][0], t[h][1], (j & 1) == 1, 16)
-    return [exchange(s[q][0], s[q][1], (k & 1) == 1, 1) for q in range(4)]
+            s[2 * h][p], s[2 * h + 1][p] = exchange(t[h][0], t[h][1], *y_bit)
+    return [exchange(s[q][0], s[q][1], *z_bit) for q in range(4)]
 
 
 def given_rows(x, q, oz):
@@ -199,7 +209,7 @@
 
 
 def restrict_given(a, b, j, k):
-    z_even, y_even, high = (k & 1) == 0, (j & 1) == 0, (j & 2) == 2
+    z_even, y_even = (k & 1) == 0, (j & 1) == 0
     u = []
     for q in range(4):
         lo, hi = a[q][0] + b[q][0], a[q][1] + b[q][1]
@@ -208,7 +218,7 @@
     for h in range(2):
         m.append(jnp.where(y_even, u[2 * h] + roll(u[2 * h], 112), u[2 * h + 1] + roll(u[2 * h + 1], 16)))
     index = spread_index(j, k)
-    return [0.5 * jnp.take_along_axis(n, index, axis=1) for n in exchange(m[0], m[1], high, 32)]
+    return [0.5 * jnp.take_along_axis(n, index, axis=1) for n in exchange(m[0], m[1], *lane_bits(j, k)[2])]
 
 
 def parent_slots(parent, blk):
@@ -252,17 +262,20 @@
     for n in range(8):
         buf, slot, tag = arrived[n // 4], n % 4, tags[n]
 
-        @pl.when(tag >= 0)
-        def _(buf=buf, slot=slot, tag=tag):
-            for s in range(2):
-                for half in range(2):
-                    at, oy, oz = block_place(tag, s, half)
-                    here = ((j >> 2) == oy) & ((k >> 3) == oz)
-                    value = rows(buf, slot * 32 + s * 16 + half * 8)
-                    for t in range(2):
-                        for p in range(2):
-                            spread = jnp.take_along_axis(value, index[t][p], axis=1)
-                            rhs[at[t][p], :] = rhs[at[t][p], :] + jnp.where(here, spread, 0.0)
+        used, block = tag >= 0, jnp.maximum(tag, 0)
+        places, spread = [], []
+        for s in range(2):
+            for half in range(2):
+                at, oy, oz = block_place(block, s, half)
+                here = ((j >> 2) == jnp.where(used, oy, -1)) & ((k >> 3) == oz)
+                value = rows(buf, slot * 32 + s * 16 + half * 8)
+                for t in range(2):
+                    for p in range(2):
+                        places.append(at[t][p])
+                        spread.append(jnp.where(here, jnp.take_along_axis(value, index[t][p], axis=1), 0.0))
+        total = [rhs[at, :] + value for at, value in zip(places, spread)]
+        for at, value in zip(places, total):
+            rhs[at, :] = value
 
 
 def answer(correction, tags, out):
@@ -271,21 +284,20 @@
     for n in range(8):
         buf, slot, tag = out[n // 4], n % 4, tags[n]
 
-        @pl.when(tag >= 0)
-        def _(buf=buf, slot=slot, tag=tag):
-            for s in range(2):
-                for half in range(2):
-                    at, oy, oz = block_place(tag, s, half)
-                    index = (4 * oy + (j >> 1)) * 16 + 8 * oz + (k >> 1)
-                    v = [
-                        [jnp.take_along_axis(correction[at[t][p], :], index, axis=1) for p in range(2)]
-                        for t in range(2)
-                    ]
-                    v = [jnp.where(z_odd, v[t][1], v[t][0]) for t in range(2)]
-                    put(buf, slot * 32 + s * 16 + half * 8, jnp.where(y_odd, v[1], v[0]))
-
-
-def first_down_kernel(parent, source, own, nxt, down):
+        block = jnp.maximum(tag, 0)
+        found = []
+        for s in range(2):
+            for half in range(2):
+                at, oy, oz = block_place(block, s, half)
+                index = (4 * oy + (j >> 1)) * 16 + 8 * oz + (k >> 1)
+                v = [[jnp.take_along_axis(correction[at[t][p], :], index, axis=1) for p in range(2)] for t in range(2)]
+                v = [jnp.where(z_odd, v[t][1], v[t][0]) for t in range(2)]
+                found.append(jnp.where(y_odd, v[1], v[0]))
+        for i, value in enumerate(found):
+            put(buf, slot * 32 + i * 8, value)
+
+
+def first_down_kernel(parent, source, nxt, own, down):
     sec, blk = position()
     j, k = lane_parts()
 
@@ -327,22 +339,14 @@
 
 def coarse_kernel(first, *refs):
     if first:
-        res, sol, in_own, in_next, out_sol, out_own, out_next, tags, rhs, mid, smem, sem = refs
+        res, in_next, in_own, out_sol, out_next, out_own, tags, rhs, mid, smem, sem = refs
     else:
-        tags, res, sol, in_own, in_next, out_sol, out_own, out_next, rhs, mid, corr = refs
+        tags, res, sol, _, in_next, in_own, out_sol, out_next, out_own, rhs, mid, corr = refs
     sec, _ = position()
 
     if first:
         for j in range(8):
             tags[j] = jnp.int32(-1)
-
-    @pl.when(sec == 0)
-    def _():
-        def copy(i, _):
-            put(out_sol, i * 64, rows(sol, i * 64, 64))
-            return 0
-
-        lax.fori_loop(1, 33, copy, 0)
 
     @pl.when(sec == 1)
     def _():
@@ -377,7 +381,7 @@
         answer(out_sol if first else corr, tags, (out_own, out_next))
 
 
-def lift_kernel(parent, sol, in_own, in_next, out_sol, *refs):
+def lift_kernel(parent, sol, coarse_sol, in_next, in_own, out_sol, *refs):
     out, (lift, face) = refs[:6], refs[6:]
     sec, blk = position()
     j, k = lane_parts()
@@ -438,100 +442,97 @@
 
     @pl.when(sec == 1)
     def _():
-        lax.fori_loop(0, 4, functools.partial(pack, lambda g: [plane(sol, 8 * g + m) for m in range(8)]), 0)
+        lax.fori_loop(0, 4, functools.partial(pack, lambda g: [plane(coarse_sol, 8 * g + m) for m in range(8)]), 0)
 
     put(face, 0, rows(out_sol, 64, 64))
     put(face, 64, rows(out_sol, 32 * 64, 64))
     for axis, parity in enumerate(parities(blk)):
         for color in range(2):
             d = 2 * axis + (parity == color).astype(jnp.int32)
-            out[2 * axis + color][...] = rows(face, d * 64, 64)
-
-
-def residual_kernel(last, parent, neighbor, src, sol, *refs):
-    sent, got = refs[:6], refs[6:12]
+            out[ORDER.index(2 * axis + color)][...] = rows(face, d * 64, 64)
+
+
+def residual_kernel(level, parent, neighbor, src, sol, *refs):
+    sent, got = ([refs[first + ORDER.index(n)] for n in range(6)] for first in (0, 6))
+    last, fine = level is None, level == 0
+    if fine:
+        res, nxt, own, halo, table, down = refs[12:]
+    else:
+        res, halo, table = refs[12:]
+    sec, blk = position()
+
+    def whole():
+        j, k = lane_parts()
+
+        for axis, parity in enumerate(parities(blk)):
+            for color in range(2):
+                odd = (parity == color).astype(jnp.int32)
+                put(table, (2 * axis + 1 - odd) * 128, sent[2 * axis + color][...])
+                put(table, (2 * axis + odd) * 128 + 64, got[2 * axis + color][...])
+        device = sec * N_BLK + blk
+
+        def gather(g, _):
+            for d in range(6):
+                other = neighbor[g, d]
+                local = (other >> 3) == device
+                start = d * 128 + jnp.where(local, 0, 64) + (other & 7)
+                value = table[pl.ds(start, 8, stride=8), :]
+                halo[pl.ds(d * 64 + g, 8, stride=8), :] = jnp.where(other >= 0, value, 0.0)
+            return 0
+
+        lax.fori_loop(0, FAM, gather, 0)
+
+        def side(base):
+            return [[rows(halo, base + (q * 2 + o) * 8) for o in range(2)] for q in range(4)]
+
+        def residue(x, a, below, above):
+            y_at, z_at = x & 7, x & 15
+            y_rows = [128 + (o * 4 + (x >> 3)) * 8 for o in range(2)]
+            hy = [
+                [roll(rows(halo, y_rows[o]), (128 - 16 * y_at) & 127) for o in range(2)],
+                [roll(rows(halo, y_rows[o] + 64), 112 - 16 * y_at) for o in range(2)],
+            ]
+            hz = []
+            for q in range(4):
+                at = 256 + (q * 2 + (x >> 4)) * 8
+                hz.append([roll(rows(halo, at), (128 - z_at) & 127), roll(rows(halo, at + 64), 15 - z_at)])
+            m = around(a, below, above, j, k, hy, hz)
+            s = plane(src, x)
+            return [[s[q][o] - 6.0 * a[q][o] + m[q][o] for o in range(2)] for q in range(4)]
+
+        def store(x, r):
+            if last:
+                put_given(res, x, to_given(r, j, k))
+            else:
+                put_plane(res, x, r)
+
+        def group(i, _, low=None, high=None):
+            x = GROUP * i
+            p = [plane(sol, x + m) for m in range(GROUP)]
+            p = [plane(sol, x - 1) if low is None else low] + p + [plane(sol, x + GROUP) if high is None else high]
+            r = [residue(x + m, p[m + 1], p[m], p[m + 2]) for m in range(GROUP)]
+            for m in range(GROUP):
+                store(x + m, r[m])
+            if fine:
+                for m in range(GROUP // 2):
+                    put_down(down, (GROUP // 2) * i + m, restrict_pair(r[2 * m], r[2 * m + 1]))
+            return 0
+
+        count = 32 // GROUP
+        group(0, 0, low=side(0))
+        lax.fori_loop(1, count - 1, group, 0)
+        group(count - 1, 0, high=side(64))
+        if fine:
+            send_down(down, parent, blk, own, nxt, False)
+
     if last:
-        res, halo, table = refs[12:]
+        whole()
     else:
-        res, own, nxt, halo, table, down = refs[12:]
-    sec, blk = position()
-    j, k = lane_parts()
-
-    for axis, parity in enumerate(parities(blk)):
-        for color in range(2):
-            odd = (parity == color).astype(jnp.int32)
-            put(table, (2 * axis + 1 - odd) * 128, sent[2 * axis + color][...])
-            put(table, (2 * axis + odd) * 128 + 64, got[2 * axis + color][...])
-    device = sec * N_BLK + blk
-
-    def gather(g, _):
-        for d in range(6):
-            other = neighbor[g, d]
-            local = (other >> 3) == device
-            start = d * 128 + jnp.where(local, 0, 64) + (other & 7)
-            value = table[pl.ds(start, 8, stride=8), :]
-            halo[pl.ds(d * 64 + g, 8, stride=8), :] = jnp.where(other >= 0, value, 0.0)
-        return 0
-
-    lax.fori_loop(0, FAM, gather, 0)
-
-    def side(base):
-        return [[rows(halo, base + (q * 2 + o) * 8) for o in range(2)] for q in range(4)]
-
-    def residue(x, a, below, above):
-        y_at, z_at = x & 7, x & 15
-        y_rows = [128 + (o * 4 + (x >> 3)) * 8 for o in range(2)]
-        hy = [
-            [roll(rows(halo, y_rows[o]), (128 - 16 * y_at) & 127) for o in range(2)],
-            [roll(rows(halo, y_rows[o] + 64), 112 - 16 * y_at) for o in range(2)],
-        ]
-        hz = []
-        for q in range(4):
-            at = 256 + (q * 2 + (x >> 4)) * 8
-            hz.append([roll(rows(halo, at), (128 - z_at) & 127), roll(rows(halo, at + 64), 15 - z_at)])
-        m = around(a, below, above, j, k, hy, hz)
-        s = plane(src, x)
-        return [[s[q][o] - 6.0 * a[q][o] + m[q][o] for o in range(2)] for q in range(4)]
-
-    def store(x, r):
-        if last:
-            put_given(res, x, to_given(r, j, k))
-        else:
-            put_plane(res, x, r)
-
-    def group(i, _, low=None, high=None):
-        x = GROUP * i
-        p = [plane(sol, x + m) for m in range(GROUP)]
-        p = [plane(sol, x - 1) if low is None else low] + p + [plane(sol, x + GROUP) if high is None else high]
-        r = [residue(x + m, p[m + 1], p[m], p[m + 2]) for m in range(GROUP)]
-        for m in range(GROUP):
-            store(x + m, r[m])
-        if not last:
-            for m in range(GROUP // 2):
-                put_down(down, (GROUP // 2) * i + m, restrict_pair(r[2 * m], r[2 * m + 1]))
-        return 0
-
-    count = 32 // GROUP
-    group(0, 0, low=side(0))
-    lax.fori_loop(1, count - 1, group, 0)
-    group(count - 1, 0, high=side(64))
-    if not last:
-
-        @pl.when(sec == 0)
-        def _():
-            send_down(down, parent, blk, own, nxt, False)
+        pl.when(sec == level)(whole)
 
 
 def fine_kernel(res, sol, out_sol, rhs, mid):
     sec, _ = position()
-
-    @pl.when(sec == 1)
-    def _():
-        def copy(i, _):
-            put(out_sol, i * 64, rows(sol, i * 64, 64))
-            return 0
-
-        lax.fori_loop(1, 33, copy, 0)
 
     @pl.when(sec == 0)
     def _():
@@ -583,64 +584,59 @@
     tiles = source.reshape(FAM, 8, 32, 128).transpose(0, 2, 1, 3).reshape(2048, 128)
     pad, pads = shape(PAD_ROWS), scratch(PAD_ROWS)
 
-    def both(own, nxt):
-        return swap(nxt, NEXT_PAIRS), swap(own, OWN_PAIRS)
-
-    own, nxt = call(first_down_kernel, "first_down", [SMEM, VMEM], (shape(136), shape(136)), [scratch(256)])(
+    def both(nxt, own, pairs):
+        return swap(nxt, pairs), swap(own, OWN_PAIRS)
+
+    nxt, own = call(first_down_kernel, "first_down", [SMEM, VMEM], (shape(136), shape(136)), [scratch(256)])(
         parent, tiles
     )
-    got_next, got_own = both(own, nxt)
-    src, sol = call(load_kernel, "load", [VMEM], (pad, pad), [pads])(tiles)
-    res, tags = src, None
-    for iteration in range(2):
-        first = iteration == 0
-        if first:
-            sol, own, nxt, tags = call(
-                lambda *refs: coarse_kernel(True, *refs),
-                "coarse_0",
-                [VMEM] * 4,
-                (pad, shape(128), shape(128), jax.ShapeDtypeStruct((8,), jnp.int32)),
-                [pads, pads, pltpu.SMEM((2, 8, 128), F32), pltpu.SemaphoreType.DMA((2,))],
-                [VMEM, VMEM, VMEM, SMEM],
-            )(res, sol, got_own, got_next)
-        else:
-            sol, own, nxt = call(
-                lambda *refs: coarse_kernel(False, *refs),
-                "coarse_1",
-                [SMEM] + [VMEM] * 4,
-                (pad, shape(128), shape(128)),
-                [pads, pads, pads],
-            )(tags, res, sol, got_own, got_next)
-        got_next, got_own = both(own, nxt)
+    got_next, got_own = both(nxt, own, DOWN_PAIRS)
+    src, fine_sol = call(load_kernel, "load", [VMEM], (pad, pad), [pads])(tiles)
+    coarse_sol, nxt, own, tags = call(
+        functools.partial(coarse_kernel, True),
+        "coarse_0",
+        [VMEM] * 3,
+        (pad, shape(128), shape(128), jax.ShapeDtypeStruct((8,), jnp.int32)),
+        [pads, pads, pltpu.SMEM((2, 8, 128), F32), pltpu.SemaphoreType.DMA((2,))],
+        [VMEM, VMEM, VMEM, SMEM],
+    )(src, got_next, got_own)
+
+    def lift_and_share(n, nxt, own):
+        got_next, got_own = both(nxt, own, UP_PAIRS)
         out = call(
             lift_kernel,
-            f"lift_{iteration}",
-            [SMEM, VMEM, VMEM, VMEM],
+            f"lift_{n}",
+            [SMEM] + [VMEM] * 4,
             (pad,) + (shape(64),) * 6,
             [scratch(256), scratch(384)],
-        )(parent, sol, got_own, got_next)
+        )(parent, fine_sol, coarse_sol, got_next, got_own)
         sol, sent = out[0], out[1:]
-        got = [swap(s, pairs) for s, pairs in zip(sent, HALO_PAIRS)]
-        ins = [SMEM, SMEM] + [VMEM] * 14
-        if first:
-            res, own, nxt = call(
-                lambda *refs: residual_kernel(False, *refs),
-                "residual_0",
-                ins,
-                (pad, shape(128), shape(128)),
-                [scratch(384), scratch(768), scratch(256)],
-            )(parent, neighbor, src, sol, *sent, *got)
-            got_next, got_own = both(own, nxt)
-            (sol,) = call(fine_kernel, "fine", [VMEM, VMEM], (pad,), [pads, pads])(res, sol)
-        else:
-            (solution,) = call(unload_kernel, "unload", [VMEM], (shape(2048),))(sol)
-            (residual,) = call(
-                lambda *refs: residual_kernel(True, *refs),
-                "residual_1",
-                ins,
-                (shape(2048),),
-                [scratch(384), scratch(768)],
-            )(parent, neighbor, src, sol, *sent, *got)
+        return sol, [*sent, *(swap(face, HALO_PAIRS[n]) for face, n in zip(sent, ORDER))]
+
+    def residue_of(level, name, sol, faces, out_shape, more=()):
+        return call(
+            functools.partial(residual_kernel, level),
+            name,
+            [SMEM, SMEM] + [VMEM] * 14,
+            out_shape,
+            [scratch(384), scratch(768), *more],
+        )(parent, neighbor, src, sol, *faces)
+
+    sol, faces = lift_and_share(0, nxt, own)
+    res, nxt, own = residue_of(0, "residue_fine", sol, faces, (pad, shape(128), shape(128)), [scratch(256)])
+    got_next, got_own = both(nxt, own, DOWN_PAIRS)
+    (coarse_res,) = residue_of(1, "residue_coarse", sol, faces, (pad,))
+    (fine_sol,) = call(fine_kernel, "fine", [VMEM, VMEM], (pad,), [pads, pads])(res, sol)
+    coarse_sol, nxt, own = call(
+        functools.partial(coarse_kernel, False),
+        "coarse_1",
+        [SMEM] + [VMEM] * 5,
+        (pad, shape(128), shape(128)),
+        [pads, pads, pads],
+    )(tags, coarse_res, sol, fine_sol, got_next, got_own)
+    sol, faces = lift_and_share(1, nxt, own)
+    (solution,) = call(unload_kernel, "unload", [VMEM], (shape(2048),))(sol)
+    (residual,) = residue_of(None, "residual", sol, faces, (shape(2048),))
 
     def blocks(x):
         return x.reshape(FAM, 32, 8, 128).transpose(0, 2, 1, 3).reshape(64, 4096)

time: 81.5 us -> 67.3 us (0.83)
  the two profiles are of different devices: /device:TPU:3 before, /device:TPU:18 now
where the time goes in v3:
time: 67.3 us; the launch traced here: 67.1 us
  starting transfers between devices  32.5 us (48%)
  Pallas kernels  26.2 us (39%)
  waiting for transfers between devices  5.76 us (9%)
  local copies, waits for them, and re-layouts  1.88 us (3%)
  between operations  0.8 us (1%)
    ppermute x20, starting transfers between devices, swap(): return lax.ppermute(x, AX, pairs)  32.5 us
    pallas_call x3, Pallas kernels, residue_of(): call(functools.partial(residual_kernel, level), name, [SMEM, SMEM] + [VME...  8.54 us
    ppermute x20, waiting for transfers between devices, swap(): return lax.ppermute(x, AX, pairs)  5.76 us
    pallas_call x1, Pallas kernels, local(): src, fine_sol = call(load_kernel, 'load', [VMEM], (pad, pad), [pads])(tiles)  4.86 us
    pallas_call x1, Pallas kernels, local(): solution, = call(unload_kernel, 'unload', [VMEM], (shape(2048),))(sol)  3.84 us
    pallas_call x2, Pallas kernels, lift_and_share(): call(lift_kernel, f'lift_{n}', [SMEM] + [VMEM] * 4, (pad,) + (shape(64),)...  3.24 us
    pallas_call x1, Pallas kernels, local(): call(first_down_kernel, 'first_down', [SMEM, VMEM], (shape(136), shape(13...  2.34 us
    pallas_call x1, Pallas kernels, local(): call(fine_kernel, 'fine', [VMEM, VMEM], (pad,), [pads, pads])(res, sol)  2.2 us
  transfers between devices with their start and end apart: 20, of which 5 were waited for; matrix products, arithmetic and copies ran while one was open for 0% of the time, Pallas kernels for 17%

profile of v3, /device:TPU:18, one launch (start us, length us, event | category | flops | bytes accessed | tf_op | source)
XLA Modules:
  0.0 67.1 jit_solution(7939021775511821745)
XLA Ops:
  0.6 1.2 %copy-done = f32[64,4096]{1,0:T(8,128)S(1)} copy-done((f32[64,4096]{1,0:T(8,128)S(1)}, f32[64,4096]{1,0:T(8,128)}, u32[]{:S(2)}) %copy-start) | copy-done | bytes 1048600
  1.9 0.7 copy-done.2
  2.5 2.3 %first_down.1 = (f32[136,128]{1,0:T(8,128)S(1)}, f32[136,128]{1,0:T(8,128)S(1)}) custom-call(s32[8]{0:T(128)S(1)} %copy-done.2, f32[2048,128]{1,0:T(8,128)S(1)} %bitcast.15), custom_call_target="tpu_custom_call" | custom-call | tf_op jit(solution)/shard_map/first_down/pallas_call | solution.py:590
  4.9 0.1 collective-permute-start
  4.9 0.0 copy-start.3
  5.0 0.5 collective-permute-start.1
  5.4 4.9 %load.1 = (f32[2176,128]{1,0:T(8,128)S(1)}, f32[2176,128]{1,0:T(8,128)S(1)}) custom-call(f32[2048,128]{1,0:T(8,128)S(1)} %bitcast.16), custom_call_target="tpu_custom_call" | custom-call | tf_op jit(solution)/shard_map/load/pallas_call | solution.py:594
  10.3 0.0 collective-permute-done.refs_1_
  10.3 0.6 coarse_0.1
  11.0 4.4 %collective-permute-start.2 = (f32[128,128]{1,0:T(8,128)S(1)}, f32[128,128]{1,0:T(8,128)S(1)}, u32[]{:S(2)}, u32[]{:S(2)}) collective-permute-start(f32[128,128]{1,0:T(8,128)S(1)} %get-tuple-element.35), channel_id=1, source_target_pairs={{65,0},{0,64},{66,1},{1,65},{67,2},{2,66},{68,3},{3,67},{69,4},{4,... | collective-permute-start | bytes 196616 | tf_op jit(solution)/shard_map/ppermute | solution.py:51
  15.4 0.1 collective-permute-start.3
  15.5 0.8 %collective-permute-done.2.in_next = f32[128,128]{1,0:T(8,128)S(1)} collective-permute-done((f32[128,128]{1,0:T(8,128)S(1)}, f32[128,128]{1,0:T(8,128)S(1)}, u32[]{:S(2)}, u32[]{:S(2)}) %collective-permute-start.2) | collective-permute-done | bytes 65568 | tf_op jit(solution)/shard_map/ppermute | solution.py:51
  16.3 0.3 collective-permute-done.3.in_own
  16.7 1.6 %lift_0.1 = (f32[2176,128]{1,0:T(8,128)S(1)}, f32[64,128]{1,0:T(8,128)S(1)}, f32[64,128]{1,0:T(8,128)S(1)}, f32[64,128]{1,0:T(8,128)S(1)}, f32[64,128]{1,0:T(8,1...) custom-call(s32[8]{0:T(128)S(1)} %copy-done.3, f32[2176,128]{1,0:T(8,128)S(1)} %get-tuple-element.31.sol, ...), custom_call_target="tpu_custom_call" | custom-call | tf_op jit(solution)/shard_map/lift_0/pallas_call | solution.py:606
  18.3 1.7 %collective-permute-start.4 = (f32[64,128]{1,0:T(8,128)S(1)}, f32[64,128]{1,0:T(8,128)S(1)}, u32[]{:S(2)}, u32[]{:S(2)}) collective-permute-start(f32[64,128]{1,0:T(8,128)S(1)} %get-tuple-element.38.refs_0_), channel_id=1, source_target_pairs={{0,1},{1,0},{64,65},{65,64},{2,3},{3,2},{66,67},{67,66},{4,5},{5,4... | collective-permute-start | bytes 98312 | tf_op jit(solution)/shard_map/ppermute | solution.py:51
  20.0 2.9 %collective-permute-start.5 = (f32[64,128]{1,0:T(8,128)S(1)}, f32[64,128]{1,0:T(8,128)S(1)}, u32[]{:S(2)}, u32[]{:S(2)}) collective-permute-start(f32[64,128]{1,0:T(8,128)S(1)} %get-tuple-element.39.refs_1_), channel_id=1, source_target_pairs={{1,2},{2,1},{65,66},{66,65},{3,4},{4,3},{67,68},{68,67},{5,6},{6,5... | collective-permute-start | bytes 98312 | tf_op jit(solution)/shard_map/ppermute | solution.py:51
  22.9 1.6 %collective-permute-start.6 = (f32[64,128]{1,0:T(8,128)S(1)}, f32[64,128]{1,0:T(8,128)S(1)}, u32[]{:S(2)}, u32[]{:S(2)}) collective-permute-start(f32[64,128]{1,0:T(8,128)S(1)} %get-tuple-element.40.refs_2_), channel_id=1, source_target_pairs={{0,4},{4,0},{64,68},{68,64},{1,5},{5,1},{65,69},{69,65},{2,6},{6,2... | collective-permute-start | bytes 98312 | tf_op jit(solution)/shard_map/ppermute | solution.py:51
  24.5 4.0 %collective-permute-start.7 = (f32[64,128]{1,0:T(8,128)S(1)}, f32[64,128]{1,0:T(8,128)S(1)}, u32[]{:S(2)}, u32[]{:S(2)}) collective-permute-start(f32[64,128]{1,0:T(8,128)S(1)} %get-tuple-element.41.refs_3_), channel_id=1, source_target_pairs={{4,8},{8,4},{68,72},{72,68},{5,9},{9,5},{69,73},{73,69},{6,10},{10... | collective-permute-start | bytes 98312 | tf_op jit(solution)/shard_map/ppermute | solution.py:51
  28.4 0.0 collective-permute-start.8
  28.5 0.0 collective-permute-done.4.refs_6_
  28.5 3.0 %collective-permute-start.9 = (f32[64,128]{1,0:T(8,128)S(1)}, f32[64,128]{1,0:T(8,128)S(1)}, u32[]{:S(2)}, u32[]{:S(2)}) collective-permute-start(f32[64,128]{1,0:T(8,128)S(1)} %get-tuple-element.43.refs_5_), channel_id=1, source_target_pairs={{16,32},{32,16},{80,96},{96,80},{17,33},{33,17},{81,97},{97,81},{1... | collective-permute-start | bytes 98312 | tf_op jit(solution)/shard_map/ppermute | solution.py:51
  31.4 0.0 collective-permute-done.5.refs_7_
  31.4 0.0 collective-permute-done.6.refs_8_
  31.4 0.0 collective-permute-done.7.refs_9_
  31.5 0.9 %collective-permute-done.8.refs_10_ = f32[64,128]{1,0:T(8,128)S(1)} collective-permute-done((f32[64,128]{1,0:T(8,128)S(1)}, f32[64,128]{1,0:T(8,128)S(1)}, u32[]{:S(2)}, u32[]{:S(2)}) %collective-permute-start.8) | collective-permute-done | bytes 32800 | tf_op jit(solution)/shard_map/ppermute | solution.py:51
  32.4 1.0 %collective-permute-done.9.refs_11_ = f32[64,128]{1,0:T(8,128)S(1)} collective-permute-done((f32[64,128]{1,0:T(8,128)S(1)}, f32[64,128]{1,0:T(8,128)S(1)}, u32[]{:S(2)}, u32[]{:S(2)}) %collective-permute-start.9) | collective-permute-done | bytes 32800 | tf_op jit(solution)/shard_map/ppermute | solution.py:51
  33.3 2.4 %residue_fine.1 = (f32[2176,128]{1,0:T(8,128)S(1)}, f32[128,128]{1,0:T(8,128)S(1)}, f32[128,128]{1,0:T(8,128)S(1)}) custom-call(s32[8]{0:T(128)S(1)} %copy-done.3, s32[8,6]{1,0:T(8,128)S(1)} %copy-done.1, f32[2176,128]{1,0:T(8,128)S(1)} %get-tuple-element.30.refs_0_.src, f32[2176,128]{1,0:T(8,128)S(1)} %get-tuple-element.37.sol.refs_2_, ...), custom_call_target="tpu_custom_call" | custom-call | tf_op jit(solution)/shard_map/residue_fine/pallas_call | solution.py:617
  35.7 0.1 collective-permute-start.10
  35.8 0.5 collective-permute-start.11
  36.3 2.2 %fine.1.refs_3_.sol = f32[2176,128]{1,0:T(8,128)S(1)} custom-call(f32[2176,128]{1,0:T(8,128)S(1)} %get-tuple-element.44.res, f32[2176,128]{1,0:T(8,128)S(1)} %get-tuple-element.37.sol.refs_2_), custom_call_target="tpu_custom_call" | custom-call | tf_op jit(solution)/shard_map/fine/pallas_call | solution.py:629
  38.5 0.6 residue_coarse.1.refs_1_
  39.1 0.6 coarse_1.1
  39.7 2.9 %collective-permute-start.12 = (f32[128,128]{1,0:T(8,128)S(1)}, f32[128,128]{1,0:T(8,128)S(1)}, u32[]{:S(2)}, u32[]{:S(2)}) collective-permute-start(f32[128,128]{1,0:T(8,128)S(1)} %get-tuple-element.49), channel_id=1, source_target_pairs={{65,0},{0,64},{66,1},{1,65},{67,2},{2,66},{68,3},{3,67},{69,4},{4,... | collective-permute-start | bytes 196616 | tf_op jit(solution)/shard_map/ppermute | solution.py:51
  42.6 0.1 collective-permute-start.13
  42.7 2.7 %collective-permute-done.12.in_next = f32[128,128]{1,0:T(8,128)S(1)} collective-permute-done((f32[128,128]{1,0:T(8,128)S(1)}, f32[128,128]{1,0:T(8,128)S(1)}, u32[]{:S(2)}, u32[]{:S(2)}) %collective-permute-start.12) | collective-permute-done | bytes 65568 | tf_op jit(solution)/shard_map/ppermute | solution.py:51
  45.4 0.0 collective-permute-done.13.in_own
  45.4 1.6 %lift_1.1 = (f32[2176,128]{1,0:T(8,128)S(1)}, f32[64,128]{1,0:T(8,128)S(1)}, f32[64,128]{1,0:T(8,128)S(1)}, f32[64,128]{1,0:T(8,128)S(1)}, f32[64,128]{1,0:T(8,1...) custom-call(s32[8]{0:T(128)S(1)} %copy-done.3, f32[2176,128]{1,0:T(8,128)S(1)} %fine.1.refs_3_.sol, ...), custom_call_target="tpu_custom_call" | custom-call | tf_op jit(solution)/shard_map/lift_1/pallas_call | solution.py:606
  47.0 0.3 collective-permute-start.14
  47.3 2.8 %collective-permute-start.15 = (f32[64,128]{1,0:T(8,128)S(1)}, f32[64,128]{1,0:T(8,128)S(1)}, u32[]{:S(2)}, u32[]{:S(2)}) collective-permute-start(f32[64,128]{1,0:T(8,128)S(1)} %get-tuple-element.53.refs_1_), channel_id=1, source_target_pairs={{1,2},{2,1},{65,66},{66,65},{3,4},{4,3},{67,68},{68,67},{5,6},{6,5... | collective-permute-start | bytes 98312 | tf_op jit(solution)/shard_map/ppermute | solution.py:51
  50.1 1.1 %collective-permute-start.16 = (f32[64,128]{1,0:T(8,128)S(1)}, f32[64,128]{1,0:T(8,128)S(1)}, u32[]{:S(2)}, u32[]{:S(2)}) collective-permute-start(f32[64,128]{1,0:T(8,128)S(1)} %get-tuple-element.54.refs_2_), channel_id=1, source_target_pairs={{0,4},{4,0},{64,68},{68,64},{1,5},{5,1},{65,69},{69,65},{2,6},{6,2... | collective-permute-start | bytes 98312 | tf_op jit(solution)/shard_map/ppermute | solution.py:51
  51.2 3.5 %collective-permute-start.17 = (f32[64,128]{1,0:T(8,128)S(1)}, f32[64,128]{1,0:T(8,128)S(1)}, u32[]{:S(2)}, u32[]{:S(2)}) collective-permute-start(f32[64,128]{1,0:T(8,128)S(1)} %get-tuple-element.55.refs_3_), channel_id=1, source_target_pairs={{4,8},{8,4},{68,72},{72,68},{5,9},{9,5},{69,73},{73,69},{6,10},{10... | collective-permute-start | bytes 98312 | tf_op jit(solution)/shard_map/ppermute | solution.py:51
  54.7 0.0 collective-permute-start.18
  54.7 0.0 collective-permute-done.14.refs_6_
  54.7 3.0 %collective-permute-start.19 = (f32[64,128]{1,0:T(8,128)S(1)}, f32[64,128]{1,0:T(8,128)S(1)}, u32[]{:S(2)}, u32[]{:S(2)}) collective-permute-start(f32[64,128]{1,0:T(8,128)S(1)} %get-tuple-element.57.refs_5_), channel_id=1, source_target_pairs={{16,32},{32,16},{80,96},{96,80},{17,33},{33,17},{81,97},{97,81},{1... | collective-permute-start | bytes 98312 | tf_op jit(solution)/shard_map/ppermute | solution.py:51
  57.7 3.8 %unload.1 = f32[2048,128]{1,0:T(8,128)} custom-call(f32[2176,128]{1,0:T(8,128)S(1)} %get-tuple-element.51.sol), custom_call_target="tpu_custom_call" | custom-call | tf_op jit(solution)/shard_map/unload/pallas_call | solution.py:638
  61.5 0.0 collective-permute-done.15.refs_7_
  61.5 0.0 collective-permute-done.16.refs_8_
  61.6 5.6 %residual.1 = f32[2048,128]{1,0:T(8,128)} custom-call(s32[8]{0:T(128)S(1)} %copy-done.3, s32[8,6]{1,0:T(8,128)S(1)} %copy-done.1, f32[2176,128]{1,0:T(8,128)S(1)} %get-tuple-element.30.refs_0_.src, f32[2176,128]{1,0:T(8,128)S(1)} %get-tuple-element.51.sol, f32[64,128]{1,0:T(8,128)S(1)} %get-tuple-element.52.refs_0_, ...), custom_call_target="tpu_custom_call" | custom-call | tf_op jit(solution)/shard_map/residual/pallas_call | solution.py:617
  (11 shorter events, 0.0 us)
Async XLA Ops:
  0.6 1.2 %copy-start = (f32[64,4096]{1,0:T(8,128)S(1)}, f32[64,4096]{1,0:T(8,128)}, u32[]{:S(2)}) copy-start(f32[64,4096]{1,0:T(8,128)} %param.3) | copy-start | bytes 3145732
  1.9 0.7 copy-start.2
  4.9 5.5 %collective-permute-start = (f32[136,128]{1,0:T(8,128)S(1)}, f32[136,128]{1,0:T(8,128)S(1)}, u32[]{:S(2)}, u32[]{:S(2)}) collective-permute-start(f32[136,128]{1,0:T(8,128)S(1)} %get-tuple-element.32), channel_id=1, source_target_pairs={{0,65},{64,0},{1,66},{65,1},{2,67},{66,2},{3,68},{67,3},{4,69},{68... | collective-permute-start | bytes 208904 | tf_op jit(solution)/shard_map/ppermute | solution.py:51
  4.9 11.7 %copy-start.3 = (s32[8]{0:T(128)S(1)}, s32[8]{0:T(128)}, u32[]{:S(2)}) copy-start(s32[8]{0:T(128)} %parent.11) | copy-start | bytes 100
  5.0 5.4 %collective-permute-start.1 = (f32[136,128]{1,0:T(8,128)S(1)}, f32[136,128]{1,0:T(8,128)S(1)}, u32[]{:S(2)}, u32[]{:S(2)}) collective-permute-start(f32[136,128]{1,0:T(8,128)S(1)} %get-tuple-element.33), channel_id=1, source_target_pairs={{0,64},{64,0},{1,65},{65,1},{2,66},{66,2},{3,67},{67,3},{4,68},{68... | collective-permute-start | bytes 208904 | tf_op jit(solution)/shard_map/ppermute | solution.py:51
  11.0 5.4 %collective-permute-start.2 = (f32[128,128]{1,0:T(8,128)S(1)}, f32[128,128]{1,0:T(8,128)S(1)}, u32[]{:S(2)}, u32[]{:S(2)}) collective-permute-start(f32[128,128]{1,0:T(8,128)S(1)} %get-tuple-element.35), channel_id=1, source_target_pairs={{65,0},{0,64},{66,1},{1,65},{67,2},{2,66},{68,3},{3,67},{69,4},{4,... | collective-permute-start | bytes 196616 | tf_op jit(solution)/shard_map/ppermute | solution.py:51
  15.4 1.3 %collective-permute-start.3 = (f32[128,128]{1,0:T(8,128)S(1)}, f32[128,128]{1,0:T(8,128)S(1)}, u32[]{:S(2)}, u32[]{:S(2)}) collective-permute-start(f32[128,128]{1,0:T(8,128)S(1)} %get-tuple-element.36), channel_id=1, source_target_pairs={{0,64},{64,0},{1,65},{65,1},{2,66},{66,2},{3,67},{67,3},{4,68},{68... | collective-permute-start | bytes 196616 | tf_op jit(solution)/shard_map/ppermute | solution.py:51
  16.7 16.7 %copy-start.1 = (s32[8,6]{1,0:T(8,128)S(1)}, s32[8,6]{1,0:T(8,128)}, u32[]{:S(2)}) copy-start(s32[8,6]{1,0:T(8,128)} %neighbor.5) | copy-start | bytes 580
  18.3 10.2 %collective-permute-start.4 = (f32[64,128]{1,0:T(8,128)S(1)}, f32[64,128]{1,0:T(8,128)S(1)}, u32[]{:S(2)}, u32[]{:S(2)}) collective-permute-start(f32[64,128]{1,0:T(8,128)S(1)} %get-tuple-element.38.refs_0_), channel_id=1, source_target_pairs={{0,1},{1,0},{64,65},{65,64},{2,3},{3,2},{66,67},{67,66},{4,5},{5,4... | collective-permute-start | bytes 98312 | tf_op jit(solution)/shard_map/ppermute | solution.py:51
  20.0 11.5 %collective-permute-start.5 = (f32[64,128]{1,0:T(8,128)S(1)}, f32[64,128]{1,0:T(8,128)S(1)}, u32[]{:S(2)}, u32[]{:S(2)}) collective-permute-start(f32[64,128]{1,0:T(8,128)S(1)} %get-tuple-element.39.refs_1_), channel_id=1, source_target_pairs={{1,2},{2,1},{65,66},{66,65},{3,4},{4,3},{67,68},{68,67},{5,6},{6,5... | collective-permute-start | bytes 98312 | tf_op jit(solution)/shard_map/ppermute | solution.py:51
  22.9 8.5 %collective-permute-start.6 = (f32[64,128]{1,0:T(8,128)S(1)}, f32[64,128]{1,0:T(8,128)S(1)}, u32[]{:S(2)}, u32[]{:S(2)}) collective-permute-start(f32[64,128]{1,0:T(8,128)S(1)} %get-tuple-element.40.refs_2_), channel_id=1, source_target_pairs={{0,4},{4,0},{64,68},{68,64},{1,5},{5,1},{65,69},{69,65},{2,6},{6,2... | collective-permute-start | bytes 98312 | tf_op jit(solution)/shard_map/ppermute | solution.py:51
  24.5 7.0 %collective-permute-start.7 = (f32[64,128]{1,0:T(8,128)S(1)}, f32[64,128]{1,0:T(8,128)S(1)}, u32[]{:S(2)}, u32[]{:S(2)}) collective-permute-start(f32[64,128]{1,0:T(8,128)S(1)} %get-tuple-element.41.refs_3_), channel_id=1, source_target_pairs={{4,8},{8,4},{68,72},{72,68},{5,9},{9,5},{69,73},{73,69},{6,10},{10... | collective-permute-start | bytes 98312 | tf_op jit(solution)/shard_map/ppermute | solution.py:51
  28.4 3.9 %collective-permute-start.8 = (f32[64,128]{1,0:T(8,128)S(1)}, f32[64,128]{1,0:T(8,128)S(1)}, u32[]{:S(2)}, u32[]{:S(2)}) collective-permute-start(f32[64,128]{1,0:T(8,128)S(1)} %get-tuple-element.42.refs_4_), channel_id=1, source_target_pairs={{0,16},{16,0},{64,80},{80,64},{1,17},{17,1},{65,81},{81,65},{2,18}... | collective-permute-start | bytes 98312 | tf_op jit(solution)/shard_map/ppermute | solution.py:51
  28.5 4.9 %collective-permute-start.9 = (f32[64,128]{1,0:T(8,128)S(1)}, f32[64,128]{1,0:T(8,128)S(1)}, u32[]{:S(2)}, u32[]{:S(2)}) collective-permute-start(f32[64,128]{1,0:T(8,128)S(1)} %get-tuple-element.43.refs_5_), channel_id=1, source_target_pairs={{16,32},{32,16},{80,96},{96,80},{17,33},{33,17},{81,97},{97,81},{1... | collective-permute-start | bytes 98312 | tf_op jit(solution)/shard_map/ppermute | solution.py:51
  35.7 3.4 %collective-permute-start.10 = (f32[128,128]{1,0:T(8,128)S(1)}, f32[128,128]{1,0:T(8,128)S(1)}, u32[]{:S(2)}, u32[]{:S(2)}) collective-permute-start(f32[128,128]{1,0:T(8,128)S(1)} %get-tuple-element.46), channel_id=1, source_target_pairs={{0,65},{64,0},{1,66},{65,1},{2,67},{66,2},{3,68},{67,3},{4,69},{68... | collective-permute-start | bytes 196616 | tf_op jit(solution)/shard_map/ppermute | solution.py:51
  35.8 3.3 %collective-permute-start.11 = (f32[128,128]{1,0:T(8,128)S(1)}, f32[128,128]{1,0:T(8,128)S(1)}, u32[]{:S(2)}, u32[]{:S(2)}) collective-permute-start(f32[128,128]{1,0:T(8,128)S(1)} %get-tuple-element.47), channel_id=1, source_target_pairs={{0,64},{64,0},{1,65},{65,1},{2,66},{66,2},{3,67},{67,3},{4,68},{68... | collective-permute-start | bytes 196616 | tf_op jit(solution)/shard_map/ppermute | solution.py:51
  39.7 5.7 %collective-permute-start.12 = (f32[128,128]{1,0:T(8,128)S(1)}, f32[128,128]{1,0:T(8,128)S(1)}, u32[]{:S(2)}, u32[]{:S(2)}) collective-permute-start(f32[128,128]{1,0:T(8,128)S(1)} %get-tuple-element.49), channel_id=1, source_target_pairs={{65,0},{0,64},{66,1},{1,65},{67,2},{2,66},{68,3},{3,67},{69,4},{4,... | collective-permute-start | bytes 196616 | tf_op jit(solution)/shard_map/ppermute | solution.py:51
  42.6 2.8 %collective-permute-start.13 = (f32[128,128]{1,0:T(8,128)S(1)}, f32[128,128]{1,0:T(8,128)S(1)}, u32[]{:S(2)}, u32[]{:S(2)}) collective-permute-start(f32[128,128]{1,0:T(8,128)S(1)} %get-tuple-element.50), channel_id=1, source_target_pairs={{0,64},{64,0},{1,65},{65,1},{2,66},{66,2},{3,67},{67,3},{4,68},{68... | collective-permute-start | bytes 196616 | tf_op jit(solution)/shard_map/ppermute | solution.py:51
  47.0 7.7 %collective-permute-start.14 = (f32[64,128]{1,0:T(8,128)S(1)}, f32[64,128]{1,0:T(8,128)S(1)}, u32[]{:S(2)}, u32[]{:S(2)}) collective-permute-start(f32[64,128]{1,0:T(8,128)S(1)} %get-tuple-element.52.refs_0_), channel_id=1, source_target_pairs={{0,1},{1,0},{64,65},{65,64},{2,3},{3,2},{66,67},{67,66},{4,5},{5,4... | collective-permute-start | bytes 98312 | tf_op jit(solution)/shard_map/ppermute | solution.py:51
  47.3 14.2 %collective-permute-start.15 = (f32[64,128]{1,0:T(8,128)S(1)}, f32[64,128]{1,0:T(8,128)S(1)}, u32[]{:S(2)}, u32[]{:S(2)}) collective-permute-start(f32[64,128]{1,0:T(8,128)S(1)} %get-tuple-element.53.refs_1_), channel_id=1, source_target_pairs={{1,2},{2,1},{65,66},{66,65},{3,4},{4,3},{67,68},{68,67},{5,6},{6,5... | collective-permute-start | bytes 98312 | tf_op jit(solution)/shard_map/ppermute | solution.py:51
  50.1 11.4 %collective-permute-start.16 = (f32[64,128]{1,0:T(8,128)S(1)}, f32[64,128]{1,0:T(8,128)S(1)}, u32[]{:S(2)}, u32[]{:S(2)}) collective-permute-start(f32[64,128]{1,0:T(8,128)S(1)} %get-tuple-element.54.refs_2_), channel_id=1, source_target_pairs={{0,4},{4,0},{64,68},{68,64},{1,5},{5,1},{65,69},{69,65},{2,6},{6,2... | collective-permute-start | bytes 98312 | tf_op jit(solution)/shard_map/ppermute | solution.py:51
  51.2 10.3 %collective-permute-start.17 = (f32[64,128]{1,0:T(8,128)S(1)}, f32[64,128]{1,0:T(8,128)S(1)}, u32[]{:S(2)}, u32[]{:S(2)}) collective-permute-start(f32[64,128]{1,0:T(8,128)S(1)} %get-tuple-element.55.refs_3_), channel_id=1, source_target_pairs={{4,8},{8,4},{68,72},{72,68},{5,9},{9,5},{69,73},{73,69},{6,10},{10... | collective-permute-start | bytes 98312 | tf_op jit(solution)/shard_map/ppermute | solution.py:51
  54.7 6.8 %collective-permute-start.18 = (f32[64,128]{1,0:T(8,128)S(1)}, f32[64,128]{1,0:T(8,128)S(1)}, u32[]{:S(2)}, u32[]{:S(2)}) collective-permute-start(f32[64,128]{1,0:T(8,128)S(1)} %get-tuple-element.56.refs_4_), channel_id=1, source_target_pairs={{0,16},{16,0},{64,80},{80,64},{1,17},{17,1},{65,81},{81,65},{2,18}... | collective-permute-start | bytes 98312 | tf_op jit(solution)/shard_map/ppermute | solution.py:51
  54.7 6.8 %collective-permute-start.19 = (f32[64,128]{1,0:T(8,128)S(1)}, f32[64,128]{1,0:T(8,128)S(1)}, u32[]{:S(2)}, u32[]{:S(2)}) collective-permute-start(f32[64,128]{1,0:T(8,128)S(1)} %get-tuple-element.57.refs_5_), channel_id=1, source_target_pairs={{16,32},{32,16},{80,96},{96,80},{17,33},{33,17},{81,97},{97,81},{1... | collective-permute-start | bytes 98312 | tf_op jit(solution)/shard_map/ppermute | solution.py:51

commit v4 on v3

--- a/solution.py
+++ b/solution.py
@@ -12,10 +12,13 @@
 FAM = 8
 WEIGHT = 0.8 / 6.0
 PAD_ROWS = 34 * 64
-GROUP = 4
+SWEEP = 16
+RESIDUE = 8
+CONVERT = 8
 F32 = jnp.float32
 VMEM = pl.BlockSpec(memory_space=pltpu.VMEM)
 SMEM = pl.BlockSpec(memory_space=pltpu.SMEM)
+HBM = pl.BlockSpec(memory_space=pltpu.HBM)
 
 
 def swap_pairs(unit, color):
@@ -159,6 +162,11 @@
             ref[given_rows(x, q, oz), :] = v[q][oz]
 
 
+def half_copies(source, target, sems, half):
+    parts = [pl.ds(f * 256 + half * 128, 128) for f in range(FAM)]
+    return [pltpu.make_async_copy(source.at[at], target.at[at], sems.at[half, f]) for f, at in enumerate(parts)]
+
+
 def put_plane(ref, x, a):
     for r in range(4):
         for p in range(2):
@@ -177,16 +185,16 @@
 
     def sweep(src, write):
         def body(i, _):
-            x0 = i * GROUP
-            p = [plane(src, x0 + m - 1) for m in range(GROUP + 2)]
-            result = [around(p[m + 1], p[m], p[m + 2], j, k) for m in range(GROUP)]
-            for m in range(GROUP):
+            x0 = i * SWEEP
+            p = [plane(src, x0 + m - 1) for m in range(SWEEP + 2)]
+            result = [around(p[m + 1], p[m], p[m + 2], j, k) for m in range(SWEEP)]
+            for m in range(SWEEP):
                 for r in range(4):
                     for c in range(2):
                         write((x0 + m + 1) * 64 + (r * 2 + c) * 8, p[m + 1][r][c], result[m][r][c])
             return 0
 
-        lax.fori_loop(0, 32 // GROUP, body, 0)
+        lax.fori_loop(0, 32 // SWEEP, body, 0)
 
     def first(at, a, m):
         put(mid, at, 1.2 * a + WEIGHT * m)
@@ -297,23 +305,55 @@
             put(buf, slot * 32 + i * 8, value)
 
 
-def first_down_kernel(parent, source, nxt, own, down):
+def unload_half(source, given, out, sems, half):
+    j, k = lane_parts()
+
+    def convert(n, _):
+        first = 16 * n + 8 * half
+        planes = [to_given(plane(source, first + m), j, k) for m in range(8)]
+        for m in range(8):
+            put_given(given, first + m, planes[m])
+        return 0
+
+    lax.fori_loop(0, 2, convert, 0)
+    for copy in half_copies(given, out, sems, half):
+        copy.start()
+
+
+def finish_unload(given, out, sems):
+    for half in range(2):
+        for copy in half_copies(given, out, sems, half):
+            copy.wait()
+
+
+def first_down_kernel(parent, tiles, nxt, own, down, source, places, sems, place_sem):
     sec, blk = position()
     j, k = lane_parts()
 
     @pl.when(sec == 0)
     def _():
+        halves = [half_copies(tiles, source, sems, half) for half in range(2)]
+        place = pltpu.make_async_copy(parent, places, place_sem)
+        for copy in (*halves[0], *halves[1], place):
+            copy.start()
+
         def pair(i):
             return restrict_given(given_plane(source, 2 * i), given_plane(source, 2 * i + 1), j, k)
 
-        def pairs(n, _):
-            done = [pair(4 * n + m) for m in range(4)]
-            for m in range(4):
-                put_down(down, 4 * n + m, done[m])
-            return 0
-
-        lax.fori_loop(0, 4, pairs, 0)
-        send_down(down, parent, blk, own, nxt, True)
+        for half in range(2):
+            for copy in halves[half]:
+                copy.wait()
+
+            def pairs(n, _):
+                first = 8 * n + 4 * half
+                done = [pair(first + m) for m in range(4)]
+                for m in range(4):
+                    put_down(down, first + m, done[m])
+                return 0
+
+            lax.fori_loop(0, 2, pairs, 0)
+        place.wait()
+        send_down(down, places, blk, own, nxt, True)
 
 
 def load_kernel(source, src, sol, mid):
@@ -322,12 +362,12 @@
     j, k = lane_parts()
 
     def convert(i, _):
-        planes = [to_working(given_plane(source, GROUP * i + m), j, k) for m in range(GROUP)]
-        for m in range(GROUP):
-            put_plane(src, GROUP * i + m, planes[m])
+        planes = [to_working(given_plane(source, CONVERT * i + m), j, k) for m in range(CONVERT)]
+        for m in range(CONVERT):
+            put_plane(src, CONVERT * i + m, planes[m])
         return 0
 
-    lax.fori_loop(0, 32 // GROUP, convert, 0)
+    lax.fori_loop(0, 32 // CONVERT, convert, 0)
 
     @pl.when(sec == 0)
     def _():
@@ -457,6 +497,8 @@
     last, fine = level is None, level == 0
     if fine:
         res, nxt, own, halo, table, down = refs[12:]
+    elif last:
+        out, halo, table, res, given, sems = refs[12:]
     else:
         res, halo, table = refs[12:]
     sec, blk = position()
@@ -500,28 +542,25 @@
             s = plane(src, x)
             return [[s[q][o] - 6.0 * a[q][o] + m[q][o] for o in range(2)] for q in range(4)]
 
-        def store(x, r):
+        def group(x):
+            p = [side(0) if x == 0 else plane(sol, x - 1)]
+            p += [plane(sol, x + m) for m in range(RESIDUE)]
+            p.append(side(64) if x + RESIDUE == 32 else plane(sol, x + RESIDUE))
+            r = [residue(x + m, p[m + 1], p[m], p[m + 2]) for m in range(RESIDUE)]
+            for m in range(RESIDUE):
+                put_plane(res, x + m, r[m])
+            if fine:
+                for m in range(0, RESIDUE, 2):
+                    put_down(down, (x + m) // 2, restrict_pair(r[m], r[m + 1]))
+
+        for half in range(2):
+            for x in range(8 * half, 32, 16):
+                for first in range(x, x + 8, RESIDUE):
+                    group(first)
             if last:
-                put_given(res, x, to_given(r, j, k))
-            else:
-                put_plane(res, x, r)
-
-        def group(i, _, low=None, high=None):
-            x = GROUP * i
-            p = [plane(sol, x + m) for m in range(GROUP)]
-            p = [plane(sol, x - 1) if low is None else low] + p + [plane(sol, x + GROUP) if high is None else high]
-            r = [residue(x + m, p[m + 1], p[m], p[m + 2]) for m in range(GROUP)]
-            for m in range(GROUP):
-                store(x + m, r[m])
-            if fine:
-                for m in range(GROUP // 2):
-                    put_down(down, (GROUP // 2) * i + m, restrict_pair(r[2 * m], r[2 * m + 1]))
-            return 0
-
-        count = 32 // GROUP
-        group(0, 0, low=side(0))
-        lax.fori_loop(1, count - 1, group, 0)
-        group(count - 1, 0, high=side(64))
+                unload_half(res, given, out, sems, half)
+        if last:
+            finish_unload(given, out, sems)
         if fine:
             send_down(down, parent, blk, own, nxt, False)
 
@@ -548,16 +587,10 @@
         smooth(rhs, mid, emit)
 
 
-def unload_kernel(sol, out):
-    j, k = lane_parts()
-
-    def convert(i, _):
-        planes = [to_given(plane(sol, GROUP * i + m), j, k) for m in range(GROUP)]
-        for m in range(GROUP):
-            put_given(out, GROUP * i + m, planes[m])
-        return 0
-
-    lax.fori_loop(0, 32 // GROUP, convert, 0)
+def unload_kernel(sol, out, given, sems):
+    for half in range(2):
+        unload_half(sol, given, out, sems, half)
+    finish_unload(given, out, sems)
 
 
 def shape(n, dtype=F32):
@@ -582,14 +615,26 @@
 
 def local(source, parent, neighbor):
     tiles = source.reshape(FAM, 8, 32, 128).transpose(0, 2, 1, 3).reshape(2048, 128)
+    here = pltpu.with_memory_space_constraint(tiles, pltpu.HBM)
+    place = pltpu.with_memory_space_constraint(parent, pltpu.HBM)
     pad, pads = shape(PAD_ROWS), scratch(PAD_ROWS)
 
     def both(nxt, own, pairs):
         return swap(nxt, pairs), swap(own, OWN_PAIRS)
 
-    nxt, own = call(first_down_kernel, "first_down", [SMEM, VMEM], (shape(136), shape(136)), [scratch(256)])(
-        parent, tiles
-    )
+    nxt, own = call(
+        first_down_kernel,
+        "first_down",
+        [HBM, HBM],
+        (shape(136), shape(136)),
+        [
+            scratch(256),
+            scratch(2048),
+            pltpu.SMEM((FAM,), jnp.int32),
+            pltpu.SemaphoreType.DMA((2, FAM)),
+            pltpu.SemaphoreType.DMA,
+        ],
+    )(place, here)
     got_next, got_own = both(nxt, own, DOWN_PAIRS)
     src, fine_sol = call(load_kernel, "load", [VMEM], (pad, pad), [pads])(tiles)
     coarse_sol, nxt, own, tags = call(
@@ -613,13 +658,14 @@
         sol, sent = out[0], out[1:]
         return sol, [*sent, *(swap(face, HALO_PAIRS[n]) for face, n in zip(sent, ORDER))]
 
-    def residue_of(level, name, sol, faces, out_shape, more=()):
+    def residue_of(level, name, sol, faces, out_shape, more=(), out_specs=None):
         return call(
             functools.partial(residual_kernel, level),
             name,
             [SMEM, SMEM] + [VMEM] * 14,
             out_shape,
             [scratch(384), scratch(768), *more],
+            out_specs,
         )(parent, neighbor, src, sol, *faces)
 
     sol, faces = lift_and_share(0, nxt, own)
@@ -635,8 +681,9 @@
         [pads, pads, pads],
     )(tags, coarse_res, sol, fine_sol, got_next, got_own)
     sol, faces = lift_and_share(1, nxt, own)
-    (solution,) = call(unload_kernel, "unload", [VMEM], (shape(2048),))(sol)
-    (residual,) = residue_of(None, "residual", sol, faces, (shape(2048),))
+    leave = [scratch(2048), pltpu.SemaphoreType.DMA((2, FAM))]
+    (solution,) = call(unload_kernel, "unload", [VMEM], (shape(2048),), leave, [HBM])(sol)
+    (residual,) = residue_of(None, "residual", sol, faces, (shape(2048),), [pads, *leave], [HBM])
 
     def blocks(x):
         return x.reshape(FAM, 32, 8, 128).transpose(0, 2, 1, 3).reshape(64, 4096)

time: 67.3 us -> 62.4 us (0.927)
  Pallas kernels: 26.2 us -> 22 us
  local copies, waits for them, and re-layouts: 1.88 us -> 0.01 us
    pallas_call x1, Pallas kernels: 4.86 us -> 2.89 us  [local(): src, fine_sol = call(load_kernel, 'load', [VMEM], (pad, pad), [pads])(tiles)]
    unnamed x8 -> x6, local copies, waits for them, and re-layouts: 1.88 us -> 0.01 us
    pallas_call x3, Pallas kernels: 8.54 us -> 7.1 us  [residue_of(): call(functools.partial(residual_kernel, level), name, [SMEM, SMEM] + [VME...]
    pallas_call x1, Pallas kernels: 2.2 us -> 1.36 us  [local(): call(fine_kernel, 'fine', [VMEM, VMEM], (pad,), [pads, pads])(res, sol)]
  transfers between devices with their start and end apart: 20 -> 20, of which waited for: 5 -> 5; matrix products, arithmetic and copies ran while one was open for 0% -> 0% of each run, Pallas kernels for 17% -> 12%
where the time goes in v4:
time: 62.4 us; the launch traced here: 62.3 us
  starting transfers between devices  33.1 us (53%)
  Pallas kernels  22 us (35%)
  waiting for transfers between devices  6.14 us (10%)
  between operations  0.99 us (2%)
    ppermute x20, starting transfers between devices, swap(): return lax.ppermute(x, AX, pairs)  33.1 us
    pallas_call x3, Pallas kernels, residue_of(): call(functools.partial(residual_kernel, level), name, [SMEM, SMEM] + [VME...  7.1 us
    ppermute x20, waiting for transfers between devices, swap(): return lax.ppermute(x, AX, pairs)  6.14 us
    pallas_call x2, Pallas kernels, lift_and_share(): call(lift_kernel, f'lift_{n}', [SMEM] + [VMEM] * 4, (pad,) + (shape(64),)...  3.41 us
    pallas_call x1, Pallas kernels, local(): call(first_down_kernel, 'first_down', [HBM, HBM], (shape(136), shape(136)...  3.19 us
    pallas_call x1, Pallas kernels, local(): src, fine_sol = call(load_kernel, 'load', [VMEM], (pad, pad), [pads])(tiles)  2.89 us
    pallas_call x1, Pallas kernels, local(): call(unload_kernel, 'unload', [VMEM], (shape(2048),), leave, [HBM])(sol)  2.87 us
    pallas_call x1, Pallas kernels, local(): call(fine_kernel, 'fine', [VMEM, VMEM], (pad,), [pads, pads])(res, sol)  1.36 us
  transfers between devices with their start and end apart: 20, of which 5 were waited for; matrix products, arithmetic and copies ran while one was open for 0% of the time, Pallas kernels for 12%

profile of v4, /device:TPU:18, one launch (start us, length us, event | category | flops | bytes accessed | tf_op | source)
XLA Modules:
  0.0 62.3 jit_solution(11195961595137928624)
XLA Ops:
  0.6 3.2 %first_down.1 = (f32[136,128]{1,0:T(8,128)S(1)}, f32[136,128]{1,0:T(8,128)S(1)}) custom-call(s32[8]{0:T(128)} %parent.11, f32[2048,128]{1,0:T(8,128)} %bitcast.15), custom_call_target="tpu_custom_call" | custom-call | tf_op jit(solution)/shard_map/first_down/pallas_call | solution.py:625
  3.8 0.1 collective-permute-start
  3.9 0.0 copy-start.2
  3.9 0.5 collective-permute-start.1
  4.4 2.9 %load.1 = (f32[2176,128]{1,0:T(8,128)S(1)}, f32[2176,128]{1,0:T(8,128)S(1)}) custom-call(f32[2048,128]{1,0:T(8,128)S(1)} %bitcast.16), custom_call_target="tpu_custom_call" | custom-call | tf_op jit(solution)/shard_map/load/pallas_call | solution.py:639
  7.3 0.0 collective-permute-done.refs_1_
  7.3 0.0 collective-permute-done.1.refs_2_
  7.3 0.6 %coarse_0.1 = (f32[2176,128]{1,0:T(8,128)S(1)}, f32[128,128]{1,0:T(8,128)S(1)}, f32[128,128]{1,0:T(8,128)S(1)}, s32[8]{0:T(128)S(1)}) custom-call(f32[2176,128]{1,0:T(8,128)S(1)} %get-tuple-element.30.refs_0_.src, f32[136,128]{1,0:T(8,128)S(1)} %collective-permute-done.refs_1_, f32[136,128]{1,0:T(8,128)S(1)} %collective-permute-done.1.refs_2_), custom_call_target="tpu_custom_call" | custom-call | tf_op jit(solution)/shard_map/coarse_0/pallas_call | solution.py:640
  8.0 5.5 %collective-permute-start.2 = (f32[128,128]{1,0:T(8,128)S(1)}, f32[128,128]{1,0:T(8,128)S(1)}, u32[]{:S(2)}, u32[]{:S(2)}) collective-permute-start(f32[128,128]{1,0:T(8,128)S(1)} %get-tuple-element.35), channel_id=1, source_target_pairs={{65,0},{0,64},{66,1},{1,65},{67,2},{2,66},{68,3},{3,67},{69,4},{4,... | collective-permute-start | bytes 196616 | tf_op jit(solution)/shard_map/ppermute | solution.py:54
  13.5 0.1 collective-permute-start.3
  13.6 0.8 %collective-permute-done.2.in_next = f32[128,128]{1,0:T(8,128)S(1)} collective-permute-done((f32[128,128]{1,0:T(8,128)S(1)}, f32[128,128]{1,0:T(8,128)S(1)}, u32[]{:S(2)}, u32[]{:S(2)}) %collective-permute-start.2) | collective-permute-done | bytes 65568 | tf_op jit(solution)/shard_map/ppermute | solution.py:54
  14.4 0.4 collective-permute-done.3.in_own
  14.8 1.6 %lift_0.1 = (f32[2176,128]{1,0:T(8,128)S(1)}, f32[64,128]{1,0:T(8,128)S(1)}, f32[64,128]{1,0:T(8,128)S(1)}, f32[64,128]{1,0:T(8,128)S(1)}, f32[64,128]{1,0:T(8,1...) custom-call(s32[8]{0:T(128)S(1)} %copy-done.2, f32[2176,128]{1,0:T(8,128)S(1)} %get-tuple-element.31.sol, ...), custom_call_target="tpu_custom_call" | custom-call | tf_op jit(solution)/shard_map/lift_0/pallas_call | solution.py:651
  16.4 0.6 collective-permute-start.4
  17.0 4.0 %collective-permute-start.5 = (f32[64,128]{1,0:T(8,128)S(1)}, f32[64,128]{1,0:T(8,128)S(1)}, u32[]{:S(2)}, u32[]{:S(2)}) collective-permute-start(f32[64,128]{1,0:T(8,128)S(1)} %get-tuple-element.39.refs_1_), channel_id=1, source_target_pairs={{1,2},{2,1},{65,66},{66,65},{3,4},{4,3},{67,68},{68,67},{5,6},{6,5... | collective-permute-start | bytes 98312 | tf_op jit(solution)/shard_map/ppermute | solution.py:54
  21.0 1.6 %collective-permute-start.6 = (f32[64,128]{1,0:T(8,128)S(1)}, f32[64,128]{1,0:T(8,128)S(1)}, u32[]{:S(2)}, u32[]{:S(2)}) collective-permute-start(f32[64,128]{1,0:T(8,128)S(1)} %get-tuple-element.40.refs_2_), channel_id=1, source_target_pairs={{0,4},{4,0},{64,68},{68,64},{1,5},{5,1},{65,69},{69,65},{2,6},{6,2... | collective-permute-start | bytes 98312 | tf_op jit(solution)/shard_map/ppermute | solution.py:54
  22.6 4.0 %collective-permute-start.7 = (f32[64,128]{1,0:T(8,128)S(1)}, f32[64,128]{1,0:T(8,128)S(1)}, u32[]{:S(2)}, u32[]{:S(2)}) collective-permute-start(f32[64,128]{1,0:T(8,128)S(1)} %get-tuple-element.41.refs_3_), channel_id=1, source_target_pairs={{4,8},{8,4},{68,72},{72,68},{5,9},{9,5},{69,73},{73,69},{6,10},{10... | collective-permute-start | bytes 98312 | tf_op jit(solution)/shard_map/ppermute | solution.py:54
  26.5 0.0 collective-permute-start.8
  26.5 0.0 collective-permute-done.4.refs_6_
  26.5 3.0 %collective-permute-start.9 = (f32[64,128]{1,0:T(8,128)S(1)}, f32[64,128]{1,0:T(8,128)S(1)}, u32[]{:S(2)}, u32[]{:S(2)}) collective-permute-start(f32[64,128]{1,0:T(8,128)S(1)} %get-tuple-element.43.refs_5_), channel_id=1, source_target_pairs={{16,32},{32,16},{80,96},{96,80},{17,33},{33,17},{81,97},{97,81},{1... | collective-permute-start | bytes 98312 | tf_op jit(solution)/shard_map/ppermute | solution.py:54
  29.5 0.0 collective-permute-done.5.refs_7_
  29.5 0.0 collective-permute-done.6.refs_8_
  29.5 0.9 %collective-permute-done.8.refs_10_ = f32[64,128]{1,0:T(8,128)S(1)} collective-permute-done((f32[64,128]{1,0:T(8,128)S(1)}, f32[64,128]{1,0:T(8,128)S(1)}, u32[]{:S(2)}, u32[]{:S(2)}) %collective-permute-start.8) | collective-permute-done | bytes 32800 | tf_op jit(solution)/shard_map/ppermute | solution.py:54
  30.5 1.0 %collective-permute-done.9.refs_11_ = f32[64,128]{1,0:T(8,128)S(1)} collective-permute-done((f32[64,128]{1,0:T(8,128)S(1)}, f32[64,128]{1,0:T(8,128)S(1)}, u32[]{:S(2)}, u32[]{:S(2)}) %collective-permute-start.9) | collective-permute-done | bytes 32800 | tf_op jit(solution)/shard_map/ppermute | solution.py:54
  31.4 1.8 %residue_fine.1 = (f32[2176,128]{1,0:T(8,128)S(1)}, f32[128,128]{1,0:T(8,128)S(1)}, f32[128,128]{1,0:T(8,128)S(1)}) custom-call(s32[8]{0:T(128)S(1)} %copy-done.2, s32[8,6]{1,0:T(8,128)S(1)} %copy-done.1, f32[2176,128]{1,0:T(8,128)S(1)} %get-tuple-element.30.refs_0_.src, f32[2176,128]{1,0:T(8,128)S(1)} %get-tuple-element.37.sol.refs_2_, ...), custom_call_target="tpu_custom_call" | custom-call | tf_op jit(solution)/shard_map/residue_fine/pallas_call | solution.py:662
  33.3 0.1 collective-permute-start.10
  33.4 0.5 collective-permute-start.11
  33.9 1.4 %fine.1.refs_3_.sol = f32[2176,128]{1,0:T(8,128)S(1)} custom-call(f32[2176,128]{1,0:T(8,128)S(1)} %get-tuple-element.44.res, f32[2176,128]{1,0:T(8,128)S(1)} %get-tuple-element.37.sol.refs_2_), custom_call_target="tpu_custom_call" | custom-call | tf_op jit(solution)/shard_map/fine/pallas_call | solution.py:675
  35.2 0.6 %residue_coarse.1.refs_1_ = f32[2176,128]{1,0:T(8,128)S(1)} custom-call(s32[8]{0:T(128)S(1)} %copy-done.2, s32[8,6]{1,0:T(8,128)S(1)} %copy-done.1, f32[2176,128]{1,0:T(8,128)S(1)} %get-tuple-element.30.refs_0_.src, f32[2176,128]{1,0:T(8,128)S(1)} %get-tuple-element.37.sol.refs_2_, f32[64,128]{1,0:T(8,128)S(1)} %get-tuple-element.38.refs_0_, ...), custom_call_target="tpu_custom_call" | custom-call | tf_op jit(solution)/shard_map/residue_coarse/pallas_call | solution.py:662
  35.9 0.0 collective-permute-done.10.refs_4_
  35.9 0.0 collective-permute-done.11.refs_5_
  35.9 0.6 coarse_1.1
  36.4 2.5 %collective-permute-start.12 = (f32[128,128]{1,0:T(8,128)S(1)}, f32[128,128]{1,0:T(8,128)S(1)}, u32[]{:S(2)}, u32[]{:S(2)}) collective-permute-start(f32[128,128]{1,0:T(8,128)S(1)} %get-tuple-element.49), channel_id=1, source_target_pairs={{65,0},{0,64},{66,1},{1,65},{67,2},{2,66},{68,3},{3,67},{69,4},{4,... | collective-permute-start | bytes 196616 | tf_op jit(solution)/shard_map/ppermute | solution.py:54
  38.9 0.1 collective-permute-start.13
  39.0 3.1 %collective-permute-done.12.in_next = f32[128,128]{1,0:T(8,128)S(1)} collective-permute-done((f32[128,128]{1,0:T(8,128)S(1)}, f32[128,128]{1,0:T(8,128)S(1)}, u32[]{:S(2)}, u32[]{:S(2)}) %collective-permute-start.12) | collective-permute-done | bytes 65568 | tf_op jit(solution)/shard_map/ppermute | solution.py:54
  42.1 1.8 %lift_1.1 = (f32[2176,128]{1,0:T(8,128)S(1)}, f32[64,128]{1,0:T(8,128)S(1)}, f32[64,128]{1,0:T(8,128)S(1)}, f32[64,128]{1,0:T(8,128)S(1)}, f32[64,128]{1,0:T(8,1...) custom-call(s32[8]{0:T(128)S(1)} %copy-done.2, f32[2176,128]{1,0:T(8,128)S(1)} %fine.1.refs_3_.sol, ...), custom_call_target="tpu_custom_call" | custom-call | tf_op jit(solution)/shard_map/lift_1/pallas_call | solution.py:651
  43.9 0.3 collective-permute-start.14
  44.2 2.4 %collective-permute-start.15 = (f32[64,128]{1,0:T(8,128)S(1)}, f32[64,128]{1,0:T(8,128)S(1)}, u32[]{:S(2)}, u32[]{:S(2)}) collective-permute-start(f32[64,128]{1,0:T(8,128)S(1)} %get-tuple-element.53.refs_1_), channel_id=1, source_target_pairs={{1,2},{2,1},{65,66},{66,65},{3,4},{4,3},{67,68},{68,67},{5,6},{6,5... | collective-permute-start | bytes 98312 | tf_op jit(solution)/shard_map/ppermute | solution.py:54
  46.6 1.0 %collective-permute-start.16 = (f32[64,128]{1,0:T(8,128)S(1)}, f32[64,128]{1,0:T(8,128)S(1)}, u32[]{:S(2)}, u32[]{:S(2)}) collective-permute-start(f32[64,128]{1,0:T(8,128)S(1)} %get-tuple-element.54.refs_2_), channel_id=1, source_target_pairs={{0,4},{4,0},{64,68},{68,64},{1,5},{5,1},{65,69},{69,65},{2,6},{6,2... | collective-permute-start | bytes 98312 | tf_op jit(solution)/shard_map/ppermute | solution.py:54
  47.6 4.0 %collective-permute-start.17 = (f32[64,128]{1,0:T(8,128)S(1)}, f32[64,128]{1,0:T(8,128)S(1)}, u32[]{:S(2)}, u32[]{:S(2)}) collective-permute-start(f32[64,128]{1,0:T(8,128)S(1)} %get-tuple-element.55.refs_3_), channel_id=1, source_target_pairs={{4,8},{8,4},{68,72},{72,68},{5,9},{9,5},{69,73},{73,69},{6,10},{10... | collective-permute-start | bytes 98312 | tf_op jit(solution)/shard_map/ppermute | solution.py:54
  51.6 0.0 collective-permute-start.18
  51.6 0.0 collective-permute-done.14.refs_6_
  51.6 3.0 %collective-permute-start.19 = (f32[64,128]{1,0:T(8,128)S(1)}, f32[64,128]{1,0:T(8,128)S(1)}, u32[]{:S(2)}, u32[]{:S(2)}) collective-permute-start(f32[64,128]{1,0:T(8,128)S(1)} %get-tuple-element.57.refs_5_), channel_id=1, source_target_pairs={{16,32},{32,16},{80,96},{96,80},{17,33},{33,17},{81,97},{97,81},{1... | collective-permute-start | bytes 98312 | tf_op jit(solution)/shard_map/ppermute | solution.py:54
  54.6 2.9 %unload.1 = f32[2048,128]{1,0:T(8,128)} custom-call(f32[2176,128]{1,0:T(8,128)S(1)} %get-tuple-element.51.sol), custom_call_target="tpu_custom_call" | custom-call | tf_op jit(solution)/shard_map/unload/pallas_call | solution.py:685
  57.4 0.0 collective-permute-done.16.refs_8_
  57.5 0.0 collective-permute-done.17.refs_9_
  57.5 0.0 collective-permute-done.19.refs_11_
  57.5 4.6 %residual.1 = f32[2048,128]{1,0:T(8,128)} custom-call(s32[8]{0:T(128)S(1)} %copy-done.2, s32[8,6]{1,0:T(8,128)S(1)} %copy-done.1, f32[2176,128]{1,0:T(8,128)S(1)} %get-tuple-element.30.refs_0_.src, f32[2176,128]{1,0:T(8,128)S(1)} %get-tuple-element.51.sol, f32[64,128]{1,0:T(8,128)S(1)} %get-tuple-element.52.refs_0_, ...), custom_call_target="tpu_custom_call" | custom-call | tf_op jit(solution)/shard_map/residual/pallas_call | solution.py:662
  (9 shorter events, 0.0 us)
Async XLA Ops:
  0.6 3.8 %copy-start = (f32[64,4096]{1,0:T(8,128)S(1)}, f32[64,4096]{1,0:T(8,128)}, u32[]{:S(2)}) copy-start(f32[64,4096]{1,0:T(8,128)} %param.3) | copy-start | bytes 3145732
  3.8 3.5 %collective-permute-start = (f32[136,128]{1,0:T(8,128)S(1)}, f32[136,128]{1,0:T(8,128)S(1)}, u32[]{:S(2)}, u32[]{:S(2)}) collective-permute-start(f32[136,128]{1,0:T(8,128)S(1)} %get-tuple-element.32), channel_id=1, source_target_pairs={{0,65},{64,0},{1,66},{65,1},{2,67},{66,2},{3,68},{67,3},{4,69},{68... | collective-permute-start | bytes 208904 | tf_op jit(solution)/shard_map/ppermute | solution.py:54
  3.9 10.8 %copy-start.2 = (s32[8]{0:T(128)S(1)}, s32[8]{0:T(128)}, u32[]{:S(2)}) copy-start(s32[8]{0:T(128)} %parent.11) | copy-start | bytes 100
  3.9 3.4 %collective-permute-start.1 = (f32[136,128]{1,0:T(8,128)S(1)}, f32[136,128]{1,0:T(8,128)S(1)}, u32[]{:S(2)}, u32[]{:S(2)}) collective-permute-start(f32[136,128]{1,0:T(8,128)S(1)} %get-tuple-element.33), channel_id=1, source_target_pairs={{0,64},{64,0},{1,65},{65,1},{2,66},{66,2},{3,67},{67,3},{4,68},{68... | collective-permute-start | bytes 208904 | tf_op jit(solution)/shard_map/ppermute | solution.py:54
  8.0 6.4 %collective-permute-start.2 = (f32[128,128]{1,0:T(8,128)S(1)}, f32[128,128]{1,0:T(8,128)S(1)}, u32[]{:S(2)}, u32[]{:S(2)}) collective-permute-start(f32[128,128]{1,0:T(8,128)S(1)} %get-tuple-element.35), channel_id=1, source_target_pairs={{65,0},{0,64},{66,1},{1,65},{67,2},{2,66},{68,3},{3,67},{69,4},{4,... | collective-permute-start | bytes 196616 | tf_op jit(solution)/shard_map/ppermute | solution.py:54
  13.5 1.3 %collective-permute-start.3 = (f32[128,128]{1,0:T(8,128)S(1)}, f32[128,128]{1,0:T(8,128)S(1)}, u32[]{:S(2)}, u32[]{:S(2)}) collective-permute-start(f32[128,128]{1,0:T(8,128)S(1)} %get-tuple-element.36), channel_id=1, source_target_pairs={{0,64},{64,0},{1,65},{65,1},{2,66},{66,2},{3,67},{67,3},{4,68},{68... | collective-permute-start | bytes 196616 | tf_op jit(solution)/shard_map/ppermute | solution.py:54
  14.7 16.7 %copy-start.1 = (s32[8,6]{1,0:T(8,128)S(1)}, s32[8,6]{1,0:T(8,128)}, u32[]{:S(2)}) copy-start(s32[8,6]{1,0:T(8,128)} %neighbor.5) | copy-start | bytes 580
  16.4 10.2 %collective-permute-start.4 = (f32[64,128]{1,0:T(8,128)S(1)}, f32[64,128]{1,0:T(8,128)S(1)}, u32[]{:S(2)}, u32[]{:S(2)}) collective-permute-start(f32[64,128]{1,0:T(8,128)S(1)} %get-tuple-element.38.refs_0_), channel_id=1, source_target_pairs={{0,1},{1,0},{64,65},{65,64},{2,3},{3,2},{66,67},{67,66},{4,5},{5,4... | collective-permute-start | bytes 98312 | tf_op jit(solution)/shard_map/ppermute | solution.py:54
  17.0 12.6 %collective-permute-start.5 = (f32[64,128]{1,0:T(8,128)S(1)}, f32[64,128]{1,0:T(8,128)S(1)}, u32[]{:S(2)}, u32[]{:S(2)}) collective-permute-start(f32[64,128]{1,0:T(8,128)S(1)} %get-tuple-element.39.refs_1_), channel_id=1, source_target_pairs={{1,2},{2,1},{65,66},{66,65},{3,4},{4,3},{67,68},{68,67},{5,6},{6,5... | collective-permute-start | bytes 98312 | tf_op jit(solution)/shard_map/ppermute | solution.py:54
  21.0 8.5 %collective-permute-start.6 = (f32[64,128]{1,0:T(8,128)S(1)}, f32[64,128]{1,0:T(8,128)S(1)}, u32[]{:S(2)}, u32[]{:S(2)}) collective-permute-start(f32[64,128]{1,0:T(8,128)S(1)} %get-tuple-element.40.refs_2_), channel_id=1, source_target_pairs={{0,4},{4,0},{64,68},{68,64},{1,5},{5,1},{65,69},{69,65},{2,6},{6,2... | collective-permute-start | bytes 98312 | tf_op jit(solution)/shard_map/ppermute | solution.py:54
  22.6 7.0 %collective-permute-start.7 = (f32[64,128]{1,0:T(8,128)S(1)}, f32[64,128]{1,0:T(8,128)S(1)}, u32[]{:S(2)}, u32[]{:S(2)}) collective-permute-start(f32[64,128]{1,0:T(8,128)S(1)} %get-tuple-element.41.refs_3_), channel_id=1, source_target_pairs={{4,8},{8,4},{68,72},{72,68},{5,9},{9,5},{69,73},{73,69},{6,10},{10... | collective-permute-start | bytes 98312 | tf_op jit(solution)/shard_map/ppermute | solution.py:54
  26.5 3.9 %collective-permute-start.8 = (f32[64,128]{1,0:T(8,128)S(1)}, f32[64,128]{1,0:T(8,128)S(1)}, u32[]{:S(2)}, u32[]{:S(2)}) collective-permute-start(f32[64,128]{1,0:T(8,128)S(1)} %get-tuple-element.42.refs_4_), channel_id=1, source_target_pairs={{0,16},{16,0},{64,80},{80,64},{1,17},{17,1},{65,81},{81,65},{2,18}... | collective-permute-start | bytes 98312 | tf_op jit(solution)/shard_map/ppermute | solution.py:54
  26.5 4.9 %collective-permute-start.9 = (f32[64,128]{1,0:T(8,128)S(1)}, f32[64,128]{1,0:T(8,128)S(1)}, u32[]{:S(2)}, u32[]{:S(2)}) collective-permute-start(f32[64,128]{1,0:T(8,128)S(1)} %get-tuple-element.43.refs_5_), channel_id=1, source_target_pairs={{16,32},{32,16},{80,96},{96,80},{17,33},{33,17},{81,97},{97,81},{1... | collective-permute-start | bytes 98312 | tf_op jit(solution)/shard_map/ppermute | solution.py:54
  33.3 2.6 %collective-permute-start.10 = (f32[128,128]{1,0:T(8,128)S(1)}, f32[128,128]{1,0:T(8,128)S(1)}, u32[]{:S(2)}, u32[]{:S(2)}) collective-permute-start(f32[128,128]{1,0:T(8,128)S(1)} %get-tuple-element.46), channel_id=1, source_target_pairs={{0,65},{64,0},{1,66},{65,1},{2,67},{66,2},{3,68},{67,3},{4,69},{68... | collective-permute-start | bytes 196616 | tf_op jit(solution)/shard_map/ppermute | solution.py:54
  33.4 2.5 %collective-permute-start.11 = (f32[128,128]{1,0:T(8,128)S(1)}, f32[128,128]{1,0:T(8,128)S(1)}, u32[]{:S(2)}, u32[]{:S(2)}) collective-permute-start(f32[128,128]{1,0:T(8,128)S(1)} %get-tuple-element.47), channel_id=1, source_target_pairs={{0,64},{64,0},{1,65},{65,1},{2,66},{66,2},{3,67},{67,3},{4,68},{68... | collective-permute-start | bytes 196616 | tf_op jit(solution)/shard_map/ppermute | solution.py:54
  36.4 5.6 %collective-permute-start.12 = (f32[128,128]{1,0:T(8,128)S(1)}, f32[128,128]{1,0:T(8,128)S(1)}, u32[]{:S(2)}, u32[]{:S(2)}) collective-permute-start(f32[128,128]{1,0:T(8,128)S(1)} %get-tuple-element.49), channel_id=1, source_target_pairs={{65,0},{0,64},{66,1},{1,65},{67,2},{2,66},{68,3},{3,67},{69,4},{4,... | collective-permute-start | bytes 196616 | tf_op jit(solution)/shard_map/ppermute | solution.py:54
  38.9 3.2 %collective-permute-start.13 = (f32[128,128]{1,0:T(8,128)S(1)}, f32[128,128]{1,0:T(8,128)S(1)}, u32[]{:S(2)}, u32[]{:S(2)}) collective-permute-start(f32[128,128]{1,0:T(8,128)S(1)} %get-tuple-element.50), channel_id=1, source_target_pairs={{0,64},{64,0},{1,65},{65,1},{2,66},{66,2},{3,67},{67,3},{4,68},{68... | collective-permute-start | bytes 196616 | tf_op jit(solution)/shard_map/ppermute | solution.py:54
  43.9 7.7 %collective-permute-start.14 = (f32[64,128]{1,0:T(8,128)S(1)}, f32[64,128]{1,0:T(8,128)S(1)}, u32[]{:S(2)}, u32[]{:S(2)}) collective-permute-start(f32[64,128]{1,0:T(8,128)S(1)} %get-tuple-element.52.refs_0_), channel_id=1, source_target_pairs={{0,1},{1,0},{64,65},{65,64},{2,3},{3,2},{66,67},{67,66},{4,5},{5,4... | collective-permute-start | bytes 98312 | tf_op jit(solution)/shard_map/ppermute | solution.py:54
  44.2 13.3 %collective-permute-start.15 = (f32[64,128]{1,0:T(8,128)S(1)}, f32[64,128]{1,0:T(8,128)S(1)}, u32[]{:S(2)}, u32[]{:S(2)}) collective-permute-start(f32[64,128]{1,0:T(8,128)S(1)} %get-tuple-element.53.refs_1_), channel_id=1, source_target_pairs={{1,2},{2,1},{65,66},{66,65},{3,4},{4,3},{67,68},{68,67},{5,6},{6,5... | collective-permute-start | bytes 98312 | tf_op jit(solution)/shard_map/ppermute | solution.py:54
  46.6 10.9 %collective-permute-start.16 = (f32[64,128]{1,0:T(8,128)S(1)}, f32[64,128]{1,0:T(8,128)S(1)}, u32[]{:S(2)}, u32[]{:S(2)}) collective-permute-start(f32[64,128]{1,0:T(8,128)S(1)} %get-tuple-element.54.refs_2_), channel_id=1, source_target_pairs={{0,4},{4,0},{64,68},{68,64},{1,5},{5,1},{65,69},{69,65},{2,6},{6,2... | collective-permute-start | bytes 98312 | tf_op jit(solution)/shard_map/ppermute | solution.py:54
  47.6 9.9 %collective-permute-start.17 = (f32[64,128]{1,0:T(8,128)S(1)}, f32[64,128]{1,0:T(8,128)S(1)}, u32[]{:S(2)}, u32[]{:S(2)}) collective-permute-start(f32[64,128]{1,0:T(8,128)S(1)} %get-tuple-element.55.refs_3_), channel_id=1, source_target_pairs={{4,8},{8,4},{68,72},{72,68},{5,9},{9,5},{69,73},{73,69},{6,10},{10... | collective-permute-start | bytes 98312 | tf_op jit(solution)/shard_map/ppermute | solution.py:54
  51.6 5.9 %collective-permute-start.18 = (f32[64,128]{1,0:T(8,128)S(1)}, f32[64,128]{1,0:T(8,128)S(1)}, u32[]{:S(2)}, u32[]{:S(2)}) collective-permute-start(f32[64,128]{1,0:T(8,128)S(1)} %get-tuple-element.56.refs_4_), channel_id=1, source_target_pairs={{0,16},{16,0},{64,80},{80,64},{1,17},{17,1},{65,81},{81,65},{2,18}... | collective-permute-start | bytes 98312 | tf_op jit(solution)/shard_map/ppermute | solution.py:54
  51.6 5.9 %collective-permute-start.19 = (f32[64,128]{1,0:T(8,128)S(1)}, f32[64,128]{1,0:T(8,128)S(1)}, u32[]{:S(2)}, u32[]{:S(2)}) collective-permute-start(f32[64,128]{1,0:T(8,128)S(1)} %get-tuple-element.57.refs_5_), channel_id=1, source_target_pairs={{16,32},{32,16},{80,96},{96,80},{17,33},{33,17},{81,97},{97,81},{1... | collective-permute-start | bytes 98312 | tf_op jit(solution)/shard_map/ppermute | solution.py:54

commit v5 on v4

--- a/solution.py
+++ b/solution.py
@@ -351,7 +351,7 @@
                     put_down(down, first + m, done[m])
                 return 0
 
-            lax.fori_loop(0, 2, pairs, 0)
+            lax.fori_loop(0, 2, pairs, 0, unroll=True)
         place.wait()
         send_down(down, places, blk, own, nxt, True)
 
@@ -478,11 +478,11 @@
                             planes[x][r] = [planes[x][r][p] + value for p in range(2)]
             return planes
 
-        lax.fori_loop(0, 4, functools.partial(pack, lifted), 0)
+        lax.fori_loop(0, 4, functools.partial(pack, lifted), 0, unroll=True)
 
     @pl.when(sec == 1)
     def _():
-        lax.fori_loop(0, 4, functools.partial(pack, lambda g: [plane(coarse_sol, 8 * g + m) for m in range(8)]), 0)
+        lax.fori_loop(0, 4, functools.partial(pack, lambda g: [plane(coarse_sol, 8 * g + m) for m in range(8)]), 0, unroll=True)
 
     put(face, 0, rows(out_sol, 64, 64))
     put(face, 64, rows(out_sol, 32 * 64, 64))

time: 62.4 us -> 61.2 us (0.981)
  Pallas kernels: 22 us -> 20.8 us
    pallas_call x2, Pallas kernels: 3.41 us -> 2.62 us  [lift_and_share(): call(lift_kernel, f'lift_{n}', [SMEM] + [VMEM] * 4, (pad,) + (shape(64),)...]
  transfers between devices with their start and end apart: 20 -> 20, of which waited for: 5 -> 5; matrix products, arithmetic and copies ran while one was open for 0% -> 0% of each run, Pallas kernels for 12% -> 13%
where the time goes in v5:
time: 61.2 us; the launch traced here: 61.1 us
  starting transfers between devices  33.1 us (54%)
  Pallas kernels  20.8 us (34%)
  waiting for transfers between devices  6.13 us (10%)
  between operations  0.99 us (2%)
    ppermute x20, starting transfers between devices, swap(): return lax.ppermute(x, AX, pairs)  33.1 us
    pallas_call x3, Pallas kernels, residue_of(): call(functools.partial(residual_kernel, level), name, [SMEM, SMEM] + [VME...  7.1 us
    ppermute x20, waiting for transfers between devices, swap(): return lax.ppermute(x, AX, pairs)  6.13 us
    pallas_call x1, Pallas kernels, local(): src, fine_sol = call(load_kernel, 'load', [VMEM], (pad, pad), [pads])(tiles)  2.89 us
    pallas_call x1, Pallas kernels, local(): call(unload_kernel, 'unload', [VMEM], (shape(2048),), leave, [HBM])(sol)  2.87 us
    pallas_call x2, Pallas kernels, lift_and_share(): call(lift_kernel, f'lift_{n}', [SMEM] + [VMEM] * 4, (pad,) + (shape(64),)...  2.62 us
    pallas_call x1, Pallas kernels, local(): call(first_down_kernel, 'first_down', [HBM, HBM], (shape(136), shape(136)...  2.62 us
    pallas_call x1, Pallas kernels, local(): call(fine_kernel, 'fine', [VMEM, VMEM], (pad,), [pads, pads])(res, sol)  1.36 us
  transfers between devices with their start and end apart: 20, of which 5 were waited for; matrix products, arithmetic and copies ran while one was open for 0% of the time, Pallas kernels for 13%

profile of v5, /device:TPU:18, one launch (start us, length us, event | category | flops | bytes accessed | tf_op | source)
XLA Modules:
  0.0 61.1 jit_solution(13554688687238117091)
XLA Ops:
  0.6 2.6 %first_down.1 = (f32[136,128]{1,0:T(8,128)S(1)}, f32[136,128]{1,0:T(8,128)S(1)}) custom-call(s32[8]{0:T(128)} %parent.11, f32[2048,128]{1,0:T(8,128)} %bitcast.15), custom_call_target="tpu_custom_call" | custom-call | tf_op jit(solution)/shard_map/first_down/pallas_call | solution.py:625
  3.3 0.1 collective-permute-start
  3.4 0.0 copy-start.2
  3.4 0.5 collective-permute-start.1
  3.9 2.9 %load.1 = (f32[2176,128]{1,0:T(8,128)S(1)}, f32[2176,128]{1,0:T(8,128)S(1)}) custom-call(f32[2048,128]{1,0:T(8,128)S(1)} %bitcast.16), custom_call_target="tpu_custom_call" | custom-call | tf_op jit(solution)/shard_map/load/pallas_call | solution.py:639
  6.7 0.0 collective-permute-done.refs_1_
  6.8 0.0 collective-permute-done.1.refs_2_
  6.8 0.6 %coarse_0.1 = (f32[2176,128]{1,0:T(8,128)S(1)}, f32[128,128]{1,0:T(8,128)S(1)}, f32[128,128]{1,0:T(8,128)S(1)}, s32[8]{0:T(128)S(1)}) custom-call(f32[2176,128]{1,0:T(8,128)S(1)} %get-tuple-element.30.refs_0_.src, f32[136,128]{1,0:T(8,128)S(1)} %collective-permute-done.refs_1_, f32[136,128]{1,0:T(8,128)S(1)} %collective-permute-done.1.refs_2_), custom_call_target="tpu_custom_call" | custom-call | tf_op jit(solution)/shard_map/coarse_0/pallas_call | solution.py:640
  7.4 5.5 %collective-permute-start.2 = (f32[128,128]{1,0:T(8,128)S(1)}, f32[128,128]{1,0:T(8,128)S(1)}, u32[]{:S(2)}, u32[]{:S(2)}) collective-permute-start(f32[128,128]{1,0:T(8,128)S(1)} %get-tuple-element.35), channel_id=1, source_target_pairs={{65,0},{0,64},{66,1},{1,65},{67,2},{2,66},{68,3},{3,67},{69,4},{4,... | collective-permute-start | bytes 196616 | tf_op jit(solution)/shard_map/ppermute | solution.py:54
  12.9 0.1 collective-permute-start.3
  13.0 0.8 %collective-permute-done.2.in_next = f32[128,128]{1,0:T(8,128)S(1)} collective-permute-done((f32[128,128]{1,0:T(8,128)S(1)}, f32[128,128]{1,0:T(8,128)S(1)}, u32[]{:S(2)}, u32[]{:S(2)}) %collective-permute-start.2) | collective-permute-done | bytes 65568 | tf_op jit(solution)/shard_map/ppermute | solution.py:54
  13.8 0.4 collective-permute-done.3.in_own
  14.2 1.3 %lift_0.1 = (f32[2176,128]{1,0:T(8,128)S(1)}, f32[64,128]{1,0:T(8,128)S(1)}, f32[64,128]{1,0:T(8,128)S(1)}, f32[64,128]{1,0:T(8,128)S(1)}, f32[64,128]{1,0:T(8,1...) custom-call(s32[8]{0:T(128)S(1)} %copy-done.2, f32[2176,128]{1,0:T(8,128)S(1)} %get-tuple-element.31.sol, ...), custom_call_target="tpu_custom_call" | custom-call | tf_op jit(solution)/shard_map/lift_0/pallas_call | solution.py:651
  15.5 0.6 collective-permute-start.4
  16.1 4.0 %collective-permute-start.5 = (f32[64,128]{1,0:T(8,128)S(1)}, f32[64,128]{1,0:T(8,128)S(1)}, u32[]{:S(2)}, u32[]{:S(2)}) collective-permute-start(f32[64,128]{1,0:T(8,128)S(1)} %get-tuple-element.39.refs_1_), channel_id=1, source_target_pairs={{1,2},{2,1},{65,66},{66,65},{3,4},{4,3},{67,68},{68,67},{5,6},{6,5... | collective-permute-start | bytes 98312 | tf_op jit(solution)/shard_map/ppermute | solution.py:54
  20.1 1.6 %collective-permute-start.6 = (f32[64,128]{1,0:T(8,128)S(1)}, f32[64,128]{1,0:T(8,128)S(1)}, u32[]{:S(2)}, u32[]{:S(2)}) collective-permute-start(f32[64,128]{1,0:T(8,128)S(1)} %get-tuple-element.40.refs_2_), channel_id=1, source_target_pairs={{0,4},{4,0},{64,68},{68,64},{1,5},{5,1},{65,69},{69,65},{2,6},{6,2... | collective-permute-start | bytes 98312 | tf_op jit(solution)/shard_map/ppermute | solution.py:54
  21.7 4.0 %collective-permute-start.7 = (f32[64,128]{1,0:T(8,128)S(1)}, f32[64,128]{1,0:T(8,128)S(1)}, u32[]{:S(2)}, u32[]{:S(2)}) collective-permute-start(f32[64,128]{1,0:T(8,128)S(1)} %get-tuple-element.41.refs_3_), channel_id=1, source_target_pairs={{4,8},{8,4},{68,72},{72,68},{5,9},{9,5},{69,73},{73,69},{6,10},{10... | collective-permute-start | bytes 98312 | tf_op jit(solution)/shard_map/ppermute | solution.py:54
  25.7 0.0 collective-permute-start.8
  25.7 0.0 collective-permute-done.4.refs_6_
  25.7 3.0 %collective-permute-start.9 = (f32[64,128]{1,0:T(8,128)S(1)}, f32[64,128]{1,0:T(8,128)S(1)}, u32[]{:S(2)}, u32[]{:S(2)}) collective-permute-start(f32[64,128]{1,0:T(8,128)S(1)} %get-tuple-element.43.refs_5_), channel_id=1, source_target_pairs={{16,32},{32,16},{80,96},{96,80},{17,33},{33,17},{81,97},{97,81},{1... | collective-permute-start | bytes 98312 | tf_op jit(solution)/shard_map/ppermute | solution.py:54
  28.6 0.0 collective-permute-done.5.refs_7_
  28.6 0.0 collective-permute-done.6.refs_8_
  28.7 0.0 collective-permute-done.7.refs_9_
  28.7 0.9 %collective-permute-done.8.refs_10_ = f32[64,128]{1,0:T(8,128)S(1)} collective-permute-done((f32[64,128]{1,0:T(8,128)S(1)}, f32[64,128]{1,0:T(8,128)S(1)}, u32[]{:S(2)}, u32[]{:S(2)}) %collective-permute-start.8) | collective-permute-done | bytes 32800 | tf_op jit(solution)/shard_map/ppermute | solution.py:54
  29.6 1.0 %collective-permute-done.9.refs_11_ = f32[64,128]{1,0:T(8,128)S(1)} collective-permute-done((f32[64,128]{1,0:T(8,128)S(1)}, f32[64,128]{1,0:T(8,128)S(1)}, u32[]{:S(2)}, u32[]{:S(2)}) %collective-permute-start.9) | collective-permute-done | bytes 32800 | tf_op jit(solution)/shard_map/ppermute | solution.py:54
  30.5 1.8 %residue_fine.1 = (f32[2176,128]{1,0:T(8,128)S(1)}, f32[128,128]{1,0:T(8,128)S(1)}, f32[128,128]{1,0:T(8,128)S(1)}) custom-call(s32[8]{0:T(128)S(1)} %copy-done.2, s32[8,6]{1,0:T(8,128)S(1)} %copy-done.1, f32[2176,128]{1,0:T(8,128)S(1)} %get-tuple-element.30.refs_0_.src, f32[2176,128]{1,0:T(8,128)S(1)} %get-tuple-element.37.sol.refs_2_, ...), custom_call_target="tpu_custom_call" | custom-call | tf_op jit(solution)/shard_map/residue_fine/pallas_call | solution.py:662
  32.4 0.1 collective-permute-start.10
  32.5 0.5 collective-permute-start.11
  33.0 1.4 %fine.1.refs_3_.sol = f32[2176,128]{1,0:T(8,128)S(1)} custom-call(f32[2176,128]{1,0:T(8,128)S(1)} %get-tuple-element.44.res, f32[2176,128]{1,0:T(8,128)S(1)} %get-tuple-element.37.sol.refs_2_), custom_call_target="tpu_custom_call" | custom-call | tf_op jit(solution)/shard_map/fine/pallas_call | solution.py:675
  34.3 0.6 %residue_coarse.1.refs_1_ = f32[2176,128]{1,0:T(8,128)S(1)} custom-call(s32[8]{0:T(128)S(1)} %copy-done.2, s32[8,6]{1,0:T(8,128)S(1)} %copy-done.1, f32[2176,128]{1,0:T(8,128)S(1)} %get-tuple-element.30.refs_0_.src, f32[2176,128]{1,0:T(8,128)S(1)} %get-tuple-element.37.sol.refs_2_, f32[64,128]{1,0:T(8,128)S(1)} %get-tuple-element.38.refs_0_, ...), custom_call_target="tpu_custom_call" | custom-call | tf_op jit(solution)/shard_map/residue_coarse/pallas_call | solution.py:662
  35.0 0.0 collective-permute-done.11.refs_5_
  35.0 0.7 %coarse_1.1 = (f32[2176,128]{1,0:T(8,128)S(1)}, f32[128,128]{1,0:T(8,128)S(1)}, f32[128,128]{1,0:T(8,128)S(1)}) custom-call(s32[8]{0:T(128)S(1)} %get-tuple-element.45.refs_0_, f32[2176,128]{1,0:T(8,128)S(1)} %residue_coarse.1.refs_1_, f32[2176,128]{1,0:T(8,128)S(1)} %get-tuple-element.37.sol.refs_2_, f32[2176,128]{1,0:T(8,128)S(1)} %fine.1.refs_3_.sol, ...), custom_call_target="tpu_custom_call" | custom-call | tf_op jit(solution)/shard_map/coarse_1/pallas_call | solution.py:676
  35.7 2.5 %collective-permute-start.12 = (f32[128,128]{1,0:T(8,128)S(1)}, f32[128,128]{1,0:T(8,128)S(1)}, u32[]{:S(2)}, u32[]{:S(2)}) collective-permute-start(f32[128,128]{1,0:T(8,128)S(1)} %get-tuple-element.49), channel_id=1, source_target_pairs={{65,0},{0,64},{66,1},{1,65},{67,2},{2,66},{68,3},{3,67},{69,4},{4,... | collective-permute-start | bytes 196616 | tf_op jit(solution)/shard_map/ppermute | solution.py:54
  38.2 0.1 collective-permute-start.13
  38.3 3.1 %collective-permute-done.12.in_next = f32[128,128]{1,0:T(8,128)S(1)} collective-permute-done((f32[128,128]{1,0:T(8,128)S(1)}, f32[128,128]{1,0:T(8,128)S(1)}, u32[]{:S(2)}, u32[]{:S(2)}) %collective-permute-start.12) | collective-permute-done | bytes 65568 | tf_op jit(solution)/shard_map/ppermute | solution.py:54
  41.4 1.3 %lift_1.1 = (f32[2176,128]{1,0:T(8,128)S(1)}, f32[64,128]{1,0:T(8,128)S(1)}, f32[64,128]{1,0:T(8,128)S(1)}, f32[64,128]{1,0:T(8,128)S(1)}, f32[64,128]{1,0:T(8,1...) custom-call(s32[8]{0:T(128)S(1)} %copy-done.2, f32[2176,128]{1,0:T(8,128)S(1)} %fine.1.refs_3_.sol, ...), custom_call_target="tpu_custom_call" | custom-call | tf_op jit(solution)/shard_map/lift_1/pallas_call | solution.py:651
  42.7 0.3 collective-permute-start.14
  43.0 2.4 %collective-permute-start.15 = (f32[64,128]{1,0:T(8,128)S(1)}, f32[64,128]{1,0:T(8,128)S(1)}, u32[]{:S(2)}, u32[]{:S(2)}) collective-permute-start(f32[64,128]{1,0:T(8,128)S(1)} %get-tuple-element.53.refs_1_), channel_id=1, source_target_pairs={{1,2},{2,1},{65,66},{66,65},{3,4},{4,3},{67,68},{68,67},{5,6},{6,5... | collective-permute-start | bytes 98312 | tf_op jit(solution)/shard_map/ppermute | solution.py:54
  45.4 1.0 %collective-permute-start.16 = (f32[64,128]{1,0:T(8,128)S(1)}, f32[64,128]{1,0:T(8,128)S(1)}, u32[]{:S(2)}, u32[]{:S(2)}) collective-permute-start(f32[64,128]{1,0:T(8,128)S(1)} %get-tuple-element.54.refs_2_), channel_id=1, source_target_pairs={{0,4},{4,0},{64,68},{68,64},{1,5},{5,1},{65,69},{69,65},{2,6},{6,2... | collective-permute-start | bytes 98312 | tf_op jit(solution)/shard_map/ppermute | solution.py:54
  46.4 4.0 %collective-permute-start.17 = (f32[64,128]{1,0:T(8,128)S(1)}, f32[64,128]{1,0:T(8,128)S(1)}, u32[]{:S(2)}, u32[]{:S(2)}) collective-permute-start(f32[64,128]{1,0:T(8,128)S(1)} %get-tuple-element.55.refs_3_), channel_id=1, source_target_pairs={{4,8},{8,4},{68,72},{72,68},{5,9},{9,5},{69,73},{73,69},{6,10},{10... | collective-permute-start | bytes 98312 | tf_op jit(solution)/shard_map/ppermute | solution.py:54
  50.4 0.0 collective-permute-start.18
  50.4 0.0 collective-permute-done.14.refs_6_
  50.4 3.0 %collective-permute-start.19 = (f32[64,128]{1,0:T(8,128)S(1)}, f32[64,128]{1,0:T(8,128)S(1)}, u32[]{:S(2)}, u32[]{:S(2)}) collective-permute-start(f32[64,128]{1,0:T(8,128)S(1)} %get-tuple-element.57.refs_5_), channel_id=1, source_target_pairs={{16,32},{32,16},{80,96},{96,80},{17,33},{33,17},{81,97},{97,81},{1... | collective-permute-start | bytes 98312 | tf_op jit(solution)/shard_map/ppermute | solution.py:54
  53.4 2.9 %unload.1 = f32[2048,128]{1,0:T(8,128)} custom-call(f32[2176,128]{1,0:T(8,128)S(1)} %get-tuple-element.51.sol), custom_call_target="tpu_custom_call" | custom-call | tf_op jit(solution)/shard_map/unload/pallas_call | solution.py:685
  56.2 0.0 collective-permute-done.15.refs_7_
  56.3 0.0 collective-permute-done.17.refs_9_
  56.3 0.0 collective-permute-done.18.refs_10_
  56.3 4.6 %residual.1 = f32[2048,128]{1,0:T(8,128)} custom-call(s32[8]{0:T(128)S(1)} %copy-done.2, s32[8,6]{1,0:T(8,128)S(1)} %copy-done.1, f32[2176,128]{1,0:T(8,128)S(1)} %get-tuple-element.30.refs_0_.src, f32[2176,128]{1,0:T(8,128)S(1)} %get-tuple-element.51.sol, f32[64,128]{1,0:T(8,128)S(1)} %get-tuple-element.52.refs_0_, ...), custom_call_target="tpu_custom_call" | custom-call | tf_op jit(solution)/shard_map/residual/pallas_call | solution.py:662
  (9 shorter events, 0.0 us)
Async XLA Ops:
  0.6 3.2 %copy-start = (f32[64,4096]{1,0:T(8,128)S(1)}, f32[64,4096]{1,0:T(8,128)}, u32[]{:S(2)}) copy-start(f32[64,4096]{1,0:T(8,128)} %param.3) | copy-start | bytes 3145732
  3.3 3.5 %collective-permute-start = (f32[136,128]{1,0:T(8,128)S(1)}, f32[136,128]{1,0:T(8,128)S(1)}, u32[]{:S(2)}, u32[]{:S(2)}) collective-permute-start(f32[136,128]{1,0:T(8,128)S(1)} %get-tuple-element.32), channel_id=1, source_target_pairs={{0,65},{64,0},{1,66},{65,1},{2,67},{66,2},{3,68},{67,3},{4,69},{68... | collective-permute-start | bytes 208904 | tf_op jit(solution)/shard_map/ppermute | solution.py:54
  3.4 10.8 %copy-start.2 = (s32[8]{0:T(128)S(1)}, s32[8]{0:T(128)}, u32[]{:S(2)}) copy-start(s32[8]{0:T(128)} %parent.11) | copy-start | bytes 100
  3.4 3.4 %collective-permute-start.1 = (f32[136,128]{1,0:T(8,128)S(1)}, f32[136,128]{1,0:T(8,128)S(1)}, u32[]{:S(2)}, u32[]{:S(2)}) collective-permute-start(f32[136,128]{1,0:T(8,128)S(1)} %get-tuple-element.33), channel_id=1, source_target_pairs={{0,64},{64,0},{1,65},{65,1},{2,66},{66,2},{3,67},{67,3},{4,68},{68... | collective-permute-start | bytes 208904 | tf_op jit(solution)/shard_map/ppermute | solution.py:54
  7.4 6.4 %collective-permute-start.2 = (f32[128,128]{1,0:T(8,128)S(1)}, f32[128,128]{1,0:T(8,128)S(1)}, u32[]{:S(2)}, u32[]{:S(2)}) collective-permute-start(f32[128,128]{1,0:T(8,128)S(1)} %get-tuple-element.35), channel_id=1, source_target_pairs={{65,0},{0,64},{66,1},{1,65},{67,2},{2,66},{68,3},{3,67},{69,4},{4,... | collective-permute-start | bytes 196616 | tf_op jit(solution)/shard_map/ppermute | solution.py:54
  12.9 1.3 %collective-permute-start.3 = (f32[128,128]{1,0:T(8,128)S(1)}, f32[128,128]{1,0:T(8,128)S(1)}, u32[]{:S(2)}, u32[]{:S(2)}) collective-permute-start(f32[128,128]{1,0:T(8,128)S(1)} %get-tuple-element.36), channel_id=1, source_target_pairs={{0,64},{64,0},{1,65},{65,1},{2,66},{66,2},{3,67},{67,3},{4,68},{68... | collective-permute-start | bytes 196616 | tf_op jit(solution)/shard_map/ppermute | solution.py:54
  14.2 16.4 %copy-start.1 = (s32[8,6]{1,0:T(8,128)S(1)}, s32[8,6]{1,0:T(8,128)}, u32[]{:S(2)}) copy-start(s32[8,6]{1,0:T(8,128)} %neighbor.5) | copy-start | bytes 580
  15.5 10.2 %collective-permute-start.4 = (f32[64,128]{1,0:T(8,128)S(1)}, f32[64,128]{1,0:T(8,128)S(1)}, u32[]{:S(2)}, u32[]{:S(2)}) collective-permute-start(f32[64,128]{1,0:T(8,128)S(1)} %get-tuple-element.38.refs_0_), channel_id=1, source_target_pairs={{0,1},{1,0},{64,65},{65,64},{2,3},{3,2},{66,67},{67,66},{4,5},{5,4... | collective-permute-start | bytes 98312 | tf_op jit(solution)/shard_map/ppermute | solution.py:54
  16.1 12.5 %collective-permute-start.5 = (f32[64,128]{1,0:T(8,128)S(1)}, f32[64,128]{1,0:T(8,128)S(1)}, u32[]{:S(2)}, u32[]{:S(2)}) collective-permute-start(f32[64,128]{1,0:T(8,128)S(1)} %get-tuple-element.39.refs_1_), channel_id=1, source_target_pairs={{1,2},{2,1},{65,66},{66,65},{3,4},{4,3},{67,68},{68,67},{5,6},{6,5... | collective-permute-start | bytes 98312 | tf_op jit(solution)/shard_map/ppermute | solution.py:54
  20.1 8.5 %collective-permute-start.6 = (f32[64,128]{1,0:T(8,128)S(1)}, f32[64,128]{1,0:T(8,128)S(1)}, u32[]{:S(2)}, u32[]{:S(2)}) collective-permute-start(f32[64,128]{1,0:T(8,128)S(1)} %get-tuple-element.40.refs_2_), channel_id=1, source_target_pairs={{0,4},{4,0},{64,68},{68,64},{1,5},{5,1},{65,69},{69,65},{2,6},{6,2... | collective-permute-start | bytes 98312 | tf_op jit(solution)/shard_map/ppermute | solution.py:54
  21.7 7.0 %collective-permute-start.7 = (f32[64,128]{1,0:T(8,128)S(1)}, f32[64,128]{1,0:T(8,128)S(1)}, u32[]{:S(2)}, u32[]{:S(2)}) collective-permute-start(f32[64,128]{1,0:T(8,128)S(1)} %get-tuple-element.41.refs_3_), channel_id=1, source_target_pairs={{4,8},{8,4},{68,72},{72,68},{5,9},{9,5},{69,73},{73,69},{6,10},{10... | collective-permute-start | bytes 98312 | tf_op jit(solution)/shard_map/ppermute | solution.py:54
  25.7 3.9 %collective-permute-start.8 = (f32[64,128]{1,0:T(8,128)S(1)}, f32[64,128]{1,0:T(8,128)S(1)}, u32[]{:S(2)}, u32[]{:S(2)}) collective-permute-start(f32[64,128]{1,0:T(8,128)S(1)} %get-tuple-element.42.refs_4_), channel_id=1, source_target_pairs={{0,16},{16,0},{64,80},{80,64},{1,17},{17,1},{65,81},{81,65},{2,18}... | collective-permute-start | bytes 98312 | tf_op jit(solution)/shard_map/ppermute | solution.py:54
  25.7 4.9 %collective-permute-start.9 = (f32[64,128]{1,0:T(8,128)S(1)}, f32[64,128]{1,0:T(8,128)S(1)}, u32[]{:S(2)}, u32[]{:S(2)}) collective-permute-start(f32[64,128]{1,0:T(8,128)S(1)} %get-tuple-element.43.refs_5_), channel_id=1, source_target_pairs={{16,32},{32,16},{80,96},{96,80},{17,33},{33,17},{81,97},{97,81},{1... | collective-permute-start | bytes 98312 | tf_op jit(solution)/shard_map/ppermute | solution.py:54
  32.4 2.6 %collective-permute-start.10 = (f32[128,128]{1,0:T(8,128)S(1)}, f32[128,128]{1,0:T(8,128)S(1)}, u32[]{:S(2)}, u32[]{:S(2)}) collective-permute-start(f32[128,128]{1,0:T(8,128)S(1)} %get-tuple-element.46), channel_id=1, source_target_pairs={{0,65},{64,0},{1,66},{65,1},{2,67},{66,2},{3,68},{67,3},{4,69},{68... | collective-permute-start | bytes 196616 | tf_op jit(solution)/shard_map/ppermute | solution.py:54
  32.5 2.5 %collective-permute-start.11 = (f32[128,128]{1,0:T(8,128)S(1)}, f32[128,128]{1,0:T(8,128)S(1)}, u32[]{:S(2)}, u32[]{:S(2)}) collective-permute-start(f32[128,128]{1,0:T(8,128)S(1)} %get-tuple-element.47), channel_id=1, source_target_pairs={{0,64},{64,0},{1,65},{65,1},{2,66},{66,2},{3,67},{67,3},{4,68},{68... | collective-permute-start | bytes 196616 | tf_op jit(solution)/shard_map/ppermute | solution.py:54
  35.7 5.6 %collective-permute-start.12 = (f32[128,128]{1,0:T(8,128)S(1)}, f32[128,128]{1,0:T(8,128)S(1)}, u32[]{:S(2)}, u32[]{:S(2)}) collective-permute-start(f32[128,128]{1,0:T(8,128)S(1)} %get-tuple-element.49), channel_id=1, source_target_pairs={{65,0},{0,64},{66,1},{1,65},{67,2},{2,66},{68,3},{3,67},{69,4},{4,... | collective-permute-start | bytes 196616 | tf_op jit(solution)/shard_map/ppermute | solution.py:54
  38.2 3.1 %collective-permute-start.13 = (f32[128,128]{1,0:T(8,128)S(1)}, f32[128,128]{1,0:T(8,128)S(1)}, u32[]{:S(2)}, u32[]{:S(2)}) collective-permute-start(f32[128,128]{1,0:T(8,128)S(1)} %get-tuple-element.50), channel_id=1, source_target_pairs={{0,64},{64,0},{1,65},{65,1},{2,66},{66,2},{3,67},{67,3},{4,68},{68... | collective-permute-start | bytes 196616 | tf_op jit(solution)/shard_map/ppermute | solution.py:54
  42.7 7.7 %collective-permute-start.14 = (f32[64,128]{1,0:T(8,128)S(1)}, f32[64,128]{1,0:T(8,128)S(1)}, u32[]{:S(2)}, u32[]{:S(2)}) collective-permute-start(f32[64,128]{1,0:T(8,128)S(1)} %get-tuple-element.52.refs_0_), channel_id=1, source_target_pairs={{0,1},{1,0},{64,65},{65,64},{2,3},{3,2},{66,67},{67,66},{4,5},{5,4... | collective-permute-start | bytes 98312 | tf_op jit(solution)/shard_map/ppermute | solution.py:54
  43.0 13.3 %collective-permute-start.15 = (f32[64,128]{1,0:T(8,128)S(1)}, f32[64,128]{1,0:T(8,128)S(1)}, u32[]{:S(2)}, u32[]{:S(2)}) collective-permute-start(f32[64,128]{1,0:T(8,128)S(1)} %get-tuple-element.53.refs_1_), channel_id=1, source_target_pairs={{1,2},{2,1},{65,66},{66,65},{3,4},{4,3},{67,68},{68,67},{5,6},{6,5... | collective-permute-start | bytes 98312 | tf_op jit(solution)/shard_map/ppermute | solution.py:54
  45.4 10.8 %collective-permute-start.16 = (f32[64,128]{1,0:T(8,128)S(1)}, f32[64,128]{1,0:T(8,128)S(1)}, u32[]{:S(2)}, u32[]{:S(2)}) collective-permute-start(f32[64,128]{1,0:T(8,128)S(1)} %get-tuple-element.54.refs_2_), channel_id=1, source_target_pairs={{0,4},{4,0},{64,68},{68,64},{1,5},{5,1},{65,69},{69,65},{2,6},{6,2... | collective-permute-start | bytes 98312 | tf_op jit(solution)/shard_map/ppermute | solution.py:54
  46.4 9.9 %collective-permute-start.17 = (f32[64,128]{1,0:T(8,128)S(1)}, f32[64,128]{1,0:T(8,128)S(1)}, u32[]{:S(2)}, u32[]{:S(2)}) collective-permute-start(f32[64,128]{1,0:T(8,128)S(1)} %get-tuple-element.55.refs_3_), channel_id=1, source_target_pairs={{4,8},{8,4},{68,72},{72,68},{5,9},{9,5},{69,73},{73,69},{6,10},{10... | collective-permute-start | bytes 98312 | tf_op jit(solution)/shard_map/ppermute | solution.py:54
  50.4 5.9 %collective-permute-start.18 = (f32[64,128]{1,0:T(8,128)S(1)}, f32[64,128]{1,0:T(8,128)S(1)}, u32[]{:S(2)}, u32[]{:S(2)}) collective-permute-start(f32[64,128]{1,0:T(8,128)S(1)} %get-tuple-element.56.refs_4_), channel_id=1, source_target_pairs={{0,16},{16,0},{64,80},{80,64},{1,17},{17,1},{65,81},{81,65},{2,18}... | collective-permute-start | bytes 98312 | tf_op jit(solution)/shard_map/ppermute | solution.py:54
  50.4 5.9 %collective-permute-start.19 = (f32[64,128]{1,0:T(8,128)S(1)}, f32[64,128]{1,0:T(8,128)S(1)}, u32[]{:S(2)}, u32[]{:S(2)}) collective-permute-start(f32[64,128]{1,0:T(8,128)S(1)} %get-tuple-element.57.refs_5_), channel_id=1, source_target_pairs={{16,32},{32,16},{80,96},{96,80},{17,33},{33,17},{81,97},{97,81},{1... | collective-permute-start | bytes 98312 | tf_op jit(solution)/shard_map/ppermute | solution.py:54

commit v6 on v5

--- a/solution.py
+++ b/solution.py
@@ -45,7 +45,7 @@
 
 
 UNITS = (16, 4, 1)
-ORDER = (4, 5, 2, 3, 0, 1)
+ORDER = (4, 5, 3, 2, 0, 1)
 HALO_PAIRS = [swap_pairs(unit, color) for unit in UNITS for color in (0, 1)]
 OWN_PAIRS, DOWN_PAIRS, UP_PAIRS = level_pairs()
 

time: 61.2 us -> 61.9 us (1.011); the launches traced: 61.1 us -> 61.2 us
  waiting for transfers between devices: 6.13 us -> 7.36 us
  starting transfers between devices: 33.1 us -> 32 us
    ppermute x20, waiting for transfers between devices: 6.13 us -> 7.36 us  [swap(): return lax.ppermute(x, AX, pairs)]
    ppermute x20, starting transfers between devices: 33.1 us -> 32 us  [swap(): return lax.ppermute(x, AX, pairs)]
  transfers between devices with their start and end apart: 20 -> 20, of which waited for: 5 -> 6; matrix products, arithmetic and copies ran while one was open for 0% -> 0% of each run, Pallas kernels for 13% -> 13%
where the time goes in v6:
time: 61.9 us; the launch traced here: 61.2 us
  starting transfers between devices  32 us (52%)
  Pallas kernels  20.8 us (34%)
  waiting for transfers between devices  7.36 us (12%)
  between operations  0.99 us (2%)
    ppermute x20, starting transfers between devices, swap(): return lax.ppermute(x, AX, pairs)  32 us
    ppermute x20, waiting for transfers between devices, swap(): return lax.ppermute(x, AX, pairs)  7.36 us
    pallas_call x3, Pallas kernels, residue_of(): call(functools.partial(residual_kernel, level), name, [SMEM, SMEM] + [VME...  7.09 us
    pallas_call x1, Pallas kernels, local(): src, fine_sol = call(load_kernel, 'load', [VMEM], (pad, pad), [pads])(tiles)  2.89 us
    pallas_call x1, Pallas kernels, local(): call(unload_kernel, 'unload', [VMEM], (shape(2048),), leave, [HBM])(sol)  2.87 us
    pallas_call x1, Pallas kernels, local(): call(first_down_kernel, 'first_down', [HBM, HBM], (shape(136), shape(136)...  2.62 us
    pallas_call x2, Pallas kernels, lift_and_share(): call(lift_kernel, f'lift_{n}', [SMEM] + [VMEM] * 4, (pad,) + (shape(64),)...  2.62 us
    pallas_call x1, Pallas kernels, local(): call(fine_kernel, 'fine', [VMEM, VMEM], (pad,), [pads, pads])(res, sol)  1.36 us
  transfers between devices with their start and end apart: 20, of which 6 were waited for; matrix products, arithmetic and copies ran while one was open for 0% of the time, Pallas kernels for 13%

profile of v6, /device:TPU:18, one launch (start us, length us, event | category | flops | bytes accessed | tf_op | source)
XLA Modules:
  0.0 61.2 jit_solution(13929880562124355941)
XLA Ops:
  0.6 2.6 %first_down.1 = (f32[136,128]{1,0:T(8,128)S(1)}, f32[136,128]{1,0:T(8,128)S(1)}) custom-call(s32[8]{0:T(128)} %parent.11, f32[2048,128]{1,0:T(8,128)} %bitcast.15), custom_call_target="tpu_custom_call" | custom-call | tf_op jit(solution)/shard_map/first_down/pallas_call | solution.py:625
  3.3 0.1 collective-permute-start
  3.4 0.0 copy-start.2
  3.4 0.5 collective-permute-start.1
  3.9 2.9 %load.1 = (f32[2176,128]{1,0:T(8,128)S(1)}, f32[2176,128]{1,0:T(8,128)S(1)}) custom-call(f32[2048,128]{1,0:T(8,128)S(1)} %bitcast.16), custom_call_target="tpu_custom_call" | custom-call | tf_op jit(solution)/shard_map/load/pallas_call | solution.py:639
  6.8 0.0 collective-permute-done.1.refs_2_
  6.8 0.6 %coarse_0.1 = (f32[2176,128]{1,0:T(8,128)S(1)}, f32[128,128]{1,0:T(8,128)S(1)}, f32[128,128]{1,0:T(8,128)S(1)}, s32[8]{0:T(128)S(1)}) custom-call(f32[2176,128]{1,0:T(8,128)S(1)} %get-tuple-element.30.refs_0_.src, f32[136,128]{1,0:T(8,128)S(1)} %collective-permute-done.refs_1_, f32[136,128]{1,0:T(8,128)S(1)} %collective-permute-done.1.refs_2_), custom_call_target="tpu_custom_call" | custom-call | tf_op jit(solution)/shard_map/coarse_0/pallas_call | solution.py:640
  7.4 5.5 %collective-permute-start.2 = (f32[128,128]{1,0:T(8,128)S(1)}, f32[128,128]{1,0:T(8,128)S(1)}, u32[]{:S(2)}, u32[]{:S(2)}) collective-permute-start(f32[128,128]{1,0:T(8,128)S(1)} %get-tuple-element.35), channel_id=1, source_target_pairs={{65,0},{0,64},{66,1},{1,65},{67,2},{2,66},{68,3},{3,67},{69,4},{4,... | collective-permute-start | bytes 196616 | tf_op jit(solution)/shard_map/ppermute | solution.py:54
  12.9 0.1 collective-permute-start.3
  13.0 0.8 %collective-permute-done.2.in_next = f32[128,128]{1,0:T(8,128)S(1)} collective-permute-done((f32[128,128]{1,0:T(8,128)S(1)}, f32[128,128]{1,0:T(8,128)S(1)}, u32[]{:S(2)}, u32[]{:S(2)}) %collective-permute-start.2) | collective-permute-done | bytes 65568 | tf_op jit(solution)/shard_map/ppermute | solution.py:54
  13.8 0.4 collective-permute-done.3.in_own
  14.2 1.3 %lift_0.1 = (f32[2176,128]{1,0:T(8,128)S(1)}, f32[64,128]{1,0:T(8,128)S(1)}, f32[64,128]{1,0:T(8,128)S(1)}, f32[64,128]{1,0:T(8,128)S(1)}, f32[64,128]{1,0:T(8,1...) custom-call(s32[8]{0:T(128)S(1)} %copy-done.2, f32[2176,128]{1,0:T(8,128)S(1)} %get-tuple-element.31.sol, ...), custom_call_target="tpu_custom_call" | custom-call | tf_op jit(solution)/shard_map/lift_0/pallas_call | solution.py:651
  15.5 0.6 collective-permute-start.4
  16.1 4.0 %collective-permute-start.5 = (f32[64,128]{1,0:T(8,128)S(1)}, f32[64,128]{1,0:T(8,128)S(1)}, u32[]{:S(2)}, u32[]{:S(2)}) collective-permute-start(f32[64,128]{1,0:T(8,128)S(1)} %get-tuple-element.39.refs_1_), channel_id=1, source_target_pairs={{1,2},{2,1},{65,66},{66,65},{3,4},{4,3},{67,68},{68,67},{5,6},{6,5... | collective-permute-start | bytes 98312 | tf_op jit(solution)/shard_map/ppermute | solution.py:54
  20.1 0.4 collective-permute-start.6
  20.6 6.6 %collective-permute-start.7 = (f32[64,128]{1,0:T(8,128)S(1)}, f32[64,128]{1,0:T(8,128)S(1)}, u32[]{:S(2)}, u32[]{:S(2)}) collective-permute-start(f32[64,128]{1,0:T(8,128)S(1)} %get-tuple-element.41.refs_3_), channel_id=1, source_target_pairs={{0,4},{4,0},{64,68},{68,64},{1,5},{5,1},{65,69},{69,65},{2,6},{6,2... | collective-permute-start | bytes 98312 | tf_op jit(solution)/shard_map/ppermute | solution.py:54
  27.2 0.5 collective-permute-start.8
  27.7 0.0 collective-permute-done.4.refs_6_
  27.7 1.0 %collective-permute-start.9 = (f32[64,128]{1,0:T(8,128)S(1)}, f32[64,128]{1,0:T(8,128)S(1)}, u32[]{:S(2)}, u32[]{:S(2)}) collective-permute-start(f32[64,128]{1,0:T(8,128)S(1)} %get-tuple-element.43.refs_5_), channel_id=1, source_target_pairs={{16,32},{32,16},{80,96},{96,80},{17,33},{33,17},{81,97},{97,81},{1... | collective-permute-start | bytes 98312 | tf_op jit(solution)/shard_map/ppermute | solution.py:54
  28.7 0.0 collective-permute-done.5.refs_7_
  28.7 0.0 collective-permute-done.6.refs_8_
  28.7 0.4 collective-permute-done.7.refs_9_
  29.1 2.0 %collective-permute-done.8.refs_10_ = f32[64,128]{1,0:T(8,128)S(1)} collective-permute-done((f32[64,128]{1,0:T(8,128)S(1)}, f32[64,128]{1,0:T(8,128)S(1)}, u32[]{:S(2)}, u32[]{:S(2)}) %collective-permute-start.8) | collective-permute-done | bytes 32800 | tf_op jit(solution)/shard_map/ppermute | solution.py:54
  31.1 0.5 collective-permute-done.9.refs_11_
  31.6 1.8 %residue_fine.1 = (f32[2176,128]{1,0:T(8,128)S(1)}, f32[128,128]{1,0:T(8,128)S(1)}, f32[128,128]{1,0:T(8,128)S(1)}) custom-call(s32[8]{0:T(128)S(1)} %copy-done.2, s32[8,6]{1,0:T(8,128)S(1)} %copy-done.1, f32[2176,128]{1,0:T(8,128)S(1)} %get-tuple-element.30.refs_0_.src, f32[2176,128]{1,0:T(8,128)S(1)} %get-tuple-element.37.sol.refs_2_, ...), custom_call_target="tpu_custom_call" | custom-call | tf_op jit(solution)/shard_map/residue_fine/pallas_call | solution.py:662
  33.5 0.1 collective-permute-start.10
  33.6 0.5 collective-permute-start.11
  34.1 1.4 %fine.1.refs_3_.sol = f32[2176,128]{1,0:T(8,128)S(1)} custom-call(f32[2176,128]{1,0:T(8,128)S(1)} %get-tuple-element.44.res, f32[2176,128]{1,0:T(8,128)S(1)} %get-tuple-element.37.sol.refs_2_), custom_call_target="tpu_custom_call" | custom-call | tf_op jit(solution)/shard_map/fine/pallas_call | solution.py:675
  35.4 0.6 %residue_coarse.1.refs_1_ = f32[2176,128]{1,0:T(8,128)S(1)} custom-call(s32[8]{0:T(128)S(1)} %copy-done.2, s32[8,6]{1,0:T(8,128)S(1)} %copy-done.1, f32[2176,128]{1,0:T(8,128)S(1)} %get-tuple-element.30.refs_0_.src, f32[2176,128]{1,0:T(8,128)S(1)} %get-tuple-element.37.sol.refs_2_, f32[64,128]{1,0:T(8,128)S(1)} %get-tuple-element.38.refs_0_, ...), custom_call_target="tpu_custom_call" | custom-call | tf_op jit(solution)/shard_map/residue_coarse/pallas_call | solution.py:662
  36.1 0.0 collective-permute-done.10.refs_4_
  36.1 0.7 %coarse_1.1 = (f32[2176,128]{1,0:T(8,128)S(1)}, f32[128,128]{1,0:T(8,128)S(1)}, f32[128,128]{1,0:T(8,128)S(1)}) custom-call(s32[8]{0:T(128)S(1)} %get-tuple-element.45.refs_0_, f32[2176,128]{1,0:T(8,128)S(1)} %residue_coarse.1.refs_1_, f32[2176,128]{1,0:T(8,128)S(1)} %get-tuple-element.37.sol.refs_2_, f32[2176,128]{1,0:T(8,128)S(1)} %fine.1.refs_3_.sol, ...), custom_call_target="tpu_custom_call" | custom-call | tf_op jit(solution)/shard_map/coarse_1/pallas_call | solution.py:676
  36.8 2.3 %collective-permute-start.12 = (f32[128,128]{1,0:T(8,128)S(1)}, f32[128,128]{1,0:T(8,128)S(1)}, u32[]{:S(2)}, u32[]{:S(2)}) collective-permute-start(f32[128,128]{1,0:T(8,128)S(1)} %get-tuple-element.49), channel_id=1, source_target_pairs={{65,0},{0,64},{66,1},{1,65},{67,2},{2,66},{68,3},{3,67},{69,4},{4,... | collective-permute-start | bytes 196616 | tf_op jit(solution)/shard_map/ppermute | solution.py:54
  39.2 0.1 collective-permute-start.13
  39.3 3.2 %collective-permute-done.12.in_next = f32[128,128]{1,0:T(8,128)S(1)} collective-permute-done((f32[128,128]{1,0:T(8,128)S(1)}, f32[128,128]{1,0:T(8,128)S(1)}, u32[]{:S(2)}, u32[]{:S(2)}) %collective-permute-start.12) | collective-permute-done | bytes 65568 | tf_op jit(solution)/shard_map/ppermute | solution.py:54
  42.5 0.0 collective-permute-done.13.in_own
  42.5 1.3 %lift_1.1 = (f32[2176,128]{1,0:T(8,128)S(1)}, f32[64,128]{1,0:T(8,128)S(1)}, f32[64,128]{1,0:T(8,128)S(1)}, f32[64,128]{1,0:T(8,128)S(1)}, f32[64,128]{1,0:T(8,1...) custom-call(s32[8]{0:T(128)S(1)} %copy-done.2, f32[2176,128]{1,0:T(8,128)S(1)} %fine.1.refs_3_.sol, ...), custom_call_target="tpu_custom_call" | custom-call | tf_op jit(solution)/shard_map/lift_1/pallas_call | solution.py:651
  43.8 0.1 collective-permute-start.14
  43.9 2.5 %collective-permute-start.15 = (f32[64,128]{1,0:T(8,128)S(1)}, f32[64,128]{1,0:T(8,128)S(1)}, u32[]{:S(2)}, u32[]{:S(2)}) collective-permute-start(f32[64,128]{1,0:T(8,128)S(1)} %get-tuple-element.53.refs_1_), channel_id=1, source_target_pairs={{1,2},{2,1},{65,66},{66,65},{3,4},{4,3},{67,68},{68,67},{5,6},{6,5... | collective-permute-start | bytes 98312 | tf_op jit(solution)/shard_map/ppermute | solution.py:54
  46.4 0.0 collective-permute-start.16
  46.4 5.5 %collective-permute-start.17 = (f32[64,128]{1,0:T(8,128)S(1)}, f32[64,128]{1,0:T(8,128)S(1)}, u32[]{:S(2)}, u32[]{:S(2)}) collective-permute-start(f32[64,128]{1,0:T(8,128)S(1)} %get-tuple-element.55.refs_3_), channel_id=1, source_target_pairs={{0,4},{4,0},{64,68},{68,64},{1,5},{5,1},{65,69},{69,65},{2,6},{6,2... | collective-permute-start | bytes 98312 | tf_op jit(solution)/shard_map/ppermute | solution.py:54
  51.9 0.5 collective-permute-start.18
  52.5 1.0 %collective-permute-start.19 = (f32[64,128]{1,0:T(8,128)S(1)}, f32[64,128]{1,0:T(8,128)S(1)}, u32[]{:S(2)}, u32[]{:S(2)}) collective-permute-start(f32[64,128]{1,0:T(8,128)S(1)} %get-tuple-element.57.refs_5_), channel_id=1, source_target_pairs={{16,32},{32,16},{80,96},{96,80},{17,33},{33,17},{81,97},{97,81},{1... | collective-permute-start | bytes 98312 | tf_op jit(solution)/shard_map/ppermute | solution.py:54
  53.4 2.9 %unload.1 = f32[2048,128]{1,0:T(8,128)} custom-call(f32[2176,128]{1,0:T(8,128)S(1)} %get-tuple-element.51.sol), custom_call_target="tpu_custom_call" | custom-call | tf_op jit(solution)/shard_map/unload/pallas_call | solution.py:685
  56.3 0.0 collective-permute-done.15.refs_7_
  56.3 0.0 collective-permute-done.16.refs_8_
  56.3 0.0 collective-permute-done.18.refs_10_
  56.3 0.0 collective-permute-done.19.refs_11_
  56.4 4.6 %residual.1 = f32[2048,128]{1,0:T(8,128)} custom-call(s32[8]{0:T(128)S(1)} %copy-done.2, s32[8,6]{1,0:T(8,128)S(1)} %copy-done.1, f32[2176,128]{1,0:T(8,128)S(1)} %get-tuple-element.30.refs_0_.src, f32[2176,128]{1,0:T(8,128)S(1)} %get-tuple-element.51.sol, f32[64,128]{1,0:T(8,128)S(1)} %get-tuple-element.52.refs_0_, ...), custom_call_target="tpu_custom_call" | custom-call | tf_op jit(solution)/shard_map/residual/pallas_call | solution.py:662
  (9 shorter events, 0.0 us)
Async XLA Ops:
  0.6 3.2 %copy-start = (f32[64,4096]{1,0:T(8,128)S(1)}, f32[64,4096]{1,0:T(8,128)}, u32[]{:S(2)}) copy-start(f32[64,4096]{1,0:T(8,128)} %param.3) | copy-start | bytes 3145732
  3.3 3.5 %collective-permute-start = (f32[136,128]{1,0:T(8,128)S(1)}, f32[136,128]{1,0:T(8,128)S(1)}, u32[]{:S(2)}, u32[]{:S(2)}) collective-permute-start(f32[136,128]{1,0:T(8,128)S(1)} %get-tuple-element.32), channel_id=1, source_target_pairs={{0,65},{64,0},{1,66},{65,1},{2,67},{66,2},{3,68},{67,3},{4,69},{68... | collective-permute-start | bytes 208904 | tf_op jit(solution)/shard_map/ppermute | solution.py:54
  3.4 10.8 %copy-start.2 = (s32[8]{0:T(128)S(1)}, s32[8]{0:T(128)}, u32[]{:S(2)}) copy-start(s32[8]{0:T(128)} %parent.11) | copy-start | bytes 100
  3.4 3.4 %collective-permute-start.1 = (f32[136,128]{1,0:T(8,128)S(1)}, f32[136,128]{1,0:T(8,128)S(1)}, u32[]{:S(2)}, u32[]{:S(2)}) collective-permute-start(f32[136,128]{1,0:T(8,128)S(1)} %get-tuple-element.33), channel_id=1, source_target_pairs={{0,64},{64,0},{1,65},{65,1},{2,66},{66,2},{3,67},{67,3},{4,68},{68... | collective-permute-start | bytes 208904 | tf_op jit(solution)/shard_map/ppermute | solution.py:54
  7.4 6.4 %collective-permute-start.2 = (f32[128,128]{1,0:T(8,128)S(1)}, f32[128,128]{1,0:T(8,128)S(1)}, u32[]{:S(2)}, u32[]{:S(2)}) collective-permute-start(f32[128,128]{1,0:T(8,128)S(1)} %get-tuple-element.35), channel_id=1, source_target_pairs={{65,0},{0,64},{66,1},{1,65},{67,2},{2,66},{68,3},{3,67},{69,4},{4,... | collective-permute-start | bytes 196616 | tf_op jit(solution)/shard_map/ppermute | solution.py:54
  12.9 1.3 %collective-permute-start.3 = (f32[128,128]{1,0:T(8,128)S(1)}, f32[128,128]{1,0:T(8,128)S(1)}, u32[]{:S(2)}, u32[]{:S(2)}) collective-permute-start(f32[128,128]{1,0:T(8,128)S(1)} %get-tuple-element.36), channel_id=1, source_target_pairs={{0,64},{64,0},{1,65},{65,1},{2,66},{66,2},{3,67},{67,3},{4,68},{68... | collective-permute-start | bytes 196616 | tf_op jit(solution)/shard_map/ppermute | solution.py:54
  14.2 17.5 %copy-start.1 = (s32[8,6]{1,0:T(8,128)S(1)}, s32[8,6]{1,0:T(8,128)}, u32[]{:S(2)}) copy-start(s32[8,6]{1,0:T(8,128)} %neighbor.5) | copy-start | bytes 580
  15.5 12.2 %collective-permute-start.4 = (f32[64,128]{1,0:T(8,128)S(1)}, f32[64,128]{1,0:T(8,128)S(1)}, u32[]{:S(2)}, u32[]{:S(2)}) collective-permute-start(f32[64,128]{1,0:T(8,128)S(1)} %get-tuple-element.38.refs_0_), channel_id=1, source_target_pairs={{0,1},{1,0},{64,65},{65,64},{2,3},{3,2},{66,67},{67,66},{4,5},{5,4... | collective-permute-start | bytes 98312 | tf_op jit(solution)/shard_map/ppermute | solution.py:54
  16.1 12.6 %collective-permute-start.5 = (f32[64,128]{1,0:T(8,128)S(1)}, f32[64,128]{1,0:T(8,128)S(1)}, u32[]{:S(2)}, u32[]{:S(2)}) collective-permute-start(f32[64,128]{1,0:T(8,128)S(1)} %get-tuple-element.39.refs_1_), channel_id=1, source_target_pairs={{1,2},{2,1},{65,66},{66,65},{3,4},{4,3},{67,68},{68,67},{5,6},{6,5... | collective-permute-start | bytes 98312 | tf_op jit(solution)/shard_map/ppermute | solution.py:54
  20.1 8.6 %collective-permute-start.6 = (f32[64,128]{1,0:T(8,128)S(1)}, f32[64,128]{1,0:T(8,128)S(1)}, u32[]{:S(2)}, u32[]{:S(2)}) collective-permute-start(f32[64,128]{1,0:T(8,128)S(1)} %get-tuple-element.40.refs_2_), channel_id=1, source_target_pairs={{4,8},{8,4},{68,72},{72,68},{5,9},{9,5},{69,73},{73,69},{6,10},{10... | collective-permute-start | bytes 98312 | tf_op jit(solution)/shard_map/ppermute | solution.py:54
  20.6 8.5 %collective-permute-start.7 = (f32[64,128]{1,0:T(8,128)S(1)}, f32[64,128]{1,0:T(8,128)S(1)}, u32[]{:S(2)}, u32[]{:S(2)}) collective-permute-start(f32[64,128]{1,0:T(8,128)S(1)} %get-tuple-element.41.refs_3_), channel_id=1, source_target_pairs={{0,4},{4,0},{64,68},{68,64},{1,5},{5,1},{65,69},{69,65},{2,6},{6,2... | collective-permute-start | bytes 98312 | tf_op jit(solution)/shard_map/ppermute | solution.py:54
  27.2 3.9 %collective-permute-start.8 = (f32[64,128]{1,0:T(8,128)S(1)}, f32[64,128]{1,0:T(8,128)S(1)}, u32[]{:S(2)}, u32[]{:S(2)}) collective-permute-start(f32[64,128]{1,0:T(8,128)S(1)} %get-tuple-element.42.refs_4_), channel_id=1, source_target_pairs={{0,16},{16,0},{64,80},{80,64},{1,17},{17,1},{65,81},{81,65},{2,18}... | collective-permute-start | bytes 98312 | tf_op jit(solution)/shard_map/ppermute | solution.py:54
  27.7 3.9 %collective-permute-start.9 = (f32[64,128]{1,0:T(8,128)S(1)}, f32[64,128]{1,0:T(8,128)S(1)}, u32[]{:S(2)}, u32[]{:S(2)}) collective-permute-start(f32[64,128]{1,0:T(8,128)S(1)} %get-tuple-element.43.refs_5_), channel_id=1, source_target_pairs={{16,32},{32,16},{80,96},{96,80},{17,33},{33,17},{81,97},{97,81},{1... | collective-permute-start | bytes 98312 | tf_op jit(solution)/shard_map/ppermute | solution.py:54
  33.5 2.6 %collective-permute-start.10 = (f32[128,128]{1,0:T(8,128)S(1)}, f32[128,128]{1,0:T(8,128)S(1)}, u32[]{:S(2)}, u32[]{:S(2)}) collective-permute-start(f32[128,128]{1,0:T(8,128)S(1)} %get-tuple-element.46), channel_id=1, source_target_pairs={{0,65},{64,0},{1,66},{65,1},{2,67},{66,2},{3,68},{67,3},{4,69},{68... | collective-permute-start | bytes 196616 | tf_op jit(solution)/shard_map/ppermute | solution.py:54
  33.6 2.5 %collective-permute-start.11 = (f32[128,128]{1,0:T(8,128)S(1)}, f32[128,128]{1,0:T(8,128)S(1)}, u32[]{:S(2)}, u32[]{:S(2)}) collective-permute-start(f32[128,128]{1,0:T(8,128)S(1)} %get-tuple-element.47), channel_id=1, source_target_pairs={{0,64},{64,0},{1,65},{65,1},{2,66},{66,2},{3,67},{67,3},{4,68},{68... | collective-permute-start | bytes 196616 | tf_op jit(solution)/shard_map/ppermute | solution.py:54
  36.8 5.6 %collective-permute-start.12 = (f32[128,128]{1,0:T(8,128)S(1)}, f32[128,128]{1,0:T(8,128)S(1)}, u32[]{:S(2)}, u32[]{:S(2)}) collective-permute-start(f32[128,128]{1,0:T(8,128)S(1)} %get-tuple-element.49), channel_id=1, source_target_pairs={{65,0},{0,64},{66,1},{1,65},{67,2},{2,66},{68,3},{3,67},{69,4},{4,... | collective-permute-start | bytes 196616 | tf_op jit(solution)/shard_map/ppermute | solution.py:54
  39.2 3.3 %collective-permute-start.13 = (f32[128,128]{1,0:T(8,128)S(1)}, f32[128,128]{1,0:T(8,128)S(1)}, u32[]{:S(2)}, u32[]{:S(2)}) collective-permute-start(f32[128,128]{1,0:T(8,128)S(1)} %get-tuple-element.50), channel_id=1, source_target_pairs={{0,64},{64,0},{1,65},{65,1},{2,66},{66,2},{3,67},{67,3},{4,68},{68... | collective-permute-start | bytes 196616 | tf_op jit(solution)/shard_map/ppermute | solution.py:54
  43.8 8.7 %collective-permute-start.14 = (f32[64,128]{1,0:T(8,128)S(1)}, f32[64,128]{1,0:T(8,128)S(1)}, u32[]{:S(2)}, u32[]{:S(2)}) collective-permute-start(f32[64,128]{1,0:T(8,128)S(1)} %get-tuple-element.52.refs_0_), channel_id=1, source_target_pairs={{0,1},{1,0},{64,65},{65,64},{2,3},{3,2},{66,67},{67,66},{4,5},{5,4... | collective-permute-start | bytes 98312 | tf_op jit(solution)/shard_map/ppermute | solution.py:54
  43.9 12.4 %collective-permute-start.15 = (f32[64,128]{1,0:T(8,128)S(1)}, f32[64,128]{1,0:T(8,128)S(1)}, u32[]{:S(2)}, u32[]{:S(2)}) collective-permute-start(f32[64,128]{1,0:T(8,128)S(1)} %get-tuple-element.53.refs_1_), channel_id=1, source_target_pairs={{1,2},{2,1},{65,66},{66,65},{3,4},{4,3},{67,68},{68,67},{5,6},{6,5... | collective-permute-start | bytes 98312 | tf_op jit(solution)/shard_map/ppermute | solution.py:54
  46.4 9.9 %collective-permute-start.16 = (f32[64,128]{1,0:T(8,128)S(1)}, f32[64,128]{1,0:T(8,128)S(1)}, u32[]{:S(2)}, u32[]{:S(2)}) collective-permute-start(f32[64,128]{1,0:T(8,128)S(1)} %get-tuple-element.54.refs_2_), channel_id=1, source_target_pairs={{4,8},{8,4},{68,72},{72,68},{5,9},{9,5},{69,73},{73,69},{6,10},{10... | collective-permute-start | bytes 98312 | tf_op jit(solution)/shard_map/ppermute | solution.py:54
  46.4 9.9 %collective-permute-start.17 = (f32[64,128]{1,0:T(8,128)S(1)}, f32[64,128]{1,0:T(8,128)S(1)}, u32[]{:S(2)}, u32[]{:S(2)}) collective-permute-start(f32[64,128]{1,0:T(8,128)S(1)} %get-tuple-element.55.refs_3_), channel_id=1, source_target_pairs={{0,4},{4,0},{64,68},{68,64},{1,5},{5,1},{65,69},{69,65},{2,6},{6,2... | collective-permute-start | bytes 98312 | tf_op jit(solution)/shard_map/ppermute | solution.py:54
  51.9 4.4 %collective-permute-start.18 = (f32[64,128]{1,0:T(8,128)S(1)}, f32[64,128]{1,0:T(8,128)S(1)}, u32[]{:S(2)}, u32[]{:S(2)}) collective-permute-start(f32[64,128]{1,0:T(8,128)S(1)} %get-tuple-element.56.refs_4_), channel_id=1, source_target_pairs={{0,16},{16,0},{64,80},{80,64},{1,17},{17,1},{65,81},{81,65},{2,18}... | collective-permute-start | bytes 98312 | tf_op jit(solution)/shard_map/ppermute | solution.py:54
  52.5 3.9 %collective-permute-start.19 = (f32[64,128]{1,0:T(8,128)S(1)}, f32[64,128]{1,0:T(8,128)S(1)}, u32[]{:S(2)}, u32[]{:S(2)}) collective-permute-start(f32[64,128]{1,0:T(8,128)S(1)} %get-tuple-element.57.refs_5_), channel_id=1, source_target_pairs={{16,32},{32,16},{80,96},{96,80},{17,33},{33,17},{81,97},{97,81},{1... | collective-permute-start | bytes 98312 | tf_op jit(solution)/shard_map/ppermute | solution.py:54
